TPU v7x, 32 devices: a whole 2x2x4 slice. The times are simulated.
32 devices in a mesh: fsdp: 4 (over y, core), ctx: 8 (over z, x).
Axes of the slice: x: 2, y: 2, z: 4, core: 2. Of those that a mesh axis runs over, the one named last changes fastest.
Arguments:
- inputs: bfloat16 [4, 1024, 768], P('fsdp', 'ctx'), may hold values from -6 to 6
- lengths: int32 [4], P('fsdp'), may hold values from 512 to 1024, as said below
- ln1_gain: bfloat16 [768], P('fsdp'), may hold values from 0.25 to 1.75
- ln1_bias: bfloat16 [768], P('fsdp'), may hold values from -1.75 to 1.75
- qkv_weight: bfloat16 [768, 2304], P('fsdp'), may hold values from -0.3125 to 0.3125
- qv_bias: bfloat16 [1536], P('fsdp'), may hold values from -1.75 to 1.75
- out_weight: bfloat16 [768, 768], P('fsdp'), may hold values from -0.625 to 0.625
- out_bias: bfloat16 [768], P('fsdp'), may hold values from -1.75 to 1.75
- ln2_gain: bfloat16 [768], P('fsdp'), may hold values from 0.25 to 1.75
- ln2_bias: bfloat16 [768], P('fsdp'), may hold values from -1.75 to 1.75
- fc_weight: bfloat16 [768, 3072], P('fsdp'), may hold values from -0.21875 to 0.21875
- fc_bias: bfloat16 [3072], P('fsdp'), may hold values from -1.75 to 1.75
- proj_weight: bfloat16 [3072, 768], P('fsdp'), may hold values from -0.109375 to 0.109375
- proj_bias: bfloat16 [768], P('fsdp'), may hold values from -1.75 to 1.75
- cotangent: bfloat16 [4, 1024, 768], P('fsdp', 'ctx'), may hold values from -6 to 6
Outputs:
- outputs: bfloat16 [4, 1024, 768], P('fsdp', 'ctx')
- input_grad: bfloat16 [4, 1024, 768], P('fsdp', 'ctx')
- grad_ln1_gain: float32 [768], P('fsdp')
- grad_ln1_bias: float32 [768], P('fsdp')
- grad_qkv_weight: float32 [768, 2304], P('fsdp')
- grad_qv_bias: float32 [1536], P('fsdp')
- grad_out_weight: float32 [768, 768], P('fsdp')
- grad_out_bias: float32 [768], P('fsdp')
- grad_ln2_gain: float32 [768], P('fsdp')
- grad_ln2_bias: float32 [768], P('fsdp')
- grad_fc_weight: float32 [768, 3072], P('fsdp')
- grad_fc_bias: float32 [3072], P('fsdp')
- grad_proj_weight: float32 [3072, 768], P('fsdp')
- grad_proj_bias: float32 [768], P('fsdp')
Inputs may be any that keep to these rules, and one draw needn't show every extreme that they name: Sequence s holds tokens at its first lengths[s] positions and padding after them; in every draw some sequence fills its whole slot of 1024.
All inputs are finite; a program needn't handle non-finite values.
Results may differ from a plain program's by a relative error of at most 0.02.
Values may be sent and summed in bfloat16 or wider, within the bound.
No kernel may reach another device: no remote copies, remote signals or barrier semaphores. Data moves between devices by JAX's collectives and lax.ppermute only.
A program may use at most 128 MiB of HBM per device.

v0:
```python
import functools

import jax
import jax.numpy as jnp
from jax import lax
from jax.experimental import pallas as pl
from jax.experimental.pallas import tpu as pltpu
from jax.sharding import PartitionSpec as P

HD = 64
EPSILON = 1e-05
NEGATIVE = -1e30
GELU_COEF = 0.7978845608028654
CUBE = 0.044715
F32 = jnp.float32
BF16 = jnp.bfloat16
WAYS = 4
PIECES = 8
VMEM_LIMIT = 24 * 1024 * 1024


def f_xor(x, k):
    n = lax.axis_size("fsdp")
    return lax.ppermute(x, "fsdp", [(i, i ^ k) for i in range(n)])


def c_xor(x, k):
    n = lax.axis_size("ctx")
    return lax.ppermute(x, "ctx", [(i, i ^ k) for i in range(n)])


def turned(index):
    return ((index & 1) << 1) | (index >> 1)


def swap_layout(x):
    group = lax.axis_size("ctx")
    members = group // WAYS
    perm = []
    for f in range(WAYS):
        for c in range(group):
            j, m = divmod(c, members)
            perm.append((f * group + c, turned(j) * group + turned(f) * members + m))
    return lax.ppermute(x, ("fsdp", "ctx"), perm)


def after(value, *others):
    return lax.optimization_barrier((value, *others))[0]


def gather_f(x, until=lambda far: far):
    far = f_xor(x, 2)
    near = f_xor(x, 1)
    return [x, near, far, f_xor(until(far), 1)]


class Order:
    def __init__(self, scalars):
        self.scalars = scalars
        self.token = None

    def tie(self, value):
        if self.token is None:
            return value
        return lax.optimization_barrier((value, self.token))[0]

    def mark(self, value):
        self.token = value
        return value

    def call(self, kernel, outs, args, scratch=(), flops=0, name=None, direct=False, late=()):
        scalars = after(self.tie(self.scalars), *late)
        got = call(kernel, outs, [scalars, *args], scratch, flops, name, direct)
        self.mark(min(got, key=lambda value: value.size))
        return got

    def scatter_f(self, kept_own, kept_far, sent_far, sent_own):
        return kept_own, kept_far, f_xor(sent_far, 1), f_xor(sent_own, 1)

    def scatter_f_far(self, state, late=()):
        kept_own, kept_far, got_far, got_own = state
        (far,) = self.call(
            far_kernel, [shape(kept_own.shape, BF16)], [kept_far, got_far], name="far", late=late
        )
        return kept_own, got_own, f_xor(far, 2)


X, Z1, Z2 = 0, 1, 2
ONE, OTHER = (X, Z1, Z2), (Z1, X, Z2)


def others(value):
    bit = 3
    while (1 << bit) < lax.axis_size("ctx"):
        value = (value.astype(F32) + c_xor(value, 1 << bit).astype(F32)).astype(BF16)
        bit += 1
    return value


def call(kernel, outs, args, scratch=(), flops=0, name=None, direct=False):
    vmem = pl.BlockSpec(memory_space=pltpu.VMEM)
    moved = sum(a.size * a.dtype.itemsize for a in args) + sum(
        o.size * o.dtype.itemsize for o in outs
    )
    return pl.pallas_call(
        kernel,
        out_shape=tuple(outs),
        in_specs=[pl.BlockSpec(memory_space=pltpu.SMEM)] + [vmem] * (len(args) - 1),
        out_specs=tuple([pl.BlockSpec() if direct else vmem] * len(outs)),
        scratch_shapes=list(scratch),
        cost_estimate=pl.CostEstimate(flops=flops, bytes_accessed=moved, transcendentals=0),
        compiler_params=pltpu.CompilerParams(vmem_limit_bytes=VMEM_LIMIT),
        name=name,
    )(*args)


def shape(dims, dtype):
    return jax.ShapeDtypeStruct(dims, dtype)


def dot(a, b, contract):
    return lax.dot_general(a, b, ((contract[0:1], contract[1:2]), ((), ())), preferred_element_type=F32)


def block_rows(index, size):
    return pl.ds(pl.multiple_of(index * size, size), size)


def member_rows(member, size):
    return block_rows(turned(member), size)


def normalise(values):
    centred = values - jnp.mean(values, axis=-1, keepdims=True)
    inverse = lax.rsqrt(jnp.mean(centred * centred, axis=-1, keepdims=True) + EPSILON)
    return centred * inverse, inverse


def norm_back(upstream, scaled, inverse, gain):
    weighted = upstream * gain
    return inverse * (
        weighted
        - jnp.mean(weighted, axis=-1, keepdims=True)
        - scaled * jnp.mean(weighted * scaled, axis=-1, keepdims=True)
    )


def valid_rows(sc, table, chunk, rows):
    place = (turned(chunk) * sc[3] + sc[2]) * rows + lax.broadcasted_iota(jnp.int32, (rows, 1), 0)
    return place.astype(F32) < table[6:7, 0:1]


def emit_partials(sc, rows, value_ref, own_ref, far_ref, sent_far, sent_own):
    f = sc[0]
    own_ref[...] = value_ref[member_rows(f, rows), :]
    far_ref[...] = value_ref[member_rows(f ^ 2, rows), :]
    sent_own[...] = value_ref[member_rows(f ^ 1, rows), :].astype(BF16)
    sent_far[...] = value_ref[member_rows(f ^ 3, rows), :].astype(BF16)


def far_kernel(sc, kept, got, out):
    out[...] = (kept[...] + got[...].astype(F32)).astype(BF16)


def added(a, b):
    return (a.astype(F32) + b.astype(F32)).astype(BF16)


def fold_into(keep, got, kept, sent):
    half = keep.shape[0] // 2
    sent[:half] = added(keep[half:], got[half : 2 * half])
    kept[...] = added(keep[:half], got[:half])


def mlp_fold_kernel(sc, proj, proj_got, fc, fc_got, proj_kept, proj_sent, fc_kept, fc_sent):
    fold_into(proj, proj_got, proj_kept, proj_sent)
    fold_into(fc, fc_got, fc_kept, fc_sent)


def mlp_meet_kernel(sc, proj, proj_got, fc, fc_got, kept, sent):
    for i, (keep, got) in enumerate(((proj, proj_got), (fc, fc_got))):
        kept[i] = added(keep[0], got[0])
        sent[i] = added(keep[1], got[1])


def mlp_last_kernel(sc, keep, got, proj, *pieces):
    proj[...] = added(keep[0], got[0])
    rows = pieces[0].shape[0]
    for i, piece in enumerate(pieces):
        place = slice(i * rows, (i + 1) * rows)
        piece[...] = added(keep[1, place], got[1, place])


def mlp_join_kernel(sc, proj, p0, p1, p2, p3, out):
    out[0] = proj[...]
    rows = p0.shape[0]
    for i, piece in enumerate((p0, p1, p2, p3)):
        out[1, i * rows : (i + 1) * rows] = piece[...]


def mlp_part_kernel(sc, own, got, proj, fc):
    for i, out in enumerate((proj, fc)):
        out[0] = own[i]
        out[1] = got[i]


def grow_kernel(sc, a, a_got, b, b_got, a_out, b_out):
    for own, got, out in ((a, a_got, a_out), (b, b_got, b_out)):
        count = own.shape[0]
        out[:count] = own[...]
        out[count:] = got[...]


def qkv_fold_kernel(sc, near, vec, near_got, far, far_got, near_kept, vec_out, near_sent, far_kept, far_sent):
    fold_into(near, near_got, near_kept, near_sent)
    both = added(vec[...], near_got[near.shape[0] :])
    near_sent[near.shape[0] // 2 :] = both
    vec_out[...] = both
    fold_into(far, far_got, far_kept, far_sent)


def qkv_meet_kernel(sc, near, vec, near_got, far, far_got, kept, vec_out, sent):
    rows, more = near.shape[0] // 2, far.shape[0] // 2
    kept[:rows] = added(near[:rows], near_got[:rows])
    sent[:rows] = added(near[rows:], near_got[rows : 2 * rows])
    kept[rows:] = added(far[:more], far_got[:more])
    sent[rows : rows + more] = added(far[more:], far_got[more:])
    both = added(vec[...], near_got[2 * rows :])
    sent[rows + more :] = both
    vec_out[...] = both


def qkv_last_kernel(sc, keep, vec, got, piece, vec_out):
    count = keep.shape[0]
    piece[...] = added(keep[...], got[:count])
    vec_out[...] = added(vec[...], got[count:])


def exchange_kernel(sc, piece, vec, s1, s2, s3):
    rows = s1.shape[0] - vec.shape[0]
    for k, sent in ((2, s2), (3, s3), (1, s1)):
        sent[:rows] = piece[k * rows : (k + 1) * rows]
        sent[rows:] = vec[...]


def qkv_part_kernel(sc, own, got, near, far):
    rows = near.shape[1]
    for i, ref in enumerate((own, got)):
        near[i] = ref[:rows]
        far[i] = ref[rows:]


VECTOR_ROWS = 12


def vector_place(row, block, width):
    at = row * WAYS + block
    return slice(at // 3, at // 3 + 1), slice((at % 3) * width, (at % 3 + 1) * width)


def join_kernel(sc, piece, vec, r1, r2, r3, joined, *rest):
    *mine, qv, fc, scratch = rest
    rows, width = r1.shape[0] - vec.shape[0], piece.shape[1] // 3
    joined[:rows] = piece[:rows]
    for i, got in ((1, r1), (2, r2), (3, r3)):
        joined[i * rows : (i + 1) * rows] = got[:rows]
    joined[WAYS * rows :] = piece[WAYS * rows :]
    scratch[...] = (
        vec[...].astype(F32)
        + r1[rows:].astype(F32)
        + r2[rows:].astype(F32)
        + r3[rows:].astype(F32)
    )
    for block in range(WAYS):

        @pl.when(sc[0] == block)
        def _(block=block):
            for row in range(6):
                mine[row][...] = scratch[vector_place(row, block, width)].reshape(width)
            for i in range(2):
                at = 2 * block + i
                qv[i * width : (i + 1) * width] = scratch[
                    vector_place(6 + at // WAYS, at % WAYS, width)
                ].reshape(width)
            for i in range(WAYS):
                fc[i * width : (i + 1) * width] = scratch[
                    vector_place(8 + block, i, width)
                ].reshape(width)


def small_kernel(sc, vectors, out, bias):
    width = out.shape[1]
    out[...] = jnp.zeros_like(out)
    length = sc[4]
    out[8:9, :] = jnp.full((1, width), length >> 6, jnp.int32).astype(BF16)
    out[9:10, :] = jnp.full((1, width), length & 63, jnp.int32).astype(BF16)
    for i in range(8):
        out[i : i + 1, :] = vectors[i * width : (i + 1) * width].reshape(1, width)
    bias[...] = vectors[8 * width :].reshape(bias.shape).astype(F32)


def table_kernel(sc, s0, s1, s2, s3, table, bias):
    width = s0.shape[1]
    table[7:8, :] = jnp.zeros((1, table.shape[1]), F32)
    bias[...] = jnp.zeros_like(bias)
    odd = (sc[0] & 1) == 1
    for k, ref in enumerate((s0, s1, s2, s3)):
        values = ref[...].astype(F32)
        j = sc[0] ^ k
        pair = jnp.where(odd, values[7:8], values[6:7])
        for block in range(WAYS):

            @pl.when(j == block)
            def _(values=values, block=block):
                table[0:6, block * width : (block + 1) * width] = values[0:6]

        @pl.when(j == (sc[0] >> 1))
        def _(pair=pair):
            bias[:, :width] = pair

        @pl.when(j == 2 + (sc[0] >> 1))
        def _(pair=pair):
            bias[:, 2 * width :] = pair

        @pl.when(j == sc[5])
        def _(values=values):
            row = values[8:9] * 64.0 + values[9:10]
            for block in range(WAYS):
                table[6:7, block * width : (block + 1) * width] = row


def qkv_columns_kernel(sc, weight, w0, w1, w2, w2_low, w3):
    width = w0.shape[1] // 3
    half = w2.shape[0]
    rows = {0: [(w0, 0)], 1: [(w1, 0)], 2: [(w2, 0), (w2_low, half)], 3: [(w3, 0)]}
    for k in (2, 3, 1, 0):
        for block in range(WAYS):

            @pl.when((sc[0] ^ k) == block)
            def _(k=k, block=block):
                for ref, start in rows[k]:
                    for part in range(3):
                        base = part * WAYS * width + block * width
                        ref[:, part * width : (part + 1) * width] = weight[
                            start : start + ref.shape[0], base : base + width
                        ]


def fc_columns_kernel(sc, weight, w0, w1, w2, w3):
    for k, ref in ((2, w2), (3, w3), (1, w1), (0, w0)):
        ref[...] = weight[:, block_rows(sc[0] ^ k, ref.shape[1])]


def cot_kernel(sc, c0, c1, c2, c3, proj, table, g_out, pulled, bias_row):
    rows = c0.shape[0]
    for k, ref in enumerate((c0, c1, c2, c3)):
        j = sc[0] ^ k
        kept = jnp.where(valid_rows(sc, table, j, rows), ref[...].astype(F32), 0.0)
        if k == 0:
            bias_row[...] = jnp.sum(kept, axis=0, keepdims=True)
        low = kept.astype(BF16)
        g_out[member_rows(j, rows), :] = low
        pulled[member_rows(j, rows), :] = dot(low, proj[...], (1, 1))


def qkv_kernel(sc, x0, x1, x2, x3, w0, w1, w2, w2_low, w3, table, bias, normed, scales, full, q, kv):
    rows, wrows = x0.shape[0], w0.shape[0]
    half = wrows // 2
    for k, ref in ((0, w0), (1, w1), (3, w3)):
        full[block_rows(sc[0] ^ k, wrows), :] = ref[...]
    full[block_rows((sc[0] ^ 2) * 2, half), :] = w2[...]
    full[block_rows((sc[0] ^ 2) * 2 + 1, half), :] = w2_low[...]
    for k, ref in enumerate((x0, x1, x2, x3)):
        place = member_rows(sc[0] ^ k, rows)
        scaled, _ = normalise(ref[...].astype(F32))
        low = (scaled * table[0:1, :] + table[1:2, :]).astype(BF16)
        normed[place, :] = low
        scales[place, :] = scaled.astype(BF16)
        got = (dot(low, full[...], (1, 0)) + bias[...]).astype(BF16)
        width = q.shape[1]
        q[place, :] = got[:, :width] * jnp.asarray(0.125, BF16)
        kv[place, :] = got[:, width:]


def split3(value):
    high = value.astype(BF16)
    rest = value - high.astype(F32)
    mid = rest.astype(BF16)
    low = (rest - mid.astype(F32)).astype(BF16)
    return high, mid, low


def lanes(columns, rows, width, dtype):
    lane = lax.broadcasted_iota(jnp.int32, (rows, width), 1)
    out = jnp.zeros((rows, width), F32)
    for i, column in enumerate(columns):
        out = jnp.where(lane == i, column.astype(F32), out)
    return out.astype(dtype)


def joined(ref, base, count, h):
    total = None
    for part in range(3):
        column = base + part * count + h
        piece = ref[:, column : column + 1].astype(F32)
        total = piece if total is None else total + piece
    return total


def threshold(sc, other):
    return jnp.where(other == sc[2], 0, jnp.where(other < sc[2], 1 << 20, -(1 << 20)))


def attend(sc, step, first, last, refs):
    if first:
        q, kv = refs[:2]
        state_in = None
        rest = refs[2:]
    else:
        q, kv, acc_in, stat_in = refs[:4]
        rest = refs[4:]
    if last:
        out_w, attended, low, q_ext, own, far, sent, sent_own, scratch = rest
    else:
        acc_out, stat_out = rest
    total, width = q.shape
    rows = total // WAYS
    heads = width // HD
    limit = threshold(sc, sc[2] ^ step)
    ahead = lax.broadcasted_iota(jnp.int32, (rows, rows), 1) - lax.broadcasted_iota(
        jnp.int32, (rows, rows), 0
    )
    allowed = ahead <= limit
    for jq in range(WAYS):
        place = slice(jq * rows, (jq + 1) * rows)
        parts, tops, sums = [], [], []
        for h in range(heads):
            cols = slice(h * HD, (h + 1) * HD)
            vcols = slice(width + h * HD, width + (h + 1) * HD)
            qh = q[place, cols]
            diag = jnp.where(allowed, dot(qh, kv[place, cols], (1, 1)), NEGATIVE)
            top = jnp.max(diag, axis=-1, keepdims=True)
            if jq > 0:
                before = dot(qh, kv[: jq * rows, cols], (1, 1))
                top = jnp.maximum(top, jnp.max(before, axis=-1, keepdims=True))
            if not first:
                old = stat_in[place, h : h + 1]
                top = jnp.maximum(top, old)
            weight = jnp.exp(diag - top)
            count = jnp.sum(weight, axis=-1, keepdims=True)
            acc = dot(weight.astype(BF16), kv[place, vcols], (1, 0))
            if jq > 0:
                weight = jnp.exp(before - top)
                count = count + jnp.sum(weight, axis=-1, keepdims=True)
                acc = acc + dot(weight.astype(BF16), kv[: jq * rows, vcols], (1, 0))
            if not first:
                shrink = jnp.exp(old - top)
                count = count + shrink * stat_in[place, heads + h : heads + h + 1]
                acc = acc + shrink * acc_in[place, cols]
            if last:
                acc = acc / count
                tops.append(top + jnp.log(count))
            else:
                tops.append(top)
                sums.append(count)
            parts.append(acc)
        joined_parts = jnp.concatenate(parts, axis=1)
        if last:
            attended[place, :] = joined_parts
            low_part = joined_parts.astype(BF16)
            low[place, :] = low_part
            scratch[place, :] = dot(low_part, out_w[...], (1, 0))
            split = [split3(t) for t in tops]
            columns = [split[h][part] for part in range(3) for h in range(heads)]
            q_ext[place, :width] = q[place, :]
            q_ext[place, width:] = lanes(columns, rows, q_ext.shape[1] - width, BF16)
        else:
            acc_out[place, :] = joined_parts
            stat_out[place, :] = lanes(tops + sums, rows, stat_out.shape[1], F32)
    if last:
        emit_partials(sc, rows, scratch, own, far, sent, sent_own)


def second_norm_kernel(sc, own, got, far, x, table, residual, normed):
    value = (
        x[...].astype(F32)
        + own[...]
        + got[...].astype(F32)
        + far[...].astype(F32)
        + table[2:3, :]
    )
    residual[...] = value
    scaled, _ = normalise(value)
    normed[...] = (scaled * table[3:4, :] + table[4:5, :]).astype(BF16)


def assemble_kernel(sc, w0, w1, w2, w3, full):
    for k, ref in enumerate((w0, w1, w2, w3)):
        full[block_rows(sc[0] ^ k, ref.shape[0]), :] = ref[...]


def feed_kernel(
    sc, n0, n1, n2, n3, full, bias, pulled,
    normed, active, g_hidden, bias_row, own, far, sent, sent_own, scratch,
):
    rows = n0.shape[0]
    total = jnp.zeros_like(bias_row)
    for k, ref in enumerate((n0, n1, n2, n3)):
        place = member_rows(sc[0] ^ k, rows)
        normed[place, :] = ref[...]
        hidden = dot(ref[...], full[...], (1, 0)) + bias[...]
        square = hidden * hidden
        bend = jnp.tanh(GELU_COEF * (hidden + CUBE * hidden * square))
        active[place, :] = (0.5 * hidden * (1.0 + bend)).astype(BF16)
        slope = 0.5 * (1.0 + bend) + 0.5 * hidden * (1.0 - bend * bend) * (
            GELU_COEF * (1.0 + 3.0 * CUBE * square)
        )
        low = (pulled[place, :] * slope).astype(BF16)
        g_hidden[place, :] = low
        total = total + jnp.sum(low.astype(F32), axis=0, keepdims=True)
        scratch[place, :] = dot(low, full[...], (1, 1))
    bias_row[...] = total
    emit_partials(sc, rows, scratch, own, far, sent, sent_own)


def result_kernel(sc, active, proj, own, far, sent, sent_own, scratch):
    rows = active.shape[0] // WAYS
    scratch[...] = dot(active[...], proj[...], (1, 0))
    emit_partials(sc, rows, scratch, own, far, sent, sent_own)


def piece_of(sc, bits, slot):
    r = 0
    for i, bit in enumerate(bits):
        r |= ((slot >> (2 - i)) & 1) << bit
    return (sc[1] ^ r) & 7


def place_halves(keep, send):
    half = keep.shape[0]
    return [(slot, keep if slot < half else send, slot % half) for slot in range(2 * half)]


def tile_grad_kernel(bits, sc, active, g_out, keep, send, scratch):
    step_rows, step_cols = keep.shape[1], keep.shape[2]
    scratch[...] = dot(active[...], g_out[...], (0, 0)).astype(BF16)
    for slot, ref, at in place_halves(keep, send):
        piece = piece_of(sc, bits, slot)
        ref[at] = scratch[block_rows(piece >> 1, step_rows), block_rows(piece & 1, step_cols)]


def fc_grad_kernel(bits, sc, normed, g_hidden, keep, send, scratch):
    step_rows, step_cols = keep.shape[1], keep.shape[2]
    quarter = step_rows // WAYS
    scratch[...] = dot(normed[...], g_hidden[...], (0, 0)).astype(BF16)
    for slot, ref, at in place_halves(keep, send):
        piece = piece_of(sc, bits, slot)
        for k in range(WAYS):
            start = (sc[0] ^ k) * WAYS + (piece >> 1)
            ref[at, k * quarter : (k + 1) * quarter, :] = scratch[
                block_rows(start, quarter), block_rows(piece & 1, step_cols)
            ]


def second_back_kernel(sc, own, got, far, residual, cot, table, g_residual, g_branch, rows_out):
    upstream = own[...] + got[...].astype(F32) + far[...].astype(F32)
    scaled, inverse = normalise(residual[...])
    through = norm_back(upstream, scaled, inverse, table[3:4, :])
    g_out = jnp.where(valid_rows(sc, table, sc[0], cot.shape[0]), cot[...].astype(F32), 0.0)
    value = g_out + through
    g_residual[...] = value
    low = value.astype(BF16)
    g_branch[...] = low
    rows_out[0:1, :] = jnp.sum(upstream * scaled, axis=0, keepdims=True)
    rows_out[1:2, :] = jnp.sum(upstream, axis=0, keepdims=True)
    rows_out[2:3, :] = jnp.sum(low.astype(F32), axis=0, keepdims=True)


def pull_kernel(sc, b0, b1, b2, b3, out_w, attended, g_branch, do_ext):
    rows = b0.shape[0]
    width = attended.shape[1]
    heads = width // HD
    for k, ref in enumerate((b0, b1, b2, b3)):
        place = member_rows(sc[0] ^ k, rows)
        g_branch[place, :] = ref[...]
        low = dot(ref[...], out_w[...], (1, 1)).astype(BF16)
        product = low.astype(F32) * attended[place, :]
        split = [
            split3(jnp.sum(product[:, h * HD : (h + 1) * HD], axis=-1, keepdims=True))
            for h in range(heads)
        ]
        columns = [split[h][part] for part in range(3) for h in range(heads)]
        do_ext[place, :width] = low
        do_ext[place, width:] = lanes(columns, rows, do_ext.shape[1] - width, BF16)


def pair_back(q, do, kv, allowed, g_q=None, g_kv=None, q_in=None):
    total = kv.shape[0]
    width = kv.shape[1] // 2
    rows = total // WAYS
    heads = width // HD
    for jq in range(WAYS):
        place = slice(jq * rows, (jq + 1) * rows)
        tail_q = q[place, width:].astype(F32)
        tail_do = do[place, width:].astype(F32)
        for h in range(heads):
            cols = slice(h * HD, (h + 1) * HD)
            vcols = slice(width + h * HD, width + (h + 1) * HD)
            qh = q[place, cols]
            doh = do[place, cols]
            pick = lambda t: (
                t[:, h : h + 1] + t[:, heads + h : heads + h + 1]
            ) + t[:, 2 * heads + h : 2 * heads + h + 1]
            lse, delta = pick(tail_q), pick(tail_do)
            grad = None if q_in is None else q_in[place, cols]
            for diag in ((True, False) if jq > 0 else (True,)):
                keys = place if diag else slice(0, jq * rows)
                scores = dot(qh, kv[keys, cols], (1, 1))
                weight = jnp.exp(scores - lse)
                if diag:
                    weight = jnp.where(allowed, weight, 0.0)
                pulled = dot(doh, kv[keys, vcols], (1, 1))
                low = (weight * (pulled - delta)).astype(BF16)
                if g_q is not None:
                    more = dot(low, kv[keys, cols], (1, 0))
                    grad = more if grad is None else grad + more
                if g_kv is not None:
                    g_kv[keys, cols] += dot(low, qh, (0, 0))
                    g_kv[keys, vcols] += dot(weight.astype(BF16), doh, (0, 0))
            if g_q is not None:
                g_q[place, cols] = grad


def ahead_of(rows):
    return lax.broadcasted_iota(jnp.int32, (rows, rows), 1) - lax.broadcasted_iota(
        jnp.int32, (rows, rows), 0
    )


def back_first(sc, q, do, kv, g_q, g_kv):
    g_kv[...] = jnp.zeros_like(g_kv)
    pair_back(q, do, kv, ahead_of(kv.shape[0] // WAYS) <= 0, g_q, g_kv)


def back_queries(sc, step, q, do, kv_other, q_in, g_q):
    limit = jnp.where((sc[2] ^ step) < sc[2], 1, -1)
    rows = kv_other.shape[0] // WAYS
    pair_back(q, do, kv_other, jnp.zeros((rows, rows), jnp.int32) <= limit, g_q=g_q, q_in=q_in)


def back_keys(sc, step, last, refs):
    q_other, do_other, kv, kv_in = refs[:4]
    if last:
        q_in, full, scales, g_proj, own, far, sent, sent_own, sums, g_kv, scratch = refs[4:]
    else:
        (g_kv,) = refs[4:]
    width = kv.shape[1] // 2
    rows = kv.shape[0] // WAYS
    limit = jnp.where(sc[2] < (sc[2] ^ step), 1, -1)
    g_kv[...] = kv_in[...]
    pair_back(q_other, do_other, kv, jnp.zeros((rows, rows), jnp.int32) <= limit, g_kv=g_kv)
    if last:
        g_proj[:, :width] = (q_in[...] * 0.125).astype(BF16)
        g_proj[:, width:] = g_kv[...].astype(BF16)
        scratch[...] = dot(g_proj[...], full[...], (1, 1))
        emit_partials(sc, rows, scratch, own, far, sent, sent_own)
        sums[0:1, :] = jnp.sum(scratch[...] * scales[...].astype(F32), axis=0, keepdims=True)
        sums[1:2, :] = jnp.sum(scratch[...], axis=0, keepdims=True)


def out_grad_kernel(bits, sc, attended, g_branch, slots, scratch):
    scratch[...] = dot(attended[...], g_branch[...], (0, 0)).astype(BF16)
    rows, cols = scratch.shape[0] // WAYS, scratch.shape[1] // 2
    tall, rest = 2 * rows // 3, rows // 3
    for slot in range(PIECES):
        piece = piece_of(sc, bits, slot)
        block = scratch[block_rows(piece >> 1, rows), block_rows(piece & 1, cols)]
        slots[slot, :, :cols] = block[:tall]
        slots[slot, :rest, cols:] = block[tall:, : cols // 2]
        slots[slot, rest:, cols:] = block[tall:, cols // 2 :]


def qkv_grad_kernel(
    near_bits, far_bits, sc, normed, g_proj, out, two, proj, fc, one, nk, ns, vec, wk, ws, scratch, rows_out
):
    half = PIECES // 2
    step = scratch.shape[0] // WAYS // PIECES
    width = nk.shape[1] // 3
    scratch[...] = dot(normed[...], g_proj[...], (0, 0))
    for base, bits, keep, send in ((2, far_bits, wk, ws), (0, near_bits, nk, ns)):
        size = keep.shape[0] // half
        for slot in range(PIECES):
            ref, at = (keep, slot) if slot < half else (send, slot - half)
            piece = piece_of(sc, bits, slot)
            for i in range(2):
                start = (sc[0] ^ (base + i)) * PIECES + piece
                ref[at * size + i * step : at * size + (i + 1) * step, :] = scratch[
                    block_rows(start, step), :
                ].astype(BF16)
            if base == 2:
                ref[at * size + 2 * step : (at + 1) * size, :] = out[slot]
    rows_out[0:2, :] = one[...]
    rows_out[2:3, :] = two[2:3, :]
    rows_out[3:5, :] = two[0:2, :]
    rows_out[5:6, :] = proj[...]
    rows_out[6:8, :] = jnp.zeros_like(rows_out[6:8, :])
    rows_out[8:12, :] = jnp.zeros_like(rows_out[8:12, :])
    total = jnp.sum(g_proj[...].astype(F32), axis=0, keepdims=True)
    for block in range(WAYS):

        @pl.when(sc[0] == block)
        def _(block=block):
            place = slice(block * width, (block + 1) * width)
            rows_out[6:7, place] = total[:, :width]
            rows_out[7:8, place] = total[:, 2 * width :]
            rows_out[8 + block : 9 + block, :] = fc[...]

    for row in range(VECTOR_ROWS):
        for block in range(WAYS):
            vec[vector_place(row, block, width)] = rows_out[
                row : row + 1, block * width : (block + 1) * width
            ].astype(BF16)
    ns[nk.shape[0] :, :] = vec[...]


def first_back_kernel(sc, own, got, far, x, table, g_residual, r_own, r_got, r_far, residual, out):
    upstream = own[...] + got[...].astype(F32) + far[...].astype(F32)
    scaled, inverse = normalise(x[...].astype(F32))
    through = norm_back(upstream, scaled, inverse, table[0:1, :])
    out[1] = (g_residual[...] + through).astype(BF16)
    value = (
        residual[...] + r_own[...] + r_got[...].astype(F32) + r_far[...].astype(F32) + table[5:6, :]
    )
    out[0] = jnp.where(valid_rows(sc, table, sc[0], x.shape[0]), value, 0.0).astype(BF16)


def slots_in(near, far):
    half = near.shape[0]
    return [(slot, near if slot < half else far, slot % half) for slot in range(2 * half)]


def proj_final_kernel(bits, sc, near, far, out):
    rows, cols = near.shape[1:]
    for slot, ref, at in slots_in(near, far):
        piece = piece_of(sc, bits, slot)
        out[block_rows(piece >> 1, rows), block_rows(piece & 1, cols)] = ref[at].astype(F32)


def fc_final_kernel(bits, sc, near, far, out):
    quarter, step_cols = near.shape[1] // WAYS, near.shape[2]
    for slot, ref, at in slots_in(near, far):
        piece = piece_of(sc, bits, slot)
        for k in range(WAYS):
            wide = block_rows((sc[0] ^ k) * 2 + (piece & 1), step_cols)
            out[block_rows(piece >> 1, quarter), wide] = ref[
                at, k * quarter : (k + 1) * quarter
            ].astype(F32)


def qkv_final_kernel(near_bits, far_bits, sc, nn, nf, wn, wf, out, out_out):
    step, width = nn.shape[1] // 2, nn.shape[2] // 3
    cols = out_out.shape[1] // 2
    rows = out_out.shape[0] // WAYS
    tall, rest = 2 * rows // 3, rows // 3
    for slot, ref, at in slots_in(wn, wf):
        piece = piece_of(sc, far_bits, slot)
        block = ref[at, 2 * step :].astype(F32)
        start = (piece >> 1) * rows
        left = pl.ds(pl.multiple_of((piece & 1) * cols, cols), cols)
        low = pl.ds(pl.multiple_of(start, 8), tall)
        out_out[low, left] = block[:, :cols]
        high = pl.ds(pl.multiple_of(start + tall, 8), rest)
        out_out[high, left] = jnp.concatenate([block[:rest, cols:], block[rest:, cols:]], axis=1)
    for member in range(WAYS):

        @pl.when(sc[0] == member)
        def _(member=member):
            for base, bits, near, far in ((0, near_bits, nn, nf), (2, far_bits, wn, wf)):
                for slot, ref, at in slots_in(near, far):
                    place = block_rows(piece_of(sc, bits, slot), step)
                    for i in range(2):
                        piece = ref[at, i * step : (i + 1) * step].astype(F32)
                        for part in range(3):
                            start = (part * WAYS + (member ^ (base + i))) * width
                            out[place, start : start + width] = piece[
                                :, part * width : (part + 1) * width
                            ]


def body(
    inputs, lengths, ln1_gain, ln1_bias, qkv_weight, qv_bias, out_weight, out_bias,
    ln2_gain, ln2_bias, fc_weight, fc_bias, proj_weight, proj_bias, cotangent,
):
    group = lax.axis_size("ctx")
    members = group // WAYS
    assert lax.axis_size("fsdp") == WAYS and inputs.shape[0] == 1
    assert group % PIECES == 0 and group & (group - 1) == 0
    f, c = lax.axis_index("fsdp"), lax.axis_index("ctx")
    rows, width = inputs.shape[1:]
    head_width = width // WAYS
    hidden_width = fc_bias.shape[0]
    total = rows * WAYS
    half = PIECES // 2
    scalars = jnp.stack(
        [f, c, c % members, jnp.asarray(members), lengths[0], turned(c // members)]
    ).astype(jnp.int32)
    order = Order(scalars)

    vectors = [ln1_gain, ln1_bias, out_bias, ln2_gain, ln2_bias, proj_bias, qv_bias, fc_bias]
    w_qkv = order.call(
        qkv_columns_kernel,
        [
            shape((head_width // (2 if i in (2, 3) else 1), 3 * head_width), BF16)
            for i in range(5)
        ],
        [qkv_weight],
        name="qkv_columns",
    )
    small, fc_row = order.call(
        small_kernel,
        [shape((16, head_width), BF16), shape((1, hidden_width), F32)],
        [jnp.concatenate(vectors)],
        name="small",
    )
    small_all = [small, f_xor(small, 1), f_xor(small, 2), f_xor(small, 3)]
    x_own = swap_layout(inputs[0])
    cot_own = swap_layout(after(cotangent[0], x_own))
    far2, far2_low = f_xor(w_qkv[2], 2), f_xor(w_qkv[3], 2)
    far3, near = f_xor(w_qkv[4], 3), f_xor(w_qkv[1], 1)
    w_qkv = [w_qkv[0], near, far2, far2_low, far3]
    x_far = f_xor(after(x_own, far2, far2_low, small), 2)
    x_all = [x_own, f_xor(x_own, 1), x_far, f_xor(after(x_far, far3), 1)]
    table, qkv_bias = order.call(
        table_kernel,
        [shape((8, width), F32), shape((1, 3 * head_width), F32)],
        small_all,
        flops=4 * 10**9,
        name="table",
        late=[x_own],
    )
    w_fc = order.call(
        fc_columns_kernel,
        [shape((head_width, hidden_width), BF16)] * WAYS,
        [fc_weight],
        name="fc_columns",
    )
    far2, far3, near = f_xor(w_fc[2], 2), f_xor(w_fc[3], 3), f_xor(w_fc[1], 1)
    w_fc = [w_fc[0], near, far2, far3]

    normed_one, scales_one, qkv_full, q, kv = order.call(
        qkv_kernel,
        [
            shape((total, width), BF16),
            shape((total, width), BF16),
            shape((width, 3 * head_width), BF16),
            shape((total, head_width), BF16),
            shape((total, 2 * head_width), BF16),
        ],
        [*x_all, *w_qkv, table, qkv_bias],
        flops=2 * total * width * 3 * head_width,
        name="qkv",
    )
    kv_other = [kv] + [c_xor(kv, r) for r in range(1, members)]

    partials = [shape((rows, width), F32)] * 2 + [shape((rows, width), BF16)] * 2
    state = []
    for r in range(members):
        first, last = r == 0, r == members - 1
        if r == 1:
            cot_all = gather_f(after(cot_own, state[1]))
        if last:
            outs = [
                shape((total, head_width), F32),
                shape((total, head_width), BF16),
                shape((total, head_width + 64), BF16),
                *partials,
            ]
            scratch = [pltpu.VMEM((total, width), F32)]
            extra = [out_weight]
        else:
            outs = [shape((total, head_width), F32), shape((total, 128), F32)]
            scratch, extra = [], []

        def kernel(sc_ref, *refs, r=r, first=first, last=last):
            attend(sc_ref, r, first, last, refs)

        state = order.call(
            kernel,
            outs,
            [q, kv_other[r], *state, *extra],
            scratch,
            flops=4 * total * total * head_width,
            name=f"attend{min(r, 1)}",
            late=[w_fc[2], cot_own] if last else [],
        )
    attended, attended_low, q_ext, *branch = state
    branch = order.scatter_f(*branch)
    q_other = [q_ext] + [c_xor(q_ext, r) for r in range(1, members)]
    (fc_full,) = order.call(
        assemble_kernel,
        [shape((width, hidden_width), BF16)],
        w_fc,
        name="fc_assemble",
        late=[cot_all[2]],
    )
    branch = order.scatter_f_far(branch)
    residual, normed_two = order.call(
        second_norm_kernel,
        [shape((rows, width), F32), shape((rows, width), BF16)],
        [*branch, x_own, table],
        name="norm2",
    )
    normed_two_all = gather_f(normed_two)
    g_out, pulled, proj_row = order.call(
        cot_kernel,
        [
            shape((total, width), BF16),
            shape((total, hidden_width), F32),
            shape((1, width), F32),
        ],
        [*cot_all, proj_weight, table],
        flops=2 * total * width * hidden_width,
        name="cot",
    )
    normed_two_full, active, g_hidden, fc_rows, *g_two = order.call(
        feed_kernel,
        [
            shape((total, width), BF16),
            shape((total, hidden_width), BF16),
            shape((total, hidden_width), BF16),
            shape((1, hidden_width), F32),
            *partials,
        ],
        [*normed_two_all, fc_full, fc_row, pulled],
        [pltpu.VMEM((total, width), F32)],
        flops=4 * total * width * hidden_width,
        name="feed",
        late=q_other[1:],
    )
    g_two = order.scatter_f(*g_two)
    slots = [shape((half, head_width, width // 2), BF16)] * 2
    proj_keep, send = order.call(
        functools.partial(tile_grad_kernel, OTHER),
        slots,
        [active, g_out],
        [pltpu.VMEM((width, width), BF16)],
        flops=2 * total * width * hidden_width,
        name="proj_grad",
    )
    proj_got = c_xor(send, 1 << OTHER[0])
    g_two = order.scatter_f_far(g_two)
    fc_keep, send = order.call(
        functools.partial(fc_grad_kernel, ONE),
        slots,
        [normed_two_full, g_hidden],
        [pltpu.VMEM((width, width), BF16)],
        flops=2 * total * width * hidden_width,
        name="fc_grad",
    )
    fc_got = c_xor(send, 1 << ONE[0])
    result = order.call(
        result_kernel,
        partials,
        [active, proj_weight],
        [pltpu.VMEM((total, width), F32)],
        flops=2 * total * width * hidden_width,
        name="result",
    )
    result = order.scatter_f(*result)
    g_residual, g_branch, two_rows = order.call(
        second_back_kernel,
        [shape((rows, width), F32), shape((rows, width), BF16), shape((3, width), F32)],
        [*g_two, residual, cot_own, table],
        name="norm2_back",
    )
    g_branch_all = gather_f(g_branch)
    g_branch_full, do_ext = order.call(
        pull_kernel,
        [shape((total, width), BF16), shape((total, head_width + 64), BF16)],
        [*g_branch_all, out_weight, attended],
        flops=2 * total * width * head_width,
        name="pull",
    )
    do_other = [do_ext] + [c_xor(do_ext, r) for r in range(1, members)]
    step = head_width // PIECES
    out_rows = head_width // 6
    (out_slots,) = order.call(
        functools.partial(out_grad_kernel, ONE),
        [shape((PIECES, out_rows, 3 * head_width), BF16)],
        [attended_low, g_branch_full],
        [pltpu.VMEM((head_width, width), BF16)],
        flops=2 * total * width * head_width,
        name="out_grad",
    )
    tile = (head_width, width // 2)
    proj_keep, proj_send, fc_keep, fc_send = order.call(
        mlp_fold_kernel,
        [shape((2, *tile), BF16)] * 4,
        [proj_keep, proj_got, fc_keep, fc_got],
        name="mlp_fold",
    )
    result = order.scatter_f_far(result)
    proj_got, fc_got = c_xor(proj_send, 1 << OTHER[1]), c_xor(fc_send, 1 << ONE[1])
    g_q, g_kv = order.call(
        back_first,
        [shape((total, head_width), F32), shape((total, 2 * head_width), F32)],
        [q_ext, do_ext, kv],
        flops=10 * total * total * head_width,
        name="back0",
    )
    mlp_keep, mlp_send = order.call(
        mlp_meet_kernel,
        [shape((2, *tile), BF16)] * 2,
        [proj_keep, proj_got, fc_keep, fc_got],
        name="mlp_meet",
    )
    mlp_got = c_xor(mlp_send, 1 << Z2)
    for r in range(1, members):

        def kernel(sc_ref, *refs, r=r):
            back_queries(sc_ref, r, *refs)

        (g_q,) = order.call(
            kernel,
            [shape(g_q.shape, F32)],
            [q_ext, do_ext, kv_other[r], g_q],
            flops=6 * total * total * head_width,
            name="back_q",
        )
    for r in range(1, members):
        last = r == members - 1
        outs, scratch, extra = [shape(g_kv.shape, F32)], [], []
        if last:
            scratch = [pltpu.VMEM(g_kv.shape, F32), pltpu.VMEM((total, width), F32)]
            outs = [shape((total, 3 * head_width), BF16), *partials, shape((2, width), F32)]
            extra = [g_q, qkv_full, scales_one]

        def kernel(sc_ref, *refs, r=r, last=last):
            back_keys(sc_ref, r, last, refs)

        grads = order.call(
            kernel,
            outs,
            [q_other[r], do_other[r], kv, g_kv, *extra],
            scratch,
            flops=8 * total * total * head_width,
            name="back_kv",
        )
        g_kv = grads[0]
    g_proj, *g_one, one_rows = grads
    g_one = order.scatter_f(*g_one)
    quarter = head_width // WAYS
    pieces = order.call(
        mlp_last_kernel,
        [shape(tile, BF16)] + [shape((quarter, tile[1]), BF16)] * WAYS,
        [mlp_keep, mlp_got],
        name="mlp_last",
    )
    proj_piece, *fc_pieces = [others(piece) for piece in pieces]
    fc_pieces = [fc_pieces[0]] + [f_xor(fc_pieces[k], k) for k in range(1, WAYS)]
    near_rows, far_rows, vec_rows, cols = 2 * step, 2 * step + out_rows, 16, 3 * head_width
    near_keep, near_send, vec, far_keep, far_send = order.call(
        functools.partial(qkv_grad_kernel, OTHER, ONE),
        [
            shape((half * near_rows, cols), BF16),
            shape((half * near_rows + vec_rows, cols), BF16),
            shape((vec_rows, cols), BF16),
            shape((half * far_rows, cols), BF16),
            shape((half * far_rows, cols), BF16),
        ],
        [normed_one, g_proj, out_slots, two_rows, proj_row, fc_rows, one_rows],
        [pltpu.VMEM((width, cols), F32), pltpu.VMEM((VECTOR_ROWS, width), F32)],
        flops=2 * total * width * cols,
        name="qkv_grad",
    )
    near_got, far_got = c_xor(near_send, 1 << OTHER[0]), c_xor(far_send, 1 << ONE[0])
    g_one = order.scatter_f_far(g_one)
    (mlp_own,) = order.call(
        mlp_join_kernel,
        [shape((2, *tile), BF16)],
        [proj_piece, *fc_pieces],
        name="mlp_join",
    )
    mlp_got = c_xor(mlp_own, 1 << Z2)
    near_keep, vec, near_send, far_keep, far_send = order.call(
        qkv_fold_kernel,
        [
            shape((2 * near_rows, cols), BF16),
            shape((vec_rows, cols), BF16),
            shape((2 * near_rows + vec_rows, cols), BF16),
            shape((2 * far_rows, cols), BF16),
            shape((2 * far_rows, cols), BF16),
        ],
        [near_keep, vec, near_got, far_keep, far_got],
        name="qkv_fold",
    )
    near_got, far_got = c_xor(near_send, 1 << OTHER[1]), c_xor(far_send, 1 << ONE[1])
    (both,) = order.call(
        first_back_kernel,
        [shape((2, rows, width), BF16)],
        [*g_one, x_own, table, g_residual, *result, residual],
        name="norm1_back",
    )
    both = swap_layout(both)
    keep, vec, send = order.call(
        qkv_meet_kernel,
        [
            shape((near_rows + far_rows, cols), BF16),
            shape((vec_rows, cols), BF16),
            shape((near_rows + far_rows + vec_rows, cols), BF16),
        ],
        [near_keep, vec, near_got, far_keep, far_got],
        name="qkv_meet",
    )
    got = c_xor(send, 1 << Z2)
    proj_own, fc_own = order.call(
        mlp_part_kernel, [shape((2, *tile), BF16)] * 2, [mlp_own, mlp_got], name="mlp_part"
    )
    proj_got, fc_got = c_xor(proj_own, 1 << OTHER[1]), c_xor(fc_own, 1 << ONE[1])
    proj_own, fc_own = order.call(
        grow_kernel,
        [shape((half, *tile), BF16)] * 2,
        [proj_own, proj_got, fc_own, fc_got],
        name="mlp_grow",
        late=[got],
    )
    proj_got, fc_got = c_xor(proj_own, 1 << OTHER[0]), c_xor(fc_own, 1 << ONE[0])
    piece, vec = order.call(
        qkv_last_kernel,
        [shape((near_rows + far_rows, cols), BF16), shape((vec_rows, cols), BF16)],
        [keep, vec, got],
        name="qkv_last",
    )
    piece, vec = others(piece), others(vec)
    s1, s2, s3 = order.call(
        exchange_kernel, [shape((step + vec_rows, cols), BF16)] * 3, [piece, vec], name="exchange"
    )
    r2, r3, r1 = f_xor(s2, 2), f_xor(s3, 3), f_xor(s1, 1)
    joined, *mine, grad_qv, grad_fc_bias = order.call(
        join_kernel,
        [
            shape((near_rows + far_rows, cols), BF16),
            *[shape((head_width,), F32)] * 6,
            shape((2 * head_width,), F32),
            shape((hidden_width,), F32),
        ],
        [piece, vec, r1, r2, r3],
        [pltpu.VMEM((vec_rows, cols), F32)],
        name="join",
    )
    got = c_xor(joined, 1 << Z2)
    near_own, far_own = order.call(
        qkv_part_kernel,
        [shape((2, near_rows, cols), BF16), shape((2, far_rows, cols), BF16)],
        [joined, got],
        name="qkv_part",
    )
    near_got, far_got = c_xor(near_own, 1 << OTHER[1]), c_xor(far_own, 1 << ONE[1])
    def finish(kernel, dims, arrays, name):
        return order.call(kernel, [shape(d, F32) for d in dims], arrays, name=name, direct=True)

    (grad_fc,) = finish(
        functools.partial(fc_final_kernel, ONE),
        [(head_width, WAYS * hidden_width)],
        [fc_own, fc_got],
        "fc_final",
    )
    (grad_proj,) = finish(
        functools.partial(proj_final_kernel, OTHER),
        [(hidden_width, width)],
        [proj_own, proj_got],
        "proj_final",
    )
    near_own, far_own = order.call(
        grow_kernel,
        [shape((half, near_rows, cols), BF16), shape((half, far_rows, cols), BF16)],
        [near_own, near_got, far_own, far_got],
        name="qkv_grow",
        late=[both],
    )
    near_got, far_got = c_xor(near_own, 1 << OTHER[0]), c_xor(far_own, 1 << ONE[0])

    grad_qkv, grad_out = finish(
        functools.partial(qkv_final_kernel, OTHER, ONE),
        [(head_width, 3 * width), (head_width, width)],
        [near_own, near_got, far_own, far_got],
        "qkv_final",
    )
    return (
        both[0:1],
        both[1:2],
        mine[0],
        mine[1],
        grad_qkv,
        grad_qv,
        grad_out,
        mine[2],
        mine[3],
        mine[4],
        grad_fc,
        grad_fc_bias,
        grad_proj,
        mine[5],
    )


def solution(mesh):
    tokens, rows, vector = P("fsdp", "ctx", None), P("fsdp", None), P("fsdp")
    in_specs = (
        tokens, vector, vector, vector, rows, vector, rows, vector,
        vector, vector, rows, vector, rows, vector, tokens,
    )
    out_specs = (
        tokens, tokens, vector, vector, rows, vector, rows, vector,
        vector, vector, rows, vector, rows, vector,
    )
    return jax.shard_map(body, mesh=mesh, in_specs=in_specs, out_specs=out_specs, check_vma=False)
```

profile of v0, /device:TPU:0, one launch (start us, length us, event | category | flops | bytes accessed | tf_op | source)
XLA Modules:
  0.0 219.9 jit_solution(10611226776217419020)
XLA Ops:
  5.2 4.9 %collective-permute-start.6 = (bf16[96,576]{1,0:T(8,128)(2,1)S(1)}, bf16[96,576]{1,0:T(8,128)(2,1)S(1)}, u32[]{:S(2)}, u32[]{:S(2)}) collective-permute-start(bf16[96,576]{1,0:T(8,128)(2,1)S(1)} %get-tuple-element.184), channel_id=1, source_target_pairs={{0,16},{8,24},{16,0},{24,8},{1,17},{9,25},{17,1},{25,9},{2,18},{10... | collective-permute-start | bytes 331784 | tf_op jit(solution)/shard_map/ppermute | solution.py:24
  10.2 3.1 %collective-permute-start.8 = (bf16[192,576]{1,0:T(8,128)(2,1)S(1)}, bf16[192,576]{1,0:T(8,128)(2,1)S(1)}, u32[]{:S(2)}, u32[]{:S(2)}) collective-permute-start(bf16[192,576]{1,0:T(8,128)(2,1)S(1)} %get-tuple-element.186), channel_id=1, source_target_pairs={{0,24},{8,16},{16,8},{24,0},{1,25},{9,17},{17,9},{25,1},{2,26},{10... | collective-permute-start | bytes 663560 | tf_op jit(solution)/shard_map/ppermute | solution.py:24
  13.3 5.5 %concatenate.3.vectors = bf16[2304]{0:T(1024)(128)(2,1)S(1)} concatenate(bf16[192]{0:T(256)(128)(2,1)} %param.17, bf16[192]{0:T(256)(128)(2,1)} %param.18, bf16[192]{0:T(256)(128)(2,1)} %param.22, bf16[192]{0:T(256)(128)(2,1)} %param.23, bf16[192]{0:T(256)(128)(2,1)} %param.24, bf16[192]{0:T(256)(128)(2,1)} %param.28, bf16[384]{0:T(512)(128)(2,1)} %param.20, bf16[768]{0:T(1024)(128)(2,1)} %param.26), dimensions={0} | concatenate | bytes 9216 | tf_op jit(solution)/shard_map/concatenate | solution.py:822
  24.4 3.9 %collective-permute-done.7.x2 = bf16[128,768]{1,0:T(8,128)(2,1)S(1)} collective-permute-done((bf16[128,768]{1,0:T(8,128)(2,1)S(1)}, bf16[128,768]{1,0:T(8,128)(2,1)S(1)}, u32[]{:S(2)}, u32[]{:S(2)}) %collective-permute-start.7) | collective-permute-done | bytes 196640 | tf_op jit(solution)/shard_map/ppermute | solution.py:24
  33.8 2.5 %collective-permute-start.11 = (bf16[192,768]{1,0:T(8,128)(2,1)S(1)}, bf16[192,768]{1,0:T(8,128)(2,1)S(1)}, u32[]{:S(2)}, u32[]{:S(2)}) collective-permute-start(bf16[192,768]{1,0:T(8,128)(2,1)S(1)} %get-tuple-element.196), channel_id=1, source_target_pairs={{0,16},{8,24},{16,0},{24,8},{1,17},{9,25},{17,1},{25,9},{2,18},{10... | collective-permute-start | bytes 884744 | tf_op jit(solution)/shard_map/ppermute | solution.py:24
  40.4 4.0 %attend0.1 = (f32[512,192]{1,0:T(8,128)S(1)}, f32[512,128]{1,0:T(8,128)S(1)}) custom-call(s32[6]{0:T(128)S(1)} %stack.19.sc.sc_ref, bf16[512,192]{1,0:T(8,128)(2,1)S(1)} %get-tuple-element.191.refs_0_, bf16[512,384]{1,0:T(8,128)(2,1)S(1)} %get-tuple-element.193.refs_1_.kv.refs_2_), custom_call_target="tpu_custom_call" | custom-call | flops 201326592 | bytes 1245208 | tf_op jit(solution)/shard_map/attend0/pallas_call | solution.py:105
  44.5 3.5 %collective-permute-done.11.w2 = bf16[192,768]{1,0:T(8,128)(2,1)S(1)} collective-permute-done((bf16[192,768]{1,0:T(8,128)(2,1)S(1)}, bf16[192,768]{1,0:T(8,128)(2,1)S(1)}, u32[]{:S(2)}, u32[]{:S(2)}) %collective-permute-start.11) | collective-permute-done | bytes 294944 | tf_op jit(solution)/shard_map/ppermute | solution.py:24
  48.0 2.5 %collective-permute-start.14 = (bf16[128,768]{1,0:T(8,128)(2,1)S(1)}, bf16[128,768]{1,0:T(8,128)(2,1)S(1)}, u32[]{:S(2)}, u32[]{:S(2)}) collective-permute-start(bf16[128,768]{1,0:T(8,128)(2,1)S(1)} %collective-permute-done.12.c0.cot), channel_id=1, source_target_pairs={{0,16},{8,24},{16,0},{24,8},{1,17},{9,25},{17,1},{25,9},{2,18},{10... | collective-permute-start | bytes 589832 | tf_op jit(solution)/shard_map/ppermute | solution.py:24
  50.5 6.5 %attend1.1 = (f32[512,192]{1,0:T(8,128)S(1)}, bf16[512,192]{1,0:T(8,128)(2,1)S(1)}, bf16[512,256]{1,0:T(8,128)(2,1)S(1)}, f32[128,768]{1,0:T(8,128)S(1)}, f32[12...) custom-call(s32[6]{0:T(128)S(1)} %stack.19.sc.sc_ref, ...), custom_call_target="tpu_custom_call" | custom-call | flops 201326592 | bytes 3571736 | tf_op jit(solution)/shard_map/attend1/pallas_call | solution.py:105
  59.1 2.4 %collective-permute-start.19 = (bf16[128,768]{1,0:T(8,128)(2,1)S(1)}, bf16[128,768]{1,0:T(8,128)(2,1)S(1)}, u32[]{:S(2)}, u32[]{:S(2)}) collective-permute-start(bf16[128,768]{1,0:T(8,128)(2,1)S(1)} %far.4), channel_id=1, source_target_pairs={{0,16},{8,24},{16,0},{24,8},{1,17},{9,25},{17,1},{25,9},{2,18},{10... | collective-permute-start | bytes 589832 | tf_op jit(solution)/shard_map/ppermute | solution.py:24
  61.5 5.6 %collective-permute-done.19.far = bf16[128,768]{1,0:T(8,128)(2,1)S(1)} collective-permute-done((bf16[128,768]{1,0:T(8,128)(2,1)S(1)}, bf16[128,768]{1,0:T(8,128)(2,1)S(1)}, u32[]{:S(2)}, u32[]{:S(2)}) %collective-permute-start.19) | collective-permute-done | bytes 196640 | tf_op jit(solution)/shard_map/ppermute | solution.py:24
  70.7 3.9 %collective-permute-done.24.n2 = bf16[128,768]{1,0:T(8,128)(2,1)S(1)} collective-permute-done((bf16[128,768]{1,0:T(8,128)(2,1)S(1)}, bf16[128,768]{1,0:T(8,128)(2,1)S(1)}, u32[]{:S(2)}, u32[]{:S(2)}) %collective-permute-start.24) | collective-permute-done | bytes 196640 | tf_op jit(solution)/shard_map/ppermute | solution.py:24
  77.2 3.2 %feed.1 = (bf16[512,768]{1,0:T(8,128)(2,1)S(1)}, bf16[512,768]{1,0:T(8,128)(2,1)S(1)}, bf16[512,768]{1,0:T(8,128)(2,1)S(1)}, f32[1,768]{1,0:T(1,128)S(1)}, f32[1...) custom-call(s32[6]{0:T(128)S(1)} %stack.19.sc.sc_ref, ...), custom_call_target="tpu_custom_call" | custom-call | flops 1207959552 | bytes 7084056 | tf_op jit(solution)/shard_map/feed/pallas_call | solution.py:105
  93.0 4.7 %collective-permute-done.30.b2 = bf16[128,768]{1,0:T(8,128)(2,1)S(1)} collective-permute-done((bf16[128,768]{1,0:T(8,128)(2,1)S(1)}, bf16[128,768]{1,0:T(8,128)(2,1)S(1)}, u32[]{:S(2)}, u32[]{:S(2)}) %collective-permute-start.30) | collective-permute-done | bytes 196640 | tf_op jit(solution)/shard_map/ppermute | solution.py:24
  107.0 6.4 %back0.1 = (f32[512,192]{1,0:T(8,128)S(1)}, f32[512,384]{1,0:T(8,128)S(1)}) custom-call(s32[6]{0:T(128)S(1)} %stack.19.sc.sc_ref, bf16[512,256]{1,0:T(8,128)(2,1)S(1)} %get-tuple-element.216.q.refs_0_, bf16[512,256]{1,0:T(8,128)(2,1)S(1)} %get-tuple-element.240.do.refs_1_, bf16[512,384]{1,0:T(8,128)(2,1)S(1)} %get-tuple-element.193.refs_1_.kv.refs_2_), custom_call_target="tpu_custom_call" | custom-call | flops 503316480 | bytes 2097176 | tf_op jit(solution)/shard_map/back0/pallas_call | solution.py:105
  115.5 4.3 %back_q.1.refs_4_ = f32[512,192]{1,0:T(8,128)S(1)} custom-call(s32[6]{0:T(128)S(1)} %stack.19.sc.sc_ref, bf16[512,256]{1,0:T(8,128)(2,1)S(1)} %get-tuple-element.216.q.refs_0_, bf16[512,256]{1,0:T(8,128)(2,1)S(1)} %get-tuple-element.240.do.refs_1_, bf16[512,384]{1,0:T(8,128)(2,1)S(1)} %collective-permute-done.13.refs_1_.refs_2_, ...), custom_call_target="tpu_custom_call" | custom-call | flops 301989888 | bytes 1703960 | tf_op jit(solution)/shard_map/back_q/pallas_call | solution.py:105
  119.8 7.6 %back_kv.1 = (bf16[512,576]{1,0:T(8,128)(2,1)S(1)}, f32[128,768]{1,0:T(8,128)S(1)}, f32[128,768]{1,0:T(8,128)S(1)}, bf16[128,768]{1,0:T(8,128)(2,1)S(1)}, bf16[1...) custom-call(s32[6]{0:T(128)S(1)} %stack.19.sc.sc_ref, bf16[512,256]{1,0:T(8,128)(2,1)S(1)} %collective-permute-done.22.refs_0_, ...), custom_call_target="tpu_custom_call" | custom-call | flops 402653184 | bytes 5543960 | tf_op jit(solution)/shard_map/back_kv/pallas_call | solution.py:105
  127.4 3.1 %collective-permute-done.38.got = bf16[2,192,384]{2,1,0:T(8,128)(2,1)S(1)} collective-permute-done((bf16[2,192,384]{2,1,0:T(8,128)(2,1)S(1)}, bf16[2,192,384]{2,1,0:T(8,128)(2,1)S(1)}, u32[]{:S(2)}, u32[]{:S(2)}) %collective-permute-start.38) | collective-permute-done | bytes 294944 | tf_op jit(solution)/shard_map/ppermute | solution.py:29
  152.0 6.4 %collective-permute-done.51.far_got = bf16[160,576]{1,0:T(8,128)(2,1)S(1)} collective-permute-done((bf16[160,576]{1,0:T(8,128)(2,1)S(1)}, bf16[160,576]{1,0:T(8,128)(2,1)S(1)}, u32[]{:S(2)}, u32[]{:S(2)}) %collective-permute-start.51) | collective-permute-done | bytes 184352 | tf_op jit(solution)/shard_map/ppermute | solution.py:29
  162.6 6.3 %collective-permute-done.53.got = bf16[144,576]{1,0:T(8,128)(2,1)S(1)} collective-permute-done((bf16[144,576]{1,0:T(8,128)(2,1)S(1)}, bf16[144,576]{1,0:T(8,128)(2,1)S(1)}, u32[]{:S(2)}, u32[]{:S(2)}) %collective-permute-start.53) | collective-permute-done | bytes 165920 | tf_op jit(solution)/shard_map/ppermute | solution.py:29
  176.9 3.8 %collective-permute-start.58 = (bf16[40,576]{1,0:T(8,128)(2,1)S(1)}, bf16[40,576]{1,0:T(8,128)(2,1)S(1)}, u32[]{:S(2)}, u32[]{:S(2)}) collective-permute-start(bf16[40,576]{1,0:T(8,128)(2,1)S(1)} %get-tuple-element.311), channel_id=1, source_target_pairs={{0,24},{8,16},{16,8},{24,0},{1,25},{9,17},{17,9},{25,1},{2,26},{10... | collective-permute-start | bytes 138248 | tf_op jit(solution)/shard_map/ppermute | solution.py:24
  183.8 6.6 %collective-permute-start.59 = (bf16[128,576]{1,0:T(8,128)(2,1)S(1)}, bf16[128,576]{1,0:T(8,128)(2,1)S(1)}, u32[]{:S(2)}, u32[]{:S(2)}) collective-permute-start(bf16[128,576]{1,0:T(8,128)(2,1)S(1)} %get-tuple-element.315.own), channel_id=1, source_target_pairs={{0,4},{1,5},{2,6},{3,7},{4,0},{5,1},{6,2},{7,3},{8,12},{9,13},{10,... | collective-permute-start | bytes 442376 | tf_op jit(solution)/shard_map/ppermute | solution.py:29
  190.3 9.9 %collective-permute-done.59.got = bf16[128,576]{1,0:T(8,128)(2,1)S(1)} collective-permute-done((bf16[128,576]{1,0:T(8,128)(2,1)S(1)}, bf16[128,576]{1,0:T(8,128)(2,1)S(1)}, u32[]{:S(2)}, u32[]{:S(2)}) %collective-permute-start.59) | collective-permute-done | bytes 147488 | tf_op jit(solution)/shard_map/ppermute | solution.py:29
  210.8 4.3 %collective-permute-done.64.nf = bf16[4,48,576]{2,1,0:T(8,128)(2,1)S(1)} collective-permute-done((bf16[4,48,576]{2,1,0:T(8,128)(2,1)S(1)}, bf16[4,48,576]{2,1,0:T(8,128)(2,1)S(1)}, u32[]{:S(2)}, u32[]{:S(2)}) %collective-permute-start.64) | collective-permute-done | bytes 221216 | tf_op jit(solution)/shard_map/ppermute | solution.py:29
  (163 shorter events, 102.9 us)
Async XLA Ops:
  0.6 18.8 %collective-permute-start = (bf16[128,768]{1,0:T(8,128)(2,1)}, bf16[128,768]{1,0:T(8,128)(2,1)S(1)}, u32[]{:S(2)}, u32[]{:S(2)}) collective-permute-start(bf16[128,768]{1,0:T(8,128)(2,1)} %bitcast.6), channel_id=1, source_target_pairs={{0,0},{1,1},{2,16},{3,17},{4,8},{5,9},{6,24},{7,25},{8,4},{9,5},{1... | collective-permute-start | bytes 589832 | tf_op jit(solution)/shard_map/ppermute | solution.py:44
  5.2 14.2 %collective-permute-start.6 = (bf16[96,576]{1,0:T(8,128)(2,1)S(1)}, bf16[96,576]{1,0:T(8,128)(2,1)S(1)}, u32[]{:S(2)}, u32[]{:S(2)}) collective-permute-start(bf16[96,576]{1,0:T(8,128)(2,1)S(1)} %get-tuple-element.184), channel_id=1, source_target_pairs={{0,16},{8,24},{16,0},{24,8},{1,17},{9,25},{17,1},{25,9},{2,18},{10... | collective-permute-start | bytes 331784 | tf_op jit(solution)/shard_map/ppermute | solution.py:24
  10.2 13.9 %collective-permute-start.8 = (bf16[192,576]{1,0:T(8,128)(2,1)S(1)}, bf16[192,576]{1,0:T(8,128)(2,1)S(1)}, u32[]{:S(2)}, u32[]{:S(2)}) collective-permute-start(bf16[192,576]{1,0:T(8,128)(2,1)S(1)} %get-tuple-element.186), channel_id=1, source_target_pairs={{0,24},{8,16},{16,8},{24,0},{1,25},{9,17},{17,9},{25,1},{2,26},{10... | collective-permute-start | bytes 663560 | tf_op jit(solution)/shard_map/ppermute | solution.py:24
  32.3 18.2 %collective-permute-start.13 = (bf16[512,384]{1,0:T(8,128)(2,1)S(1)}, bf16[512,384]{1,0:T(8,128)(2,1)S(1)}, u32[]{:S(2)}, u32[]{:S(2)}) collective-permute-start(bf16[512,384]{1,0:T(8,128)(2,1)S(1)} %get-tuple-element.193.refs_1_.kv.refs_2_), channel_id=1, source_target_pairs={{0,1},{1,0},{2,3},{3,2},{4,5},{5,4},{6,7},{7,6},{8,9},{9,8},{10,11... | collective-permute-start | bytes 1179656 | tf_op jit(solution)/shard_map/ppermute | solution.py:29
  33.8 14.1 %collective-permute-start.11 = (bf16[192,768]{1,0:T(8,128)(2,1)S(1)}, bf16[192,768]{1,0:T(8,128)(2,1)S(1)}, u32[]{:S(2)}, u32[]{:S(2)}) collective-permute-start(bf16[192,768]{1,0:T(8,128)(2,1)S(1)} %get-tuple-element.196), channel_id=1, source_target_pairs={{0,16},{8,24},{16,0},{24,8},{1,17},{9,25},{17,1},{25,9},{2,18},{10... | collective-permute-start | bytes 884744 | tf_op jit(solution)/shard_map/ppermute | solution.py:24
  37.2 20.4 %collective-permute-start.15 = (bf16[192,768]{1,0:T(8,128)(2,1)S(1)}, bf16[192,768]{1,0:T(8,128)(2,1)S(1)}, u32[]{:S(2)}, u32[]{:S(2)}) collective-permute-start(bf16[192,768]{1,0:T(8,128)(2,1)S(1)} %get-tuple-element.204), channel_id=1, source_target_pairs={{0,8},{8,0},{16,24},{24,16},{1,9},{9,1},{17,25},{25,17},{2,10},{10... | collective-permute-start | bytes 884744 | tf_op jit(solution)/shard_map/ppermute | solution.py:24
  39.5 18.1 %collective-permute-start.16 = (bf16[192,768]{1,0:T(8,128)(2,1)S(1)}, bf16[192,768]{1,0:T(8,128)(2,1)S(1)}, u32[]{:S(2)}, u32[]{:S(2)}) collective-permute-start(bf16[192,768]{1,0:T(8,128)(2,1)S(1)} %get-tuple-element.205), channel_id=1, source_target_pairs={{0,24},{8,16},{16,8},{24,0},{1,25},{9,17},{17,9},{25,1},{2,26},{10... | collective-permute-start | bytes 884744 | tf_op jit(solution)/shard_map/ppermute | solution.py:24
  82.5 19.5 %collective-permute-start.32 = (bf16[4,192,384]{2,1,0:T(8,128)(2,1)S(1)}, bf16[4,192,384]{2,1,0:T(8,128)(2,1)S(1)}, u32[]{:S(2)}, u32[]{:S(2)}) collective-permute-start(bf16[4,192,384]{2,1,0:T(8,128)(2,1)S(1)} %get-tuple-element.245), channel_id=1, source_target_pairs={{0,2},{1,3},{2,0},{3,1},{4,6},{5,7},{6,4},{7,5},{8,10},{9,11},{10,... | collective-permute-start | bytes 1769480 | tf_op jit(solution)/shard_map/ppermute | solution.py:29
  86.2 15.8 %collective-permute-start.33 = (bf16[4,192,384]{2,1,0:T(8,128)(2,1)S(1)}, bf16[4,192,384]{2,1,0:T(8,128)(2,1)S(1)}, u32[]{:S(2)}, u32[]{:S(2)}) collective-permute-start(bf16[4,192,384]{2,1,0:T(8,128)(2,1)S(1)} %get-tuple-element.246), channel_id=1, source_target_pairs={{0,1},{1,0},{2,3},{3,2},{4,5},{5,4},{6,7},{7,6},{8,9},{9,8},{10,11... | collective-permute-start | bytes 1769480 | tf_op jit(solution)/shard_map/ppermute | solution.py:29
  102.9 10.5 %collective-permute-start.35 = (bf16[2,192,384]{2,1,0:T(8,128)(2,1)S(1)}, bf16[2,192,384]{2,1,0:T(8,128)(2,1)S(1)}, u32[]{:S(2)}, u32[]{:S(2)}) collective-permute-start(bf16[2,192,384]{2,1,0:T(8,128)(2,1)S(1)} %get-tuple-element.254), channel_id=1, source_target_pairs={{0,1},{1,0},{2,3},{3,2},{4,5},{5,4},{6,7},{7,6},{8,9},{9,8},{10,11... | collective-permute-start | bytes 884744 | tf_op jit(solution)/shard_map/ppermute | solution.py:29
  103.5 9.9 %collective-permute-start.36 = (bf16[2,192,384]{2,1,0:T(8,128)(2,1)S(1)}, bf16[2,192,384]{2,1,0:T(8,128)(2,1)S(1)}, u32[]{:S(2)}, u32[]{:S(2)}) collective-permute-start(bf16[2,192,384]{2,1,0:T(8,128)(2,1)S(1)} %get-tuple-element.256), channel_id=1, source_target_pairs={{0,2},{1,3},{2,0},{3,1},{4,6},{5,7},{6,4},{7,5},{8,10},{9,11},{10,... | collective-permute-start | bytes 884744 | tf_op jit(solution)/shard_map/ppermute | solution.py:29
  104.9 14.8 %collective-permute-start.37 = (bf16[512,256]{1,0:T(8,128)(2,1)S(1)}, bf16[512,256]{1,0:T(8,128)(2,1)S(1)}, u32[]{:S(2)}, u32[]{:S(2)}) collective-permute-start(bf16[512,256]{1,0:T(8,128)(2,1)S(1)} %get-tuple-element.240.do.refs_1_), channel_id=1, source_target_pairs={{0,1},{1,0},{2,3},{3,2},{4,5},{5,4},{6,7},{7,6},{8,9},{9,8},{10,11... | collective-permute-start | bytes 786440 | tf_op jit(solution)/shard_map/ppermute | solution.py:29
  114.1 16.4 %collective-permute-start.38 = (bf16[2,192,384]{2,1,0:T(8,128)(2,1)S(1)}, bf16[2,192,384]{2,1,0:T(8,128)(2,1)S(1)}, u32[]{:S(2)}, u32[]{:S(2)}) collective-permute-start(bf16[2,192,384]{2,1,0:T(8,128)(2,1)S(1)} %get-tuple-element.265), channel_id=1, source_target_pairs={{0,4},{1,5},{2,6},{3,7},{4,0},{5,1},{6,2},{7,3},{8,12},{9,13},{10,... | collective-permute-start | bytes 884744 | tf_op jit(solution)/shard_map/ppermute | solution.py:29
  132.8 11.5 %collective-permute-start.44 = (bf16[320,576]{1,0:T(8,128)(2,1)S(1)}, bf16[320,576]{1,0:T(8,128)(2,1)S(1)}, u32[]{:S(2)}, u32[]{:S(2)}) collective-permute-start(bf16[320,576]{1,0:T(8,128)(2,1)S(1)} %get-tuple-element.283), channel_id=1, source_target_pairs={{0,1},{1,0},{2,3},{3,2},{4,5},{5,4},{6,7},{7,6},{8,9},{9,8},{10,11... | collective-permute-start | bytes 1105928 | tf_op jit(solution)/shard_map/ppermute | solution.py:29
  134.2 12.5 %collective-permute-start.47 = (bf16[128,768]{1,0:T(8,128)(2,1)S(1)}, bf16[128,768]{1,0:T(8,128)(2,1)S(1)}, u32[]{:S(2)}, u32[]{:S(2)}) collective-permute-start(bf16[128,768]{1,0:T(8,128)(2,1)S(1)} %get-tuple-element.289), channel_id=1, source_target_pairs={{0,8},{8,0},{16,24},{24,16},{1,9},{9,1},{17,25},{25,17},{2,10},{10... | collective-permute-start | bytes 589832 | tf_op jit(solution)/shard_map/ppermute | solution.py:24
  142.7 16.4 %collective-permute-start.52 = (bf16[2,192,384]{2,1,0:T(8,128)(2,1)S(1)}, bf16[2,192,384]{2,1,0:T(8,128)(2,1)S(1)}, u32[]{:S(2)}, u32[]{:S(2)}) collective-permute-start(bf16[2,192,384]{2,1,0:T(8,128)(2,1)S(1)} %mlp_join.1.own), channel_id=1, source_target_pairs={{0,4},{1,5},{2,6},{3,7},{4,0},{5,1},{6,2},{7,3},{8,12},{9,13},{10,... | collective-permute-start | bytes 884744 | tf_op jit(solution)/shard_map/ppermute | solution.py:29
  146.7 11.7 %collective-permute-start.51 = (bf16[160,576]{1,0:T(8,128)(2,1)S(1)}, bf16[160,576]{1,0:T(8,128)(2,1)S(1)}, u32[]{:S(2)}, u32[]{:S(2)}) collective-permute-start(bf16[160,576]{1,0:T(8,128)(2,1)S(1)} %get-tuple-element.294), channel_id=1, source_target_pairs={{0,2},{1,3},{2,0},{3,1},{4,6},{5,7},{6,4},{7,5},{8,10},{9,11},{10,... | collective-permute-start | bytes 552968 | tf_op jit(solution)/shard_map/ppermute | solution.py:29
  159.6 11.4 %collective-permute-start.55 = (bf16[2,192,384]{2,1,0:T(8,128)(2,1)S(1)}, bf16[2,192,384]{2,1,0:T(8,128)(2,1)S(1)}, u32[]{:S(2)}, u32[]{:S(2)}) collective-permute-start(bf16[2,192,384]{2,1,0:T(8,128)(2,1)S(1)} %get-tuple-element.301.b), channel_id=1, source_target_pairs={{0,2},{1,3},{2,0},{3,1},{4,6},{5,7},{6,4},{7,5},{8,10},{9,11},{10,... | collective-permute-start | bytes 884744 | tf_op jit(solution)/shard_map/ppermute | solution.py:29
  159.7 11.3 %collective-permute-start.54 = (bf16[2,192,384]{2,1,0:T(8,128)(2,1)S(1)}, bf16[2,192,384]{2,1,0:T(8,128)(2,1)S(1)}, u32[]{:S(2)}, u32[]{:S(2)}) collective-permute-start(bf16[2,192,384]{2,1,0:T(8,128)(2,1)S(1)} %get-tuple-element.297.a), channel_id=1, source_target_pairs={{0,1},{1,0},{2,3},{3,2},{4,5},{5,4},{6,7},{7,6},{8,9},{9,8},{10,11... | collective-permute-start | bytes 884744 | tf_op jit(solution)/shard_map/ppermute | solution.py:29
  171.7 30.8 %collective-permute-start.60 = (bf16[4,192,384]{2,1,0:T(8,128)(2,1)S(1)}, bf16[4,192,384]{2,1,0:T(8,128)(2,1)S(1)}, u32[]{:S(2)}, u32[]{:S(2)}) collective-permute-start(bf16[4,192,384]{2,1,0:T(8,128)(2,1)S(1)} %get-tuple-element.318.near), channel_id=1, source_target_pairs={{0,1},{1,0},{2,3},{3,2},{4,5},{5,4},{6,7},{7,6},{8,9},{9,8},{10,11... | collective-permute-start | bytes 1769480 | tf_op jit(solution)/shard_map/ppermute | solution.py:29
  172.5 32.2 %collective-permute-start.61 = (bf16[4,192,384]{2,1,0:T(8,128)(2,1)S(1)}, bf16[4,192,384]{2,1,0:T(8,128)(2,1)S(1)}, u32[]{:S(2)}, u32[]{:S(2)}) collective-permute-start(bf16[4,192,384]{2,1,0:T(8,128)(2,1)S(1)} %get-tuple-element.302.near), channel_id=1, source_target_pairs={{0,2},{1,3},{2,0},{3,1},{4,6},{5,7},{6,4},{7,5},{8,10},{9,11},{10,... | collective-permute-start | bytes 1769480 | tf_op jit(solution)/shard_map/ppermute | solution.py:29
  176.2 30.5 %collective-permute-start.49 = (bf16[2,128,768]{2,1,0:T(8,128)(2,1)S(1)}, bf16[2,128,768]{2,1,0:T(8,128)(2,1)S(1)}, u32[]{:S(2)}, u32[]{:S(2)}) collective-permute-start(bf16[2,128,768]{2,1,0:T(8,128)(2,1)S(1)} %norm1_back.1), channel_id=1, source_target_pairs={{0,0},{1,1},{2,16},{3,17},{4,8},{5,9},{6,24},{7,25},{8,4},{9,5},{1... | collective-permute-start | bytes 1179656 | tf_op jit(solution)/shard_map/ppermute | solution.py:44
  183.8 16.4 %collective-permute-start.59 = (bf16[128,576]{1,0:T(8,128)(2,1)S(1)}, bf16[128,576]{1,0:T(8,128)(2,1)S(1)}, u32[]{:S(2)}, u32[]{:S(2)}) collective-permute-start(bf16[128,576]{1,0:T(8,128)(2,1)S(1)} %get-tuple-element.315.own), channel_id=1, source_target_pairs={{0,4},{1,5},{2,6},{3,7},{4,0},{5,1},{6,2},{7,3},{8,12},{9,13},{10,... | collective-permute-start | bytes 442376 | tf_op jit(solution)/shard_map/ppermute | solution.py:29
  207.3 9.9 %collective-permute-start.65 = (bf16[4,80,576]{2,1,0:T(8,128)(2,1)S(1)}, bf16[4,80,576]{2,1,0:T(8,128)(2,1)S(1)}, u32[]{:S(2)}, u32[]{:S(2)}) collective-permute-start(bf16[4,80,576]{2,1,0:T(8,128)(2,1)S(1)} %get-tuple-element.325.wn), channel_id=1, source_target_pairs={{0,1},{1,0},{2,3},{3,2},{4,5},{5,4},{6,7},{7,6},{8,9},{9,8},{10,11... | collective-permute-start | bytes 1105928 | tf_op jit(solution)/shard_map/ppermute | solution.py:29
  (47 other events, 278.0 us)
where the time goes:
time: 223 us; the launch traced here: 220 us
  waiting for transfers between devices  70.7 us (32%)
  starting transfers between devices  70.2 us (31%)
  Pallas kernels  69.3 us (31%)
  local copies, waits for them, and re-layouts  7.5 us (3%)
  between operations  2.27 us (1%)
    pallas_call x42, Pallas kernels, call(): pl.pallas_call(kernel, out_shape=tuple(outs), in_specs=[pl.BlockSpec(memo...  69.3 us
    ppermute x40, starting transfers between devices, f_xor(): return lax.ppermute(x, 'fsdp', [(i, i ^ k) for i in range(n)])  40.6 us
    ppermute x23, waiting for transfers between devices, c_xor(): return lax.ppermute(x, 'ctx', [(i, i ^ k) for i in range(n)])  36.8 us
    ppermute x40, waiting for transfers between devices, f_xor(): return lax.ppermute(x, 'fsdp', [(i, i ^ k) for i in range(n)])  33.9 us
    ppermute x23, starting transfers between devices, c_xor(): return lax.ppermute(x, 'ctx', [(i, i ^ k) for i in range(n)])  26.5 us
    concatenate x1, local copies, waits for them, and re-layouts, body(): jnp.concatenate(vectors)  5.46 us
  transfers between devices with their start and end apart: 66, of which 25 were waited for; matrix products, arithmetic and copies ran while one was open for 3% of the time, Pallas kernels for 25%

commit v1 on v0

--- a/solution.py
+++ b/solution.py
@@ -191,17 +191,16 @@
         piece[...] = added(keep[1, place], got[1, place])
 
 
-def mlp_join_kernel(sc, proj, p0, p1, p2, p3, out):
-    out[0] = proj[...]
+def mlp_join_kernel(sc, p0, p1, p2, p3, out):
     rows = p0.shape[0]
     for i, piece in enumerate((p0, p1, p2, p3)):
-        out[1, i * rows : (i + 1) * rows] = piece[...]
-
-
-def mlp_part_kernel(sc, own, got, proj, fc):
-    for i, out in enumerate((proj, fc)):
-        out[0] = own[i]
-        out[1] = got[i]
+        out[i * rows : (i + 1) * rows] = piece[...]
+
+
+def mlp_part_kernel(sc, proj_own, proj_got, fc_own, fc_got, proj, fc):
+    for out, own, got in ((proj, proj_own, proj_got), (fc, fc_own, fc_got)):
+        out[0] = own[...]
+        out[1] = got[...]
 
 
 def grow_kernel(sc, a, a_got, b, b_got, a_out, b_out):
@@ -329,26 +328,41 @@
                 table[6:7, block * width : (block + 1) * width] = row
 
 
-def qkv_columns_kernel(sc, weight, w0, w1, w2, w2_low, w3):
+def half_of(sc, rows):
+    return block_rows(sc[1] & 1, rows)
+
+
+def qkv_columns_kernel(sc, weight, w0, w1, w2, w3):
     width = w0.shape[1] // 3
-    half = w2.shape[0]
-    rows = {0: [(w0, 0)], 1: [(w1, 0)], 2: [(w2, 0), (w2_low, half)], 3: [(w3, 0)]}
-    for k in (2, 3, 1, 0):
+    half = half_of(sc, w2.shape[0])
+    for k, ref in ((2, w2), (3, w3), (1, w1), (0, w0)):
         for block in range(WAYS):
 
             @pl.when((sc[0] ^ k) == block)
-            def _(k=k, block=block):
-                for ref, start in rows[k]:
-                    for part in range(3):
-                        base = part * WAYS * width + block * width
-                        ref[:, part * width : (part + 1) * width] = weight[
-                            start : start + ref.shape[0], base : base + width
-                        ]
+            def _(k=k, ref=ref, block=block):
+                for part in range(3):
+                    base = part * WAYS * width + block * width
+                    source = weight[half if k > 1 else slice(None), base : base + width]
+                    ref[:, part * width : (part + 1) * width] = source
 
 
 def fc_columns_kernel(sc, weight, w0, w1, w2, w3):
     for k, ref in ((2, w2), (3, w3), (1, w1), (0, w0)):
         ref[...] = weight[:, block_rows(sc[0] ^ k, ref.shape[1])]
+
+
+def assemble(sc, near, far, full):
+    for k, ref in enumerate(near):
+        full[block_rows(sc[0] ^ k, ref.shape[0]), :] = ref[...]
+    mine = sc[1] & 1
+    for k, halves in ((2, far[:2]), (3, far[2:])):
+        for i, ref in enumerate(halves):
+            full[block_rows((sc[0] ^ k) * 2 + (mine ^ i), ref.shape[0]), :] = ref[...]
+
+
+def fetched(w0, w1, w2, w3):
+    far2, far3 = f_xor(w2, 2), f_xor(w3, 3)
+    return [w0, f_xor(w1, 1), far2, c_xor(far2, 1 << X), far3, c_xor(far3, 1 << X)]
 
 
 def cot_kernel(sc, c0, c1, c2, c3, proj, table, g_out, pulled, bias_row):
@@ -363,13 +377,9 @@
         pulled[member_rows(j, rows), :] = dot(low, proj[...], (1, 1))
 
 
-def qkv_kernel(sc, x0, x1, x2, x3, w0, w1, w2, w2_low, w3, table, bias, normed, scales, full, q, kv):
-    rows, wrows = x0.shape[0], w0.shape[0]
-    half = wrows // 2
-    for k, ref in ((0, w0), (1, w1), (3, w3)):
-        full[block_rows(sc[0] ^ k, wrows), :] = ref[...]
-    full[block_rows((sc[0] ^ 2) * 2, half), :] = w2[...]
-    full[block_rows((sc[0] ^ 2) * 2 + 1, half), :] = w2_low[...]
+def qkv_kernel(sc, x0, x1, x2, x3, w0, w1, w2, w2_x, w3, w3_x, table, bias, normed, scales, full, q, kv):
+    rows = x0.shape[0]
+    assemble(sc, (w0, w1), (w2, w2_x, w3, w3_x), full)
     for k, ref in enumerate((x0, x1, x2, x3)):
         place = member_rows(sc[0] ^ k, rows)
         scaled, _ = normalise(ref[...].astype(F32))
@@ -409,6 +419,14 @@
 
 def threshold(sc, other):
     return jnp.where(other == sc[2], 0, jnp.where(other < sc[2], 1 << 20, -(1 << 20)))
+
+
+def mask_last(values, allowed, other):
+    rows = allowed.shape[1]
+    masked = jnp.where(allowed, values[:, values.shape[1] - rows :], other)
+    if values.shape[1] == rows:
+        return masked
+    return jnp.concatenate([values[:, : values.shape[1] - rows], masked], axis=1)
 
 
 def attend(sc, step, first, last, refs):
@@ -438,21 +456,16 @@
             cols = slice(h * HD, (h + 1) * HD)
             vcols = slice(width + h * HD, width + (h + 1) * HD)
             qh = q[place, cols]
-            diag = jnp.where(allowed, dot(qh, kv[place, cols], (1, 1)), NEGATIVE)
-            top = jnp.max(diag, axis=-1, keepdims=True)
-            if jq > 0:
-                before = dot(qh, kv[: jq * rows, cols], (1, 1))
-                top = jnp.maximum(top, jnp.max(before, axis=-1, keepdims=True))
+            keys = slice(0, (jq + 1) * rows)
+            scores = dot(qh, kv[keys, cols], (1, 1))
+            scores = mask_last(scores, allowed, NEGATIVE)
+            top = jnp.max(scores, axis=-1, keepdims=True)
             if not first:
                 old = stat_in[place, h : h + 1]
                 top = jnp.maximum(top, old)
-            weight = jnp.exp(diag - top)
+            weight = jnp.exp(scores - top)
             count = jnp.sum(weight, axis=-1, keepdims=True)
-            acc = dot(weight.astype(BF16), kv[place, vcols], (1, 0))
-            if jq > 0:
-                weight = jnp.exp(before - top)
-                count = count + jnp.sum(weight, axis=-1, keepdims=True)
-                acc = acc + dot(weight.astype(BF16), kv[: jq * rows, vcols], (1, 0))
+            acc = dot(weight.astype(BF16), kv[keys, vcols], (1, 0))
             if not first:
                 shrink = jnp.exp(old - top)
                 count = count + shrink * stat_in[place, heads + h : heads + h + 1]
@@ -612,21 +625,18 @@
                 t[:, h : h + 1] + t[:, heads + h : heads + h + 1]
             ) + t[:, 2 * heads + h : 2 * heads + h + 1]
             lse, delta = pick(tail_q), pick(tail_do)
-            grad = None if q_in is None else q_in[place, cols]
-            for diag in ((True, False) if jq > 0 else (True,)):
-                keys = place if diag else slice(0, jq * rows)
-                scores = dot(qh, kv[keys, cols], (1, 1))
-                weight = jnp.exp(scores - lse)
-                if diag:
-                    weight = jnp.where(allowed, weight, 0.0)
-                pulled = dot(doh, kv[keys, vcols], (1, 1))
-                low = (weight * (pulled - delta)).astype(BF16)
-                if g_q is not None:
-                    more = dot(low, kv[keys, cols], (1, 0))
-                    grad = more if grad is None else grad + more
-                if g_kv is not None:
-                    g_kv[keys, cols] += dot(low, qh, (0, 0))
-                    g_kv[keys, vcols] += dot(weight.astype(BF16), doh, (0, 0))
+            keys = slice(0, (jq + 1) * rows)
+            weight = jnp.exp(dot(qh, kv[keys, cols], (1, 1)) - lse)
+            weight = mask_last(weight, allowed, 0.0)
+            pulled = dot(doh, kv[keys, vcols], (1, 1))
+            low = (weight * (pulled - delta)).astype(BF16)
+            if g_q is not None:
+                grad = dot(low, kv[keys, cols], (1, 0))
+                if q_in is not None:
+                    grad = grad + q_in[place, cols]
+            if g_kv is not None:
+                g_kv[keys, cols] += dot(low, qh, (0, 0))
+                g_kv[keys, vcols] += dot(weight.astype(BF16), doh, (0, 0))
             if g_q is not None:
                 g_q[place, cols] = grad
 
@@ -723,15 +733,18 @@
     ns[nk.shape[0] :, :] = vec[...]
 
 
-def first_back_kernel(sc, own, got, far, x, table, g_residual, r_own, r_got, r_far, residual, out):
+def first_back_kernel(sc, own, got, far, x, table, g_residual, input_grad):
     upstream = own[...] + got[...].astype(F32) + far[...].astype(F32)
     scaled, inverse = normalise(x[...].astype(F32))
     through = norm_back(upstream, scaled, inverse, table[0:1, :])
-    out[1] = (g_residual[...] + through).astype(BF16)
+    input_grad[0] = (g_residual[...] + through).astype(BF16)
+
+
+def output_kernel(sc, own, got, far, residual, table, out):
     value = (
-        residual[...] + r_own[...] + r_got[...].astype(F32) + r_far[...].astype(F32) + table[5:6, :]
-    )
-    out[0] = jnp.where(valid_rows(sc, table, sc[0], x.shape[0]), value, 0.0).astype(BF16)
+        residual[...] + own[...] + got[...].astype(F32) + far[...].astype(F32) + table[5:6, :]
+    )
+    out[0] = jnp.where(valid_rows(sc, table, sc[0], out.shape[1]), value, 0.0).astype(BF16)
 
 
 def slots_in(near, far):
@@ -809,10 +822,7 @@
     vectors = [ln1_gain, ln1_bias, out_bias, ln2_gain, ln2_bias, proj_bias, qv_bias, fc_bias]
     w_qkv = order.call(
         qkv_columns_kernel,
-        [
-            shape((head_width // (2 if i in (2, 3) else 1), 3 * head_width), BF16)
-            for i in range(5)
-        ],
+        [shape((head_width // (1 + i // 2), 3 * head_width), BF16) for i in range(WAYS)],
         [qkv_weight],
         name="qkv_columns",
     )
@@ -824,19 +834,17 @@
     )
     small_all = [small, f_xor(small, 1), f_xor(small, 2), f_xor(small, 3)]
     x_own = swap_layout(inputs[0])
-    cot_own = swap_layout(after(cotangent[0], x_own))
-    far2, far2_low = f_xor(w_qkv[2], 2), f_xor(w_qkv[3], 2)
-    far3, near = f_xor(w_qkv[4], 3), f_xor(w_qkv[1], 1)
-    w_qkv = [w_qkv[0], near, far2, far2_low, far3]
-    x_far = f_xor(after(x_own, far2, far2_low, small), 2)
-    x_all = [x_own, f_xor(x_own, 1), x_far, f_xor(after(x_far, far3), 1)]
+    w_qkv = fetched(*w_qkv)
+    x_far = f_xor(after(x_own, w_qkv[2], w_qkv[4], small), 2)
+    x_all = [x_own, f_xor(x_own, 1), x_far, f_xor(x_far, 1)]
+    cot_own = swap_layout(after(cotangent[0], x_far))
     table, qkv_bias = order.call(
         table_kernel,
         [shape((8, width), F32), shape((1, 3 * head_width), F32)],
         small_all,
         flops=4 * 10**9,
         name="table",
-        late=[x_own],
+        late=[x_own, w_qkv[3], w_qkv[5]],
     )
     w_fc = order.call(
         fc_columns_kernel,
@@ -844,8 +852,7 @@
         [fc_weight],
         name="fc_columns",
     )
-    far2, far3, near = f_xor(w_fc[2], 2), f_xor(w_fc[3], 3), f_xor(w_fc[1], 1)
-    w_fc = [w_fc[0], near, far2, far3]
+    w_fc = [w_fc[0]] + [f_xor(w_fc[k], k) for k in range(1, WAYS)]
 
     normed_one, scales_one, qkv_full, q, kv = order.call(
         qkv_kernel,
@@ -891,7 +898,6 @@
             scratch,
             flops=4 * total * total * head_width,
             name=f"attend{min(r, 1)}",
-            late=[w_fc[2], cot_own] if last else [],
         )
     attended, attended_low, q_ext, *branch = state
     branch = order.scatter_f(*branch)
@@ -901,7 +907,6 @@
         [shape((width, hidden_width), BF16)],
         w_fc,
         name="fc_assemble",
-        late=[cot_all[2]],
     )
     branch = order.scatter_f_far(branch)
     residual, normed_two = order.call(
@@ -909,6 +914,7 @@
         [shape((rows, width), F32), shape((rows, width), BF16)],
         [*branch, x_own, table],
         name="norm2",
+        late=[cot_all[2]],
     )
     normed_two_all = gather_f(normed_two)
     g_out, pulled, proj_row = order.call(
@@ -974,6 +980,7 @@
         name="norm2_back",
     )
     g_branch_all = gather_f(g_branch)
+    result = order.scatter_f_far(result)
     g_branch_full, do_ext = order.call(
         pull_kernel,
         [shape((total, width), BF16), shape((total, head_width + 64), BF16)],
@@ -999,8 +1006,11 @@
         [proj_keep, proj_got, fc_keep, fc_got],
         name="mlp_fold",
     )
-    result = order.scatter_f_far(result)
     proj_got, fc_got = c_xor(proj_send, 1 << OTHER[1]), c_xor(fc_send, 1 << ONE[1])
+    (outputs,) = order.call(
+        output_kernel, [shape((1, rows, width), BF16)], [*result, residual, table], name="output"
+    )
+    outputs = swap_layout(outputs)
     g_q, g_kv = order.call(
         back_first,
         [shape((total, head_width), F32), shape((total, 2 * head_width), F32)],
@@ -1013,6 +1023,7 @@
         [shape((2, *tile), BF16)] * 2,
         [proj_keep, proj_got, fc_keep, fc_got],
         name="mlp_meet",
+        late=[outputs],
     )
     mlp_got = c_xor(mlp_send, 1 << Z2)
     for r in range(1, members):
@@ -1049,15 +1060,6 @@
         g_kv = grads[0]
     g_proj, *g_one, one_rows = grads
     g_one = order.scatter_f(*g_one)
-    quarter = head_width // WAYS
-    pieces = order.call(
-        mlp_last_kernel,
-        [shape(tile, BF16)] + [shape((quarter, tile[1]), BF16)] * WAYS,
-        [mlp_keep, mlp_got],
-        name="mlp_last",
-    )
-    proj_piece, *fc_pieces = [others(piece) for piece in pieces]
-    fc_pieces = [fc_pieces[0]] + [f_xor(fc_pieces[k], k) for k in range(1, WAYS)]
     near_rows, far_rows, vec_rows, cols = 2 * step, 2 * step + out_rows, 16, 3 * head_width
     near_keep, near_send, vec, far_keep, far_send = order.call(
         functools.partial(qkv_grad_kernel, OTHER, ONE),
@@ -1074,14 +1076,21 @@
         name="qkv_grad",
     )
     near_got, far_got = c_xor(near_send, 1 << OTHER[0]), c_xor(far_send, 1 << ONE[0])
+    quarter = head_width // WAYS
+    pieces = order.call(
+        mlp_last_kernel,
+        [shape(tile, BF16)] + [shape((quarter, tile[1]), BF16)] * WAYS,
+        [mlp_keep, mlp_got],
+        name="mlp_last",
+    )
+    proj_piece, *fc_pieces = [others(piece) for piece in pieces]
+    proj_got = c_xor(proj_piece, 1 << Z2)
+    fc_pieces = [fc_pieces[0]] + [f_xor(fc_pieces[k], k) for k in range(1, WAYS)]
     g_one = order.scatter_f_far(g_one)
-    (mlp_own,) = order.call(
-        mlp_join_kernel,
-        [shape((2, *tile), BF16)],
-        [proj_piece, *fc_pieces],
-        name="mlp_join",
-    )
-    mlp_got = c_xor(mlp_own, 1 << Z2)
+    (fc_piece,) = order.call(
+        mlp_join_kernel, [shape(tile, BF16)], fc_pieces, name="mlp_join"
+    )
+    fc_got = c_xor(fc_piece, 1 << Z2)
     near_keep, vec, near_send, far_keep, far_send = order.call(
         qkv_fold_kernel,
         [
@@ -1093,15 +1102,16 @@
         ],
         [near_keep, vec, near_got, far_keep, far_got],
         name="qkv_fold",
+        late=[proj_got],
     )
     near_got, far_got = c_xor(near_send, 1 << OTHER[1]), c_xor(far_send, 1 << ONE[1])
-    (both,) = order.call(
+    (input_grad,) = order.call(
         first_back_kernel,
-        [shape((2, rows, width), BF16)],
-        [*g_one, x_own, table, g_residual, *result, residual],
+        [shape((1, rows, width), BF16)],
+        [*g_one, x_own, table, g_residual],
         name="norm1_back",
     )
-    both = swap_layout(both)
+    input_grad = swap_layout(input_grad)
     keep, vec, send = order.call(
         qkv_meet_kernel,
         [
@@ -1114,7 +1124,10 @@
     )
     got = c_xor(send, 1 << Z2)
     proj_own, fc_own = order.call(
-        mlp_part_kernel, [shape((2, *tile), BF16)] * 2, [mlp_own, mlp_got], name="mlp_part"
+        mlp_part_kernel,
+        [shape((2, *tile), BF16)] * 2,
+        [proj_piece, proj_got, fc_piece, fc_got],
+        name="mlp_part",
     )
     proj_got, fc_got = c_xor(proj_own, 1 << OTHER[1]), c_xor(fc_own, 1 << ONE[1])
     proj_own, fc_own = order.call(
@@ -1157,7 +1170,10 @@
     )
     near_got, far_got = c_xor(near_own, 1 << OTHER[1]), c_xor(far_own, 1 << ONE[1])
     def finish(kernel, dims, arrays, name):
-        return order.call(kernel, [shape(d, F32) for d in dims], arrays, name=name, direct=True)
+        late = [input_grad] if name == "qkv_final" else []
+        return order.call(
+            kernel, [shape(d, F32) for d in dims], arrays, name=name, direct=True, late=late
+        )
 
     (grad_fc,) = finish(
         functools.partial(fc_final_kernel, ONE),
@@ -1176,7 +1192,6 @@
         [shape((half, near_rows, cols), BF16), shape((half, far_rows, cols), BF16)],
         [near_own, near_got, far_own, far_got],
         name="qkv_grow",
-        late=[both],
     )
     near_got, far_got = c_xor(near_own, 1 << OTHER[0]), c_xor(far_own, 1 << ONE[0])
 
@@ -1187,8 +1202,8 @@
         "qkv_final",
     )
     return (
-        both[0:1],
-        both[1:2],
+        outputs,
+        input_grad,
         mine[0],
         mine[1],
         grad_qkv,

time: 223 us -> 209 us (0.937)
  starting transfers between devices: 70.2 us -> 62.7 us
  Pallas kernels: 69.3 us -> 64.3 us
  waiting for transfers between devices: 70.7 us -> 67.8 us
    ppermute x40 -> x39, starting transfers between devices: 40.6 us -> 27.4 us  [f_xor(): return lax.ppermute(x, 'fsdp', [(i, i ^ k) for i in range(n)])]
    ppermute x40 -> x39, waiting for transfers between devices: 33.9 us -> 25.1 us  [f_xor(): return lax.ppermute(x, 'fsdp', [(i, i ^ k) for i in range(n)])]
    ppermute x23 -> x26, waiting for transfers between devices: 36.8 us -> 42.7 us  [c_xor(): return lax.ppermute(x, 'ctx', [(i, i ^ k) for i in range(n)])]
    ppermute x23 -> x26, starting transfers between devices: 26.5 us -> 31.6 us  [c_xor(): return lax.ppermute(x, 'ctx', [(i, i ^ k) for i in range(n)])]
    pallas_call x42 -> x43, Pallas kernels: 69.3 us -> 64.3 us  [call(): pl.pallas_call(kernel, out_shape=tuple(outs), in_specs=[pl.BlockSpec(memo...]
  transfers between devices with their start and end apart: 66 -> 69, of which waited for: 25 -> 26; matrix products, arithmetic and copies ran while one was open for 3% -> 3% of each run, Pallas kernels for 25% -> 26%
where the time goes in v1:
time: 209 us; the launch traced here: 205 us
  waiting for transfers between devices  67.8 us (32%)
  Pallas kernels  64.3 us (31%)
  starting transfers between devices  62.7 us (30%)
  local copies, waits for them, and re-layouts  8.08 us (4%)
    pallas_call x43, Pallas kernels, call(): pl.pallas_call(kernel, out_shape=tuple(outs), in_specs=[pl.BlockSpec(memo...  64.3 us
    ppermute x26, waiting for transfers between devices, c_xor(): return lax.ppermute(x, 'ctx', [(i, i ^ k) for i in range(n)])  42.7 us
    ppermute x26, starting transfers between devices, c_xor(): return lax.ppermute(x, 'ctx', [(i, i ^ k) for i in range(n)])  31.6 us
    ppermute x39, starting transfers between devices, f_xor(): return lax.ppermute(x, 'fsdp', [(i, i ^ k) for i in range(n)])  27.4 us
    ppermute x39, waiting for transfers between devices, f_xor(): return lax.ppermute(x, 'fsdp', [(i, i ^ k) for i in range(n)])  25.1 us
    concatenate x1, local copies, waits for them, and re-layouts, body(): jnp.concatenate(vectors)  5.46 us
  transfers between devices with their start and end apart: 69, of which 26 were waited for; matrix products, arithmetic and copies ran while one was open for 3% of the time, Pallas kernels for 26%

profile of v1, /device:TPU:0, one launch (start us, length us, event | category | flops | bytes accessed | tf_op | source)
XLA Modules:
  0.0 204.8 jit_solution(24990512029689881)
XLA Ops:
  5.2 6.7 %collective-permute-start.3 = (bf16[96,576]{1,0:T(8,128)(2,1)S(1)}, bf16[96,576]{1,0:T(8,128)(2,1)S(1)}, u32[]{:S(2)}, u32[]{:S(2)}) collective-permute-start(bf16[96,576]{1,0:T(8,128)(2,1)S(1)} %get-tuple-element.178), channel_id=1, source_target_pairs={{0,24},{8,16},{16,8},{24,0},{1,25},{9,17},{17,9},{25,1},{2,26},{10... | collective-permute-start | bytes 331784 | tf_op jit(solution)/shard_map/ppermute | solution.py:24
  11.8 5.5 %concatenate.3.vectors = bf16[2304]{0:T(1024)(128)(2,1)S(1)} concatenate(bf16[192]{0:T(256)(128)(2,1)} %param.17, bf16[192]{0:T(256)(128)(2,1)} %param.18, bf16[192]{0:T(256)(128)(2,1)} %param.22, bf16[192]{0:T(256)(128)(2,1)} %param.23, bf16[192]{0:T(256)(128)(2,1)} %param.24, bf16[192]{0:T(256)(128)(2,1)} %param.28, bf16[384]{0:T(512)(128)(2,1)} %param.20, bf16[768]{0:T(1024)(128)(2,1)} %param.26), dimensions={0} | concatenate | bytes 9216 | tf_op jit(solution)/shard_map/concatenate | solution.py:832
  18.9 2.5 %collective-permute-start.9 = (bf16[128,768]{1,0:T(8,128)(2,1)S(1)}, bf16[128,768]{1,0:T(8,128)(2,1)S(1)}, u32[]{:S(2)}, u32[]{:S(2)}) collective-permute-start(bf16[128,768]{1,0:T(8,128)(2,1)S(1)} %collective-permute-done.x0.x), channel_id=1, source_target_pairs={{0,16},{8,24},{16,0},{24,8},{1,17},{9,25},{17,1},{25,9},{2,18},{10... | collective-permute-start | bytes 589832 | tf_op jit(solution)/shard_map/ppermute | solution.py:24
  24.3 3.4 %collective-permute-done.4.w3_x = bf16[96,576]{1,0:T(8,128)(2,1)S(1)} collective-permute-done((bf16[96,576]{1,0:T(8,128)(2,1)S(1)}, bf16[96,576]{1,0:T(8,128)(2,1)S(1)}, u32[]{:S(2)}, u32[]{:S(2)}) %collective-permute-start.4) | collective-permute-done | bytes 110624 | tf_op jit(solution)/shard_map/ppermute | solution.py:29
  37.3 3.6 %attend0.1 = (f32[512,192]{1,0:T(8,128)S(1)}, f32[512,128]{1,0:T(8,128)S(1)}) custom-call(s32[6]{0:T(128)S(1)} %stack.19.sc.sc_ref, bf16[512,192]{1,0:T(8,128)(2,1)S(1)} %get-tuple-element.189.refs_0_, bf16[512,384]{1,0:T(8,128)(2,1)S(1)} %get-tuple-element.191.refs_1_.kv.refs_2_), custom_call_target="tpu_custom_call" | custom-call | flops 201326592 | bytes 1245208 | tf_op jit(solution)/shard_map/attend0/pallas_call | solution.py:105
  41.0 3.6 %collective-permute-done.12.refs_1_.refs_2_ = bf16[512,384]{1,0:T(8,128)(2,1)S(1)} collective-permute-done((bf16[512,384]{1,0:T(8,128)(2,1)S(1)}, bf16[512,384]{1,0:T(8,128)(2,1)S(1)}, u32[]{:S(2)}, u32[]{:S(2)}) %collective-permute-start.12) | collective-permute-done | bytes 393248 | tf_op jit(solution)/shard_map/ppermute | solution.py:29
  44.6 6.4 %attend1.1 = (f32[512,192]{1,0:T(8,128)S(1)}, bf16[512,192]{1,0:T(8,128)(2,1)S(1)}, bf16[512,256]{1,0:T(8,128)(2,1)S(1)}, f32[128,768]{1,0:T(8,128)S(1)}, f32[12...) custom-call(s32[6]{0:T(128)S(1)} %stack.19.sc.sc_ref, ...), custom_call_target="tpu_custom_call" | custom-call | flops 201326592 | bytes 3571736 | tf_op jit(solution)/shard_map/attend1/pallas_call | solution.py:105
  58.9 3.7 %collective-permute-done.20.far = bf16[128,768]{1,0:T(8,128)(2,1)S(1)} collective-permute-done((bf16[128,768]{1,0:T(8,128)(2,1)S(1)}, bf16[128,768]{1,0:T(8,128)(2,1)S(1)}, u32[]{:S(2)}, u32[]{:S(2)}) %collective-permute-start.20) | collective-permute-done | bytes 196640 | tf_op jit(solution)/shard_map/ppermute | solution.py:24
  65.8 4.0 %collective-permute-done.25.n2 = bf16[128,768]{1,0:T(8,128)(2,1)S(1)} collective-permute-done((bf16[128,768]{1,0:T(8,128)(2,1)S(1)}, bf16[128,768]{1,0:T(8,128)(2,1)S(1)}, u32[]{:S(2)}, u32[]{:S(2)}) %collective-permute-start.25) | collective-permute-done | bytes 196640 | tf_op jit(solution)/shard_map/ppermute | solution.py:24
  72.1 3.2 %feed.1 = (bf16[512,768]{1,0:T(8,128)(2,1)S(1)}, bf16[512,768]{1,0:T(8,128)(2,1)S(1)}, bf16[512,768]{1,0:T(8,128)(2,1)S(1)}, f32[1,768]{1,0:T(1,128)S(1)}, f32[1...) custom-call(s32[6]{0:T(128)S(1)} %stack.19.sc.sc_ref, ...), custom_call_target="tpu_custom_call" | custom-call | flops 1207959552 | bytes 7084056 | tf_op jit(solution)/shard_map/feed/pallas_call | solution.py:105
  87.5 5.4 %collective-permute-done.32.b2 = bf16[128,768]{1,0:T(8,128)(2,1)S(1)} collective-permute-done((bf16[128,768]{1,0:T(8,128)(2,1)S(1)}, bf16[128,768]{1,0:T(8,128)(2,1)S(1)}, u32[]{:S(2)}, u32[]{:S(2)}) %collective-permute-start.32) | collective-permute-done | bytes 196640 | tf_op jit(solution)/shard_map/ppermute | solution.py:24
  103.0 4.5 %back0.1 = (f32[512,192]{1,0:T(8,128)S(1)}, f32[512,384]{1,0:T(8,128)S(1)}) custom-call(s32[6]{0:T(128)S(1)} %stack.19.sc.sc_ref, bf16[512,256]{1,0:T(8,128)(2,1)S(1)} %get-tuple-element.213.q.refs_0_, bf16[512,256]{1,0:T(8,128)(2,1)S(1)} %get-tuple-element.240.do.refs_1_, bf16[512,384]{1,0:T(8,128)(2,1)S(1)} %get-tuple-element.191.refs_1_.kv.refs_2_), custom_call_target="tpu_custom_call" | custom-call | flops 503316480 | bytes 2097176 | tf_op jit(solution)/shard_map/back0/pallas_call | solution.py:105
  108.0 2.5 %collective-permute-done.40.fc_got = bf16[2,192,384]{2,1,0:T(8,128)(2,1)S(1)} collective-permute-done((bf16[2,192,384]{2,1,0:T(8,128)(2,1)S(1)}, bf16[2,192,384]{2,1,0:T(8,128)(2,1)S(1)}, u32[]{:S(2)}, u32[]{:S(2)}) %collective-permute-start.40) | collective-permute-done | bytes 294944 | tf_op jit(solution)/shard_map/ppermute | solution.py:29
  111.2 2.9 %back_q.1.refs_4_ = f32[512,192]{1,0:T(8,128)S(1)} custom-call(s32[6]{0:T(128)S(1)} %stack.19.sc.sc_ref, bf16[512,256]{1,0:T(8,128)(2,1)S(1)} %get-tuple-element.213.q.refs_0_, bf16[512,256]{1,0:T(8,128)(2,1)S(1)} %get-tuple-element.240.do.refs_1_, bf16[512,384]{1,0:T(8,128)(2,1)S(1)} %collective-permute-done.12.refs_1_.refs_2_, ...), custom_call_target="tpu_custom_call" | custom-call | flops 301989888 | bytes 1703960 | tf_op jit(solution)/shard_map/back_q/pallas_call | solution.py:105
  114.1 2.5 %collective-permute-start.42 = (bf16[2,192,384]{2,1,0:T(8,128)(2,1)S(1)}, bf16[2,192,384]{2,1,0:T(8,128)(2,1)S(1)}, u32[]{:S(2)}, u32[]{:S(2)}) collective-permute-start(bf16[2,192,384]{2,1,0:T(8,128)(2,1)S(1)} %get-tuple-element.269), channel_id=1, source_target_pairs={{0,4},{1,5},{2,6},{3,7},{4,0},{5,1},{6,2},{7,3},{8,12},{9,13},{10,... | collective-permute-start | bytes 884744 | tf_op jit(solution)/shard_map/ppermute | solution.py:29
  116.6 5.4 %back_kv.1 = (bf16[512,576]{1,0:T(8,128)(2,1)S(1)}, f32[128,768]{1,0:T(8,128)S(1)}, f32[128,768]{1,0:T(8,128)S(1)}, bf16[128,768]{1,0:T(8,128)(2,1)S(1)}, bf16[1...) custom-call(s32[6]{0:T(128)S(1)} %stack.19.sc.sc_ref, bf16[512,256]{1,0:T(8,128)(2,1)S(1)} %collective-permute-done.23.refs_0_, ...), custom_call_target="tpu_custom_call" | custom-call | flops 402653184 | bytes 5543960 | tf_op jit(solution)/shard_map/back_kv/pallas_call | solution.py:105
  124.6 4.3 %collective-permute-start.48 = (bf16[208,576]{1,0:T(8,128)(2,1)S(1)}, bf16[208,576]{1,0:T(8,128)(2,1)S(1)}, u32[]{:S(2)}, u32[]{:S(2)}) collective-permute-start(bf16[208,576]{1,0:T(8,128)(2,1)S(1)} %get-tuple-element.282), channel_id=1, source_target_pairs={{0,2},{1,3},{2,0},{3,1},{4,6},{5,7},{6,4},{7,5},{8,10},{9,11},{10,... | collective-permute-start | bytes 718856 | tf_op jit(solution)/shard_map/ppermute | solution.py:29
  130.2 2.7 %collective-permute-start.45 = (bf16[48,384]{1,0:T(8,128)(2,1)S(1)}, bf16[48,384]{1,0:T(8,128)(2,1)S(1)}, u32[]{:S(2)}, u32[]{:S(2)}) collective-permute-start(bf16[48,384]{1,0:T(8,128)(2,1)S(1)} %get-tuple-element.276), channel_id=1, source_target_pairs={{0,16},{8,24},{16,0},{24,8},{1,17},{9,25},{17,1},{25,9},{2,18},{10... | collective-permute-start | bytes 110600 | tf_op jit(solution)/shard_map/ppermute | solution.py:24
  144.6 3.1 %collective-permute-done.53.near_got = bf16[112,576]{1,0:T(8,128)(2,1)S(1)} collective-permute-done((bf16[112,576]{1,0:T(8,128)(2,1)S(1)}, bf16[112,576]{1,0:T(8,128)(2,1)S(1)}, u32[]{:S(2)}, u32[]{:S(2)}) %collective-permute-start.53) | collective-permute-done | bytes 129056 | tf_op jit(solution)/shard_map/ppermute | solution.py:29
  150.3 2.6 %collective-permute-start.58 = (bf16[2,192,384]{2,1,0:T(8,128)(2,1)S(1)}, bf16[2,192,384]{2,1,0:T(8,128)(2,1)S(1)}, u32[]{:S(2)}, u32[]{:S(2)}) collective-permute-start(bf16[2,192,384]{2,1,0:T(8,128)(2,1)S(1)} %get-tuple-element.301.b), channel_id=1, source_target_pairs={{0,2},{1,3},{2,0},{3,1},{4,6},{5,7},{6,4},{7,5},{8,10},{9,11},{10,... | collective-permute-start | bytes 884744 | tf_op jit(solution)/shard_map/ppermute | solution.py:29
  155.3 8.4 %collective-permute-done.56.got = bf16[144,576]{1,0:T(8,128)(2,1)S(1)} collective-permute-done((bf16[144,576]{1,0:T(8,128)(2,1)S(1)}, bf16[144,576]{1,0:T(8,128)(2,1)S(1)}, u32[]{:S(2)}, u32[]{:S(2)}) %collective-permute-start.56) | collective-permute-done | bytes 165920 | tf_op jit(solution)/shard_map/ppermute | solution.py:29
  175.6 8.8 %collective-permute-done.62.got = bf16[128,576]{1,0:T(8,128)(2,1)S(1)} collective-permute-done((bf16[128,576]{1,0:T(8,128)(2,1)S(1)}, bf16[128,576]{1,0:T(8,128)(2,1)S(1)}, u32[]{:S(2)}, u32[]{:S(2)}) %collective-permute-start.62) | collective-permute-done | bytes 147488 | tf_op jit(solution)/shard_map/ppermute | solution.py:29
  194.8 3.6 %collective-permute-done.67.nf = bf16[4,48,576]{2,1,0:T(8,128)(2,1)S(1)} collective-permute-done((bf16[4,48,576]{2,1,0:T(8,128)(2,1)S(1)}, bf16[4,48,576]{2,1,0:T(8,128)(2,1)S(1)}, u32[]{:S(2)}, u32[]{:S(2)}) %collective-permute-start.67) | collective-permute-done | bytes 221216 | tf_op jit(solution)/shard_map/ppermute | solution.py:29
  198.4 2.8 %collective-permute-done.68.wf = bf16[4,80,576]{2,1,0:T(8,128)(2,1)S(1)} collective-permute-done((bf16[4,80,576]{2,1,0:T(8,128)(2,1)S(1)}, bf16[4,80,576]{2,1,0:T(8,128)(2,1)S(1)}, u32[]{:S(2)}, u32[]{:S(2)}) %collective-permute-start.68) | collective-permute-done | bytes 368672 | tf_op jit(solution)/shard_map/ppermute | solution.py:29
  (171 shorter events, 101.0 us)
Async XLA Ops:
  0.6 18.3 %collective-permute-start = (bf16[128,768]{1,0:T(8,128)(2,1)}, bf16[128,768]{1,0:T(8,128)(2,1)S(1)}, u32[]{:S(2)}, u32[]{:S(2)}) collective-permute-start(bf16[128,768]{1,0:T(8,128)(2,1)} %bitcast.6), channel_id=1, source_target_pairs={{0,0},{1,1},{2,16},{3,17},{4,8},{5,9},{6,24},{7,25},{8,4},{9,5},{1... | collective-permute-start | bytes 589832 | tf_op jit(solution)/shard_map/ppermute | solution.py:44
  5.2 12.7 %collective-permute-start.3 = (bf16[96,576]{1,0:T(8,128)(2,1)S(1)}, bf16[96,576]{1,0:T(8,128)(2,1)S(1)}, u32[]{:S(2)}, u32[]{:S(2)}) collective-permute-start(bf16[96,576]{1,0:T(8,128)(2,1)S(1)} %get-tuple-element.178), channel_id=1, source_target_pairs={{0,24},{8,16},{16,8},{24,0},{1,25},{9,17},{17,9},{25,1},{2,26},{10... | collective-permute-start | bytes 331784 | tf_op jit(solution)/shard_map/ppermute | solution.py:24
  18.9 10.6 %collective-permute-start.9 = (bf16[128,768]{1,0:T(8,128)(2,1)S(1)}, bf16[128,768]{1,0:T(8,128)(2,1)S(1)}, u32[]{:S(2)}, u32[]{:S(2)}) collective-permute-start(bf16[128,768]{1,0:T(8,128)(2,1)S(1)} %collective-permute-done.x0.x), channel_id=1, source_target_pairs={{0,16},{8,24},{16,0},{24,8},{1,17},{9,25},{17,1},{25,9},{2,18},{10... | collective-permute-start | bytes 589832 | tf_op jit(solution)/shard_map/ppermute | solution.py:24
  33.1 11.5 %collective-permute-start.12 = (bf16[512,384]{1,0:T(8,128)(2,1)S(1)}, bf16[512,384]{1,0:T(8,128)(2,1)S(1)}, u32[]{:S(2)}, u32[]{:S(2)}) collective-permute-start(bf16[512,384]{1,0:T(8,128)(2,1)S(1)} %get-tuple-element.191.refs_1_.kv.refs_2_), channel_id=1, source_target_pairs={{0,1},{1,0},{2,3},{3,2},{4,5},{5,4},{6,7},{7,6},{8,9},{9,8},{10,11... | collective-permute-start | bytes 1179656 | tf_op jit(solution)/shard_map/ppermute | solution.py:29
  34.6 16.8 %collective-permute-start.13 = (bf16[192,768]{1,0:T(8,128)(2,1)S(1)}, bf16[192,768]{1,0:T(8,128)(2,1)S(1)}, u32[]{:S(2)}, u32[]{:S(2)}) collective-permute-start(bf16[192,768]{1,0:T(8,128)(2,1)S(1)} %get-tuple-element.197), channel_id=1, source_target_pairs={{0,8},{8,0},{16,24},{24,16},{1,9},{9,1},{17,25},{25,17},{2,10},{10... | collective-permute-start | bytes 884744 | tf_op jit(solution)/shard_map/ppermute | solution.py:24
  34.8 16.7 %collective-permute-start.14 = (bf16[192,768]{1,0:T(8,128)(2,1)S(1)}, bf16[192,768]{1,0:T(8,128)(2,1)S(1)}, u32[]{:S(2)}, u32[]{:S(2)}) collective-permute-start(bf16[192,768]{1,0:T(8,128)(2,1)S(1)} %get-tuple-element.198), channel_id=1, source_target_pairs={{0,16},{8,24},{16,0},{24,8},{1,17},{9,25},{17,1},{25,9},{2,18},{10... | collective-permute-start | bytes 884744 | tf_op jit(solution)/shard_map/ppermute | solution.py:24
  35.1 17.8 %collective-permute-start.15 = (bf16[192,768]{1,0:T(8,128)(2,1)S(1)}, bf16[192,768]{1,0:T(8,128)(2,1)S(1)}, u32[]{:S(2)}, u32[]{:S(2)}) collective-permute-start(bf16[192,768]{1,0:T(8,128)(2,1)S(1)} %get-tuple-element.199), channel_id=1, source_target_pairs={{0,24},{8,16},{16,8},{24,0},{1,25},{9,17},{17,9},{25,1},{2,26},{10... | collective-permute-start | bytes 884744 | tf_op jit(solution)/shard_map/ppermute | solution.py:24
  36.5 14.6 %collective-permute-start.17 = (bf16[128,768]{1,0:T(8,128)(2,1)S(1)}, bf16[128,768]{1,0:T(8,128)(2,1)S(1)}, u32[]{:S(2)}, u32[]{:S(2)}) collective-permute-start(bf16[128,768]{1,0:T(8,128)(2,1)S(1)} %bitcast.7), channel_id=1, source_target_pairs={{0,0},{1,1},{2,16},{3,17},{4,8},{5,9},{6,24},{7,25},{8,4},{9,5},{1... | collective-permute-start | bytes 589832 | tf_op jit(solution)/shard_map/ppermute | solution.py:44
  77.5 19.7 %collective-permute-start.34 = (bf16[4,192,384]{2,1,0:T(8,128)(2,1)S(1)}, bf16[4,192,384]{2,1,0:T(8,128)(2,1)S(1)}, u32[]{:S(2)}, u32[]{:S(2)}) collective-permute-start(bf16[4,192,384]{2,1,0:T(8,128)(2,1)S(1)} %get-tuple-element.245), channel_id=1, source_target_pairs={{0,2},{1,3},{2,0},{3,1},{4,6},{5,7},{6,4},{7,5},{8,10},{9,11},{10,... | collective-permute-start | bytes 1769480 | tf_op jit(solution)/shard_map/ppermute | solution.py:29
  80.7 16.5 %collective-permute-start.35 = (bf16[4,192,384]{2,1,0:T(8,128)(2,1)S(1)}, bf16[4,192,384]{2,1,0:T(8,128)(2,1)S(1)}, u32[]{:S(2)}, u32[]{:S(2)}) collective-permute-start(bf16[4,192,384]{2,1,0:T(8,128)(2,1)S(1)} %get-tuple-element.246), channel_id=1, source_target_pairs={{0,1},{1,0},{2,3},{3,2},{4,5},{5,4},{6,7},{7,6},{8,9},{9,8},{10,11... | collective-permute-start | bytes 1769480 | tf_op jit(solution)/shard_map/ppermute | solution.py:29
  98.1 9.9 %collective-permute-start.39 = (bf16[2,192,384]{2,1,0:T(8,128)(2,1)S(1)}, bf16[2,192,384]{2,1,0:T(8,128)(2,1)S(1)}, u32[]{:S(2)}, u32[]{:S(2)}) collective-permute-start(bf16[2,192,384]{2,1,0:T(8,128)(2,1)S(1)} %get-tuple-element.254), channel_id=1, source_target_pairs={{0,1},{1,0},{2,3},{3,2},{4,5},{5,4},{6,7},{7,6},{8,9},{9,8},{10,11... | collective-permute-start | bytes 884744 | tf_op jit(solution)/shard_map/ppermute | solution.py:29
  99.7 10.9 %collective-permute-start.40 = (bf16[2,192,384]{2,1,0:T(8,128)(2,1)S(1)}, bf16[2,192,384]{2,1,0:T(8,128)(2,1)S(1)}, u32[]{:S(2)}, u32[]{:S(2)}) collective-permute-start(bf16[2,192,384]{2,1,0:T(8,128)(2,1)S(1)} %get-tuple-element.256), channel_id=1, source_target_pairs={{0,2},{1,3},{2,0},{3,1},{4,6},{5,7},{6,4},{7,5},{8,10},{9,11},{10,... | collective-permute-start | bytes 884744 | tf_op jit(solution)/shard_map/ppermute | solution.py:29
  101.1 15.5 %collective-permute-start.41 = (bf16[512,256]{1,0:T(8,128)(2,1)S(1)}, bf16[512,256]{1,0:T(8,128)(2,1)S(1)}, u32[]{:S(2)}, u32[]{:S(2)}) collective-permute-start(bf16[512,256]{1,0:T(8,128)(2,1)S(1)} %get-tuple-element.240.do.refs_1_), channel_id=1, source_target_pairs={{0,1},{1,0},{2,3},{3,2},{4,5},{5,4},{6,7},{7,6},{8,9},{9,8},{10,11... | collective-permute-start | bytes 786440 | tf_op jit(solution)/shard_map/ppermute | solution.py:29
  114.1 15.3 %collective-permute-start.42 = (bf16[2,192,384]{2,1,0:T(8,128)(2,1)S(1)}, bf16[2,192,384]{2,1,0:T(8,128)(2,1)S(1)}, u32[]{:S(2)}, u32[]{:S(2)}) collective-permute-start(bf16[2,192,384]{2,1,0:T(8,128)(2,1)S(1)} %get-tuple-element.269), channel_id=1, source_target_pairs={{0,4},{1,5},{2,6},{3,7},{4,0},{5,1},{6,2},{7,3},{8,12},{9,13},{10,... | collective-permute-start | bytes 884744 | tf_op jit(solution)/shard_map/ppermute | solution.py:29
  124.0 15.6 %collective-permute-start.49 = (bf16[320,576]{1,0:T(8,128)(2,1)S(1)}, bf16[320,576]{1,0:T(8,128)(2,1)S(1)}, u32[]{:S(2)}, u32[]{:S(2)}) collective-permute-start(bf16[320,576]{1,0:T(8,128)(2,1)S(1)} %get-tuple-element.284), channel_id=1, source_target_pairs={{0,1},{1,0},{2,3},{3,2},{4,5},{5,4},{6,7},{7,6},{8,9},{9,8},{10,11... | collective-permute-start | bytes 1105928 | tf_op jit(solution)/shard_map/ppermute | solution.py:29
  124.6 15.0 %collective-permute-start.48 = (bf16[208,576]{1,0:T(8,128)(2,1)S(1)}, bf16[208,576]{1,0:T(8,128)(2,1)S(1)}, u32[]{:S(2)}, u32[]{:S(2)}) collective-permute-start(bf16[208,576]{1,0:T(8,128)(2,1)S(1)} %get-tuple-element.282), channel_id=1, source_target_pairs={{0,2},{1,3},{2,0},{3,1},{4,6},{5,7},{6,4},{7,5},{8,10},{9,11},{10,... | collective-permute-start | bytes 718856 | tf_op jit(solution)/shard_map/ppermute | solution.py:29
  130.0 9.6 %collective-permute-start.47 = (bf16[192,384]{1,0:T(8,128)(2,1)S(1)}, bf16[192,384]{1,0:T(8,128)(2,1)S(1)}, u32[]{:S(2)}, u32[]{:S(2)}) collective-permute-start(bf16[192,384]{1,0:T(8,128)(2,1)S(1)} %get-tuple-element.279.proj_own), channel_id=1, source_target_pairs={{0,4},{1,5},{2,6},{3,7},{4,0},{5,1},{6,2},{7,3},{8,12},{9,13},{10,... | collective-permute-start | bytes 442376 | tf_op jit(solution)/shard_map/ppermute | solution.py:29
  150.3 13.4 %collective-permute-start.58 = (bf16[2,192,384]{2,1,0:T(8,128)(2,1)S(1)}, bf16[2,192,384]{2,1,0:T(8,128)(2,1)S(1)}, u32[]{:S(2)}, u32[]{:S(2)}) collective-permute-start(bf16[2,192,384]{2,1,0:T(8,128)(2,1)S(1)} %get-tuple-element.301.b), channel_id=1, source_target_pairs={{0,2},{1,3},{2,0},{3,1},{4,6},{5,7},{6,4},{7,5},{8,10},{9,11},{10,... | collective-permute-start | bytes 884744 | tf_op jit(solution)/shard_map/ppermute | solution.py:29
  152.9 10.8 %collective-permute-start.57 = (bf16[2,192,384]{2,1,0:T(8,128)(2,1)S(1)}, bf16[2,192,384]{2,1,0:T(8,128)(2,1)S(1)}, u32[]{:S(2)}, u32[]{:S(2)}) collective-permute-start(bf16[2,192,384]{2,1,0:T(8,128)(2,1)S(1)} %get-tuple-element.297.a), channel_id=1, source_target_pairs={{0,1},{1,0},{2,3},{3,2},{4,5},{5,4},{6,7},{7,6},{8,9},{9,8},{10,11... | collective-permute-start | bytes 884744 | tf_op jit(solution)/shard_map/ppermute | solution.py:29
  153.7 10.0 %collective-permute-start.56 = (bf16[144,576]{1,0:T(8,128)(2,1)S(1)}, bf16[144,576]{1,0:T(8,128)(2,1)S(1)}, u32[]{:S(2)}, u32[]{:S(2)}) collective-permute-start(bf16[144,576]{1,0:T(8,128)(2,1)S(1)} %get-tuple-element.299), channel_id=1, source_target_pairs={{0,4},{1,5},{2,6},{3,7},{4,0},{5,1},{6,2},{7,3},{8,12},{9,13},{10,... | collective-permute-start | bytes 497672 | tf_op jit(solution)/shard_map/ppermute | solution.py:29
  164.4 21.5 %collective-permute-start.63 = (bf16[4,192,384]{2,1,0:T(8,128)(2,1)S(1)}, bf16[4,192,384]{2,1,0:T(8,128)(2,1)S(1)}, u32[]{:S(2)}, u32[]{:S(2)}) collective-permute-start(bf16[4,192,384]{2,1,0:T(8,128)(2,1)S(1)} %get-tuple-element.318.near), channel_id=1, source_target_pairs={{0,1},{1,0},{2,3},{3,2},{4,5},{5,4},{6,7},{7,6},{8,9},{9,8},{10,11... | collective-permute-start | bytes 1769480 | tf_op jit(solution)/shard_map/ppermute | solution.py:29
  165.9 22.1 %collective-permute-start.64 = (bf16[4,192,384]{2,1,0:T(8,128)(2,1)S(1)}, bf16[4,192,384]{2,1,0:T(8,128)(2,1)S(1)}, u32[]{:S(2)}, u32[]{:S(2)}) collective-permute-start(bf16[4,192,384]{2,1,0:T(8,128)(2,1)S(1)} %get-tuple-element.302.near), channel_id=1, source_target_pairs={{0,2},{1,3},{2,0},{3,1},{4,6},{5,7},{6,4},{7,5},{8,10},{9,11},{10,... | collective-permute-start | bytes 1769480 | tf_op jit(solution)/shard_map/ppermute | solution.py:29
  174.8 9.7 %collective-permute-start.62 = (bf16[128,576]{1,0:T(8,128)(2,1)S(1)}, bf16[128,576]{1,0:T(8,128)(2,1)S(1)}, u32[]{:S(2)}, u32[]{:S(2)}) collective-permute-start(bf16[128,576]{1,0:T(8,128)(2,1)S(1)} %get-tuple-element.315.own), channel_id=1, source_target_pairs={{0,4},{1,5},{2,6},{3,7},{4,0},{5,1},{6,2},{7,3},{8,12},{9,13},{10,... | collective-permute-start | bytes 442376 | tf_op jit(solution)/shard_map/ppermute | solution.py:29
  191.6 9.6 %collective-permute-start.68 = (bf16[4,80,576]{2,1,0:T(8,128)(2,1)S(1)}, bf16[4,80,576]{2,1,0:T(8,128)(2,1)S(1)}, u32[]{:S(2)}, u32[]{:S(2)}) collective-permute-start(bf16[4,80,576]{2,1,0:T(8,128)(2,1)S(1)} %get-tuple-element.325.wn), channel_id=1, source_target_pairs={{0,1},{1,0},{2,3},{3,2},{4,5},{5,4},{6,7},{7,6},{8,9},{9,8},{10,11... | collective-permute-start | bytes 1105928 | tf_op jit(solution)/shard_map/ppermute | solution.py:29
  (50 other events, 280.5 us)

commit v2 on v1

--- a/solution.py
+++ b/solution.py
@@ -392,12 +392,23 @@
         kv[place, :] = got[:, width:]
 
 
-def split3(value):
-    high = value.astype(BF16)
-    rest = value - high.astype(F32)
-    mid = rest.astype(BF16)
-    low = (rest - mid.astype(F32)).astype(BF16)
-    return high, mid, low
+def in_parts(columns, rows, width):
+    heads = len(columns)
+    lane = lax.broadcasted_iota(jnp.int32, (rows, width), 1)
+    value = jnp.zeros((rows, width), F32)
+    for h, column in enumerate(columns):
+        here = (lane == h) | (lane == heads + h) | (lane == 2 * heads + h)
+        value = jnp.where(here, column, value)
+    high = value.astype(BF16).astype(F32)
+    rest = value - high
+    mid = rest.astype(BF16).astype(F32)
+    parts = jnp.where(lane < heads, high, jnp.where(lane < 2 * heads, mid, rest - mid))
+    return parts.astype(BF16)
+
+
+def from_parts(tail, heads):
+    tail = tail.astype(F32)
+    return (tail[:, :heads] + tail[:, heads : 2 * heads]) + tail[:, 2 * heads : 3 * heads]
 
 
 def lanes(columns, rows, width, dtype):
@@ -406,15 +417,6 @@
     for i, column in enumerate(columns):
         out = jnp.where(lane == i, column.astype(F32), out)
     return out.astype(dtype)
-
-
-def joined(ref, base, count, h):
-    total = None
-    for part in range(3):
-        column = base + part * count + h
-        piece = ref[:, column : column + 1].astype(F32)
-        total = piece if total is None else total + piece
-    return total
 
 
 def threshold(sc, other):
@@ -483,10 +485,8 @@
             low_part = joined_parts.astype(BF16)
             low[place, :] = low_part
             scratch[place, :] = dot(low_part, out_w[...], (1, 0))
-            split = [split3(t) for t in tops]
-            columns = [split[h][part] for part in range(3) for h in range(heads)]
             q_ext[place, :width] = q[place, :]
-            q_ext[place, width:] = lanes(columns, rows, q_ext.shape[1] - width, BF16)
+            q_ext[place, width:] = in_parts(tops, rows, q_ext.shape[1] - width)
         else:
             acc_out[place, :] = joined_parts
             stat_out[place, :] = lanes(tops + sums, rows, stat_out.shape[1], F32)
@@ -598,13 +598,11 @@
         g_branch[place, :] = ref[...]
         low = dot(ref[...], out_w[...], (1, 1)).astype(BF16)
         product = low.astype(F32) * attended[place, :]
-        split = [
-            split3(jnp.sum(product[:, h * HD : (h + 1) * HD], axis=-1, keepdims=True))
-            for h in range(heads)
+        sums = [
+            jnp.sum(product[:, h * HD : (h + 1) * HD], axis=-1, keepdims=True) for h in range(heads)
         ]
-        columns = [split[h][part] for part in range(3) for h in range(heads)]
         do_ext[place, :width] = low
-        do_ext[place, width:] = lanes(columns, rows, do_ext.shape[1] - width, BF16)
+        do_ext[place, width:] = in_parts(sums, rows, do_ext.shape[1] - width)
 
 
 def pair_back(q, do, kv, allowed, g_q=None, g_kv=None, q_in=None):
@@ -614,17 +612,14 @@
     heads = width // HD
     for jq in range(WAYS):
         place = slice(jq * rows, (jq + 1) * rows)
-        tail_q = q[place, width:].astype(F32)
-        tail_do = do[place, width:].astype(F32)
+        tops = from_parts(q[place, width:], heads)
+        deltas = from_parts(do[place, width:], heads)
         for h in range(heads):
             cols = slice(h * HD, (h + 1) * HD)
             vcols = slice(width + h * HD, width + (h + 1) * HD)
             qh = q[place, cols]
             doh = do[place, cols]
-            pick = lambda t: (
-                t[:, h : h + 1] + t[:, heads + h : heads + h + 1]
-            ) + t[:, 2 * heads + h : 2 * heads + h + 1]
-            lse, delta = pick(tail_q), pick(tail_do)
+            lse, delta = tops[:, h : h + 1], deltas[:, h : h + 1]
             keys = slice(0, (jq + 1) * rows)
             weight = jnp.exp(dot(qh, kv[keys, cols], (1, 1)) - lse)
             weight = mask_last(weight, allowed, 0.0)
@@ -759,7 +754,8 @@
         out[block_rows(piece >> 1, rows), block_rows(piece & 1, cols)] = ref[at].astype(F32)
 
 
-def fc_final_kernel(bits, sc, near, far, out):
+def fc_final_kernel(bits, sc, near, far, tokens, out, tokens_out):
+    tokens_out[...] = tokens[...]
     quarter, step_cols = near.shape[1] // WAYS, near.shape[2]
     for slot, ref, at in slots_in(near, far):
         piece = piece_of(sc, bits, slot)
@@ -770,7 +766,8 @@
             ].astype(F32)
 
 
-def qkv_final_kernel(near_bits, far_bits, sc, nn, nf, wn, wf, out, out_out):
+def qkv_final_kernel(near_bits, far_bits, sc, nn, nf, wn, wf, tokens, out, out_out, tokens_out):
+    tokens_out[...] = tokens[...]
     step, width = nn.shape[1] // 2, nn.shape[2] // 3
     cols = out_out.shape[1] // 2
     rows = out_out.shape[0] // WAYS
@@ -1121,6 +1118,7 @@
         ],
         [near_keep, vec, near_got, far_keep, far_got],
         name="qkv_meet",
+        late=[fc_got],
     )
     got = c_xor(send, 1 << Z2)
     proj_own, fc_own = order.call(
@@ -1130,25 +1128,29 @@
         name="mlp_part",
     )
     proj_got, fc_got = c_xor(proj_own, 1 << OTHER[1]), c_xor(fc_own, 1 << ONE[1])
+    piece, vec = order.call(
+        qkv_last_kernel,
+        [shape((near_rows + far_rows, cols), BF16), shape((vec_rows, cols), BF16)],
+        [keep, vec, got],
+        flops=4 * 10**9,
+        name="qkv_last",
+    )
+    piece, vec = others(piece), others(vec)
+    s1, s2, s3 = order.call(
+        exchange_kernel,
+        [shape((step + vec_rows, cols), BF16)] * 3,
+        [piece, vec],
+        flops=4 * 10**9,
+        name="exchange",
+    )
+    r2, r3, r1 = f_xor(s2, 2), f_xor(s3, 3), f_xor(s1, 1)
     proj_own, fc_own = order.call(
         grow_kernel,
         [shape((half, *tile), BF16)] * 2,
         [proj_own, proj_got, fc_own, fc_got],
         name="mlp_grow",
-        late=[got],
     )
     proj_got, fc_got = c_xor(proj_own, 1 << OTHER[0]), c_xor(fc_own, 1 << ONE[0])
-    piece, vec = order.call(
-        qkv_last_kernel,
-        [shape((near_rows + far_rows, cols), BF16), shape((vec_rows, cols), BF16)],
-        [keep, vec, got],
-        name="qkv_last",
-    )
-    piece, vec = others(piece), others(vec)
-    s1, s2, s3 = order.call(
-        exchange_kernel, [shape((step + vec_rows, cols), BF16)] * 3, [piece, vec], name="exchange"
-    )
-    r2, r3, r1 = f_xor(s2, 2), f_xor(s3, 3), f_xor(s1, 1)
     joined, *mine, grad_qv, grad_fc_bias = order.call(
         join_kernel,
         [
@@ -1169,17 +1171,19 @@
         name="qkv_part",
     )
     near_got, far_got = c_xor(near_own, 1 << OTHER[1]), c_xor(far_own, 1 << ONE[1])
-    def finish(kernel, dims, arrays, name):
-        late = [input_grad] if name == "qkv_final" else []
-        return order.call(
-            kernel, [shape(d, F32) for d in dims], arrays, name=name, direct=True, late=late
-        )
-
-    (grad_fc,) = finish(
+    def finish(kernel, dims, arrays, name, tokens=None):
+        outs = [shape(d, F32) for d in dims]
+        if tokens is not None:
+            outs.append(shape(tokens.shape, BF16))
+            arrays = [*arrays, tokens]
+        return order.call(kernel, outs, arrays, name=name, direct=True)
+
+    grad_fc, outputs = finish(
         functools.partial(fc_final_kernel, ONE),
         [(head_width, WAYS * hidden_width)],
         [fc_own, fc_got],
         "fc_final",
+        outputs,
     )
     (grad_proj,) = finish(
         functools.partial(proj_final_kernel, OTHER),
@@ -1195,11 +1199,12 @@
     )
     near_got, far_got = c_xor(near_own, 1 << OTHER[0]), c_xor(far_own, 1 << ONE[0])
 
-    grad_qkv, grad_out = finish(
+    grad_qkv, grad_out, input_grad = finish(
         functools.partial(qkv_final_kernel, OTHER, ONE),
         [(head_width, 3 * width), (head_width, width)],
         [near_own, near_got, far_own, far_got],
         "qkv_final",
+        input_grad,
     )
     return (
         outputs,

time: 209 us -> 206 us (0.986)
  waiting for transfers between devices: 67.8 us -> 61.8 us
  starting transfers between devices: 62.7 us -> 67.4 us
    ppermute x26, waiting for transfers between devices: 42.7 us -> 36.9 us  [c_xor(): return lax.ppermute(x, 'ctx', [(i, i ^ k) for i in range(n)])]
    ppermute x26, starting transfers between devices: 31.6 us -> 35.4 us  [c_xor(): return lax.ppermute(x, 'ctx', [(i, i ^ k) for i in range(n)])]
  transfers between devices with their start and end apart: 69 -> 69, of which waited for: 26 -> 25; matrix products, arithmetic and copies ran while one was open for 3% -> 3% of each run, Pallas kernels for 26% -> 27%
where the time goes in v2:
time: 206 us; the launch traced here: 202 us
  starting transfers between devices  67.4 us (33%)
  Pallas kernels  64 us (31%)
  waiting for transfers between devices  61.8 us (30%)
  local copies, waits for them, and re-layouts  6.73 us (3%)
    pallas_call x43, Pallas kernels, call(): pl.pallas_call(kernel, out_shape=tuple(outs), in_specs=[pl.BlockSpec(memo...  64 us
    ppermute x26, waiting for transfers between devices, c_xor(): return lax.ppermute(x, 'ctx', [(i, i ^ k) for i in range(n)])  36.9 us
    ppermute x26, starting transfers between devices, c_xor(): return lax.ppermute(x, 'ctx', [(i, i ^ k) for i in range(n)])  35.4 us
    ppermute x39, starting transfers between devices, f_xor(): return lax.ppermute(x, 'fsdp', [(i, i ^ k) for i in range(n)])  28.3 us
    ppermute x39, waiting for transfers between devices, f_xor(): return lax.ppermute(x, 'fsdp', [(i, i ^ k) for i in range(n)])  24.9 us
    concatenate x1, local copies, waits for them, and re-layouts, body(): jnp.concatenate(vectors)  5.46 us
  transfers between devices with their start and end apart: 69, of which 25 were waited for; matrix products, arithmetic and copies ran while one was open for 3% of the time, Pallas kernels for 27%

profile of v2, /device:TPU:0, one launch (start us, length us, event | category | flops | bytes accessed | tf_op | source)
XLA Modules:
  0.0 201.8 jit_solution(3329555044263050359)
XLA Ops:
  5.2 6.7 %collective-permute-start.3 = (bf16[96,576]{1,0:T(8,128)(2,1)S(1)}, bf16[96,576]{1,0:T(8,128)(2,1)S(1)}, u32[]{:S(2)}, u32[]{:S(2)}) collective-permute-start(bf16[96,576]{1,0:T(8,128)(2,1)S(1)} %get-tuple-element.180), channel_id=1, source_target_pairs={{0,24},{8,16},{16,8},{24,0},{1,25},{9,17},{17,9},{25,1},{2,26},{10... | collective-permute-start | bytes 331784 | tf_op jit(solution)/shard_map/ppermute | solution.py:24
  11.8 5.5 %concatenate.3.vectors = bf16[2304]{0:T(1024)(128)(2,1)S(1)} concatenate(bf16[192]{0:T(256)(128)(2,1)} %param.17, bf16[192]{0:T(256)(128)(2,1)} %param.18, bf16[192]{0:T(256)(128)(2,1)} %param.22, bf16[192]{0:T(256)(128)(2,1)} %param.23, bf16[192]{0:T(256)(128)(2,1)} %param.24, bf16[192]{0:T(256)(128)(2,1)} %param.28, bf16[384]{0:T(512)(128)(2,1)} %param.20, bf16[768]{0:T(1024)(128)(2,1)} %param.26), dimensions={0} | concatenate | bytes 9216 | tf_op jit(solution)/shard_map/concatenate | solution.py:829
  18.9 2.5 %collective-permute-start.9 = (bf16[128,768]{1,0:T(8,128)(2,1)S(1)}, bf16[128,768]{1,0:T(8,128)(2,1)S(1)}, u32[]{:S(2)}, u32[]{:S(2)}) collective-permute-start(bf16[128,768]{1,0:T(8,128)(2,1)S(1)} %collective-permute-done.x0.x), channel_id=1, source_target_pairs={{0,16},{8,24},{16,0},{24,8},{1,17},{9,25},{17,1},{25,9},{2,18},{10... | collective-permute-start | bytes 589832 | tf_op jit(solution)/shard_map/ppermute | solution.py:24
  24.3 3.4 %collective-permute-done.4.w3_x = bf16[96,576]{1,0:T(8,128)(2,1)S(1)} collective-permute-done((bf16[96,576]{1,0:T(8,128)(2,1)S(1)}, bf16[96,576]{1,0:T(8,128)(2,1)S(1)}, u32[]{:S(2)}, u32[]{:S(2)}) %collective-permute-start.4) | collective-permute-done | bytes 110624 | tf_op jit(solution)/shard_map/ppermute | solution.py:29
  37.3 3.6 %attend0.1 = (f32[512,192]{1,0:T(8,128)S(1)}, f32[512,128]{1,0:T(8,128)S(1)}) custom-call(s32[6]{0:T(128)S(1)} %stack.19.sc.sc_ref, bf16[512,192]{1,0:T(8,128)(2,1)S(1)} %get-tuple-element.191.refs_0_, bf16[512,384]{1,0:T(8,128)(2,1)S(1)} %get-tuple-element.193.refs_1_.kv.refs_2_), custom_call_target="tpu_custom_call" | custom-call | flops 201326592 | bytes 1245208 | tf_op jit(solution)/shard_map/attend0/pallas_call | solution.py:105
  41.0 3.6 %collective-permute-done.12.refs_1_.refs_2_ = bf16[512,384]{1,0:T(8,128)(2,1)S(1)} collective-permute-done((bf16[512,384]{1,0:T(8,128)(2,1)S(1)}, bf16[512,384]{1,0:T(8,128)(2,1)S(1)}, u32[]{:S(2)}, u32[]{:S(2)}) %collective-permute-start.12) | collective-permute-done | bytes 393248 | tf_op jit(solution)/shard_map/ppermute | solution.py:29
  44.6 6.2 %attend1.1 = (f32[512,192]{1,0:T(8,128)S(1)}, bf16[512,192]{1,0:T(8,128)(2,1)S(1)}, bf16[512,256]{1,0:T(8,128)(2,1)S(1)}, f32[128,768]{1,0:T(8,128)S(1)}, f32[12...) custom-call(s32[6]{0:T(128)S(1)} %stack.19.sc.sc_ref, ...), custom_call_target="tpu_custom_call" | custom-call | flops 201326592 | bytes 3571736 | tf_op jit(solution)/shard_map/attend1/pallas_call | solution.py:105
  58.7 3.7 %collective-permute-done.20.far = bf16[128,768]{1,0:T(8,128)(2,1)S(1)} collective-permute-done((bf16[128,768]{1,0:T(8,128)(2,1)S(1)}, bf16[128,768]{1,0:T(8,128)(2,1)S(1)}, u32[]{:S(2)}, u32[]{:S(2)}) %collective-permute-start.20) | collective-permute-done | bytes 196640 | tf_op jit(solution)/shard_map/ppermute | solution.py:24
  65.6 4.0 %collective-permute-done.25.n2 = bf16[128,768]{1,0:T(8,128)(2,1)S(1)} collective-permute-done((bf16[128,768]{1,0:T(8,128)(2,1)S(1)}, bf16[128,768]{1,0:T(8,128)(2,1)S(1)}, u32[]{:S(2)}, u32[]{:S(2)}) %collective-permute-start.25) | collective-permute-done | bytes 196640 | tf_op jit(solution)/shard_map/ppermute | solution.py:24
  72.0 3.2 %feed.1 = (bf16[512,768]{1,0:T(8,128)(2,1)S(1)}, bf16[512,768]{1,0:T(8,128)(2,1)S(1)}, bf16[512,768]{1,0:T(8,128)(2,1)S(1)}, f32[1,768]{1,0:T(1,128)S(1)}, f32[1...) custom-call(s32[6]{0:T(128)S(1)} %stack.19.sc.sc_ref, ...), custom_call_target="tpu_custom_call" | custom-call | flops 1207959552 | bytes 7084056 | tf_op jit(solution)/shard_map/feed/pallas_call | solution.py:105
  87.6 5.2 %collective-permute-done.32.b2 = bf16[128,768]{1,0:T(8,128)(2,1)S(1)} collective-permute-done((bf16[128,768]{1,0:T(8,128)(2,1)S(1)}, bf16[128,768]{1,0:T(8,128)(2,1)S(1)}, u32[]{:S(2)}, u32[]{:S(2)}) %collective-permute-start.32) | collective-permute-done | bytes 196640 | tf_op jit(solution)/shard_map/ppermute | solution.py:24
  103.1 4.4 %back0.1 = (f32[512,192]{1,0:T(8,128)S(1)}, f32[512,384]{1,0:T(8,128)S(1)}) custom-call(s32[6]{0:T(128)S(1)} %stack.19.sc.sc_ref, bf16[512,256]{1,0:T(8,128)(2,1)S(1)} %get-tuple-element.215.q.refs_0_, bf16[512,256]{1,0:T(8,128)(2,1)S(1)} %get-tuple-element.242.do.refs_1_, bf16[512,384]{1,0:T(8,128)(2,1)S(1)} %get-tuple-element.193.refs_1_.kv.refs_2_), custom_call_target="tpu_custom_call" | custom-call | flops 503316480 | bytes 2097176 | tf_op jit(solution)/shard_map/back0/pallas_call | solution.py:105
  111.0 2.9 %back_q.1.refs_4_ = f32[512,192]{1,0:T(8,128)S(1)} custom-call(s32[6]{0:T(128)S(1)} %stack.19.sc.sc_ref, bf16[512,256]{1,0:T(8,128)(2,1)S(1)} %get-tuple-element.215.q.refs_0_, bf16[512,256]{1,0:T(8,128)(2,1)S(1)} %get-tuple-element.242.do.refs_1_, bf16[512,384]{1,0:T(8,128)(2,1)S(1)} %collective-permute-done.12.refs_1_.refs_2_, ...), custom_call_target="tpu_custom_call" | custom-call | flops 301989888 | bytes 1703960 | tf_op jit(solution)/shard_map/back_q/pallas_call | solution.py:105
  113.9 2.5 %collective-permute-start.42 = (bf16[2,192,384]{2,1,0:T(8,128)(2,1)S(1)}, bf16[2,192,384]{2,1,0:T(8,128)(2,1)S(1)}, u32[]{:S(2)}, u32[]{:S(2)}) collective-permute-start(bf16[2,192,384]{2,1,0:T(8,128)(2,1)S(1)} %get-tuple-element.271), channel_id=1, source_target_pairs={{0,4},{1,5},{2,6},{3,7},{4,0},{5,1},{6,2},{7,3},{8,12},{9,13},{10,... | collective-permute-start | bytes 884744 | tf_op jit(solution)/shard_map/ppermute | solution.py:29
  116.4 5.4 %back_kv.1 = (bf16[512,576]{1,0:T(8,128)(2,1)S(1)}, f32[128,768]{1,0:T(8,128)S(1)}, f32[128,768]{1,0:T(8,128)S(1)}, bf16[128,768]{1,0:T(8,128)(2,1)S(1)}, bf16[1...) custom-call(s32[6]{0:T(128)S(1)} %stack.19.sc.sc_ref, bf16[512,256]{1,0:T(8,128)(2,1)S(1)} %collective-permute-done.23.refs_0_, ...), custom_call_target="tpu_custom_call" | custom-call | flops 402653184 | bytes 5543960 | tf_op jit(solution)/shard_map/back_kv/pallas_call | solution.py:105
  124.4 4.3 %collective-permute-start.48 = (bf16[208,576]{1,0:T(8,128)(2,1)S(1)}, bf16[208,576]{1,0:T(8,128)(2,1)S(1)}, u32[]{:S(2)}, u32[]{:S(2)}) collective-permute-start(bf16[208,576]{1,0:T(8,128)(2,1)S(1)} %get-tuple-element.284), channel_id=1, source_target_pairs={{0,2},{1,3},{2,0},{3,1},{4,6},{5,7},{6,4},{7,5},{8,10},{9,11},{10,... | collective-permute-start | bytes 718856 | tf_op jit(solution)/shard_map/ppermute | solution.py:29
  130.1 2.6 %collective-permute-start.45 = (bf16[48,384]{1,0:T(8,128)(2,1)S(1)}, bf16[48,384]{1,0:T(8,128)(2,1)S(1)}, u32[]{:S(2)}, u32[]{:S(2)}) collective-permute-start(bf16[48,384]{1,0:T(8,128)(2,1)S(1)} %get-tuple-element.278), channel_id=1, source_target_pairs={{0,16},{8,24},{16,0},{24,8},{1,17},{9,25},{17,1},{25,9},{2,18},{10... | collective-permute-start | bytes 110600 | tf_op jit(solution)/shard_map/ppermute | solution.py:24
  144.4 3.6 %collective-permute-done.52.fc_got = bf16[192,384]{1,0:T(8,128)(2,1)S(1)} collective-permute-done((bf16[192,384]{1,0:T(8,128)(2,1)S(1)}, bf16[192,384]{1,0:T(8,128)(2,1)S(1)}, u32[]{:S(2)}, u32[]{:S(2)}) %collective-permute-start.52) | collective-permute-done | bytes 147488 | tf_op jit(solution)/shard_map/ppermute | solution.py:29
  149.6 2.5 %collective-permute-start.55 = (bf16[144,576]{1,0:T(8,128)(2,1)S(1)}, bf16[144,576]{1,0:T(8,128)(2,1)S(1)}, u32[]{:S(2)}, u32[]{:S(2)}) collective-permute-start(bf16[144,576]{1,0:T(8,128)(2,1)S(1)} %get-tuple-element.303), channel_id=1, source_target_pairs={{0,4},{1,5},{2,6},{3,7},{4,0},{5,1},{6,2},{7,3},{8,12},{9,13},{10,... | collective-permute-start | bytes 497672 | tf_op jit(solution)/shard_map/ppermute | solution.py:29
  155.8 3.5 %collective-permute-done.55.got = bf16[144,576]{1,0:T(8,128)(2,1)S(1)} collective-permute-done((bf16[144,576]{1,0:T(8,128)(2,1)S(1)}, bf16[144,576]{1,0:T(8,128)(2,1)S(1)}, u32[]{:S(2)}, u32[]{:S(2)}) %collective-permute-start.55) | collective-permute-done | bytes 165920 | tf_op jit(solution)/shard_map/ppermute | solution.py:29
  160.5 2.4 %collective-permute-done.57.b_got = bf16[2,192,384]{2,1,0:T(8,128)(2,1)S(1)} collective-permute-done((bf16[2,192,384]{2,1,0:T(8,128)(2,1)S(1)}, bf16[2,192,384]{2,1,0:T(8,128)(2,1)S(1)}, u32[]{:S(2)}, u32[]{:S(2)}) %collective-permute-start.57) | collective-permute-done | bytes 294944 | tf_op jit(solution)/shard_map/ppermute | solution.py:29
  166.1 2.6 %collective-permute-start.59 = (bf16[40,576]{1,0:T(8,128)(2,1)S(1)}, bf16[40,576]{1,0:T(8,128)(2,1)S(1)}, u32[]{:S(2)}, u32[]{:S(2)}) collective-permute-start(bf16[40,576]{1,0:T(8,128)(2,1)S(1)} %get-tuple-element.312), channel_id=1, source_target_pairs={{0,16},{8,24},{16,0},{24,8},{1,17},{9,25},{17,1},{25,9},{2,18},{10... | collective-permute-start | bytes 138248 | tf_op jit(solution)/shard_map/ppermute | solution.py:24
  175.0 6.6 %collective-permute-done.61.got = bf16[128,576]{1,0:T(8,128)(2,1)S(1)} collective-permute-done((bf16[128,576]{1,0:T(8,128)(2,1)S(1)}, bf16[128,576]{1,0:T(8,128)(2,1)S(1)}, u32[]{:S(2)}, u32[]{:S(2)}) %collective-permute-start.61) | collective-permute-done | bytes 147488 | tf_op jit(solution)/shard_map/ppermute | solution.py:29
  193.0 4.7 %collective-permute-done.66.nf = bf16[4,48,576]{2,1,0:T(8,128)(2,1)S(1)} collective-permute-done((bf16[4,48,576]{2,1,0:T(8,128)(2,1)S(1)}, bf16[4,48,576]{2,1,0:T(8,128)(2,1)S(1)}, u32[]{:S(2)}, u32[]{:S(2)}) %collective-permute-start.66) | collective-permute-done | bytes 221216 | tf_op jit(solution)/shard_map/ppermute | solution.py:29
  (169 shorter events, 104.4 us)
Async XLA Ops:
  0.6 18.3 %collective-permute-start = (bf16[128,768]{1,0:T(8,128)(2,1)}, bf16[128,768]{1,0:T(8,128)(2,1)S(1)}, u32[]{:S(2)}, u32[]{:S(2)}) collective-permute-start(bf16[128,768]{1,0:T(8,128)(2,1)} %bitcast.6), channel_id=1, source_target_pairs={{0,0},{1,1},{2,16},{3,17},{4,8},{5,9},{6,24},{7,25},{8,4},{9,5},{1... | collective-permute-start | bytes 589832 | tf_op jit(solution)/shard_map/ppermute | solution.py:44
  5.2 12.7 %collective-permute-start.3 = (bf16[96,576]{1,0:T(8,128)(2,1)S(1)}, bf16[96,576]{1,0:T(8,128)(2,1)S(1)}, u32[]{:S(2)}, u32[]{:S(2)}) collective-permute-start(bf16[96,576]{1,0:T(8,128)(2,1)S(1)} %get-tuple-element.180), channel_id=1, source_target_pairs={{0,24},{8,16},{16,8},{24,0},{1,25},{9,17},{17,9},{25,1},{2,26},{10... | collective-permute-start | bytes 331784 | tf_op jit(solution)/shard_map/ppermute | solution.py:24
  18.9 10.6 %collective-permute-start.9 = (bf16[128,768]{1,0:T(8,128)(2,1)S(1)}, bf16[128,768]{1,0:T(8,128)(2,1)S(1)}, u32[]{:S(2)}, u32[]{:S(2)}) collective-permute-start(bf16[128,768]{1,0:T(8,128)(2,1)S(1)} %collective-permute-done.x0.x), channel_id=1, source_target_pairs={{0,16},{8,24},{16,0},{24,8},{1,17},{9,25},{17,1},{25,9},{2,18},{10... | collective-permute-start | bytes 589832 | tf_op jit(solution)/shard_map/ppermute | solution.py:24
  33.1 11.5 %collective-permute-start.12 = (bf16[512,384]{1,0:T(8,128)(2,1)S(1)}, bf16[512,384]{1,0:T(8,128)(2,1)S(1)}, u32[]{:S(2)}, u32[]{:S(2)}) collective-permute-start(bf16[512,384]{1,0:T(8,128)(2,1)S(1)} %get-tuple-element.193.refs_1_.kv.refs_2_), channel_id=1, source_target_pairs={{0,1},{1,0},{2,3},{3,2},{4,5},{5,4},{6,7},{7,6},{8,9},{9,8},{10,11... | collective-permute-start | bytes 1179656 | tf_op jit(solution)/shard_map/ppermute | solution.py:29
  34.6 16.7 %collective-permute-start.13 = (bf16[192,768]{1,0:T(8,128)(2,1)S(1)}, bf16[192,768]{1,0:T(8,128)(2,1)S(1)}, u32[]{:S(2)}, u32[]{:S(2)}) collective-permute-start(bf16[192,768]{1,0:T(8,128)(2,1)S(1)} %get-tuple-element.199), channel_id=1, source_target_pairs={{0,8},{8,0},{16,24},{24,16},{1,9},{9,1},{17,25},{25,17},{2,10},{10... | collective-permute-start | bytes 884744 | tf_op jit(solution)/shard_map/ppermute | solution.py:24
  34.8 16.5 %collective-permute-start.14 = (bf16[192,768]{1,0:T(8,128)(2,1)S(1)}, bf16[192,768]{1,0:T(8,128)(2,1)S(1)}, u32[]{:S(2)}, u32[]{:S(2)}) collective-permute-start(bf16[192,768]{1,0:T(8,128)(2,1)S(1)} %get-tuple-element.200), channel_id=1, source_target_pairs={{0,16},{8,24},{16,0},{24,8},{1,17},{9,25},{17,1},{25,9},{2,18},{10... | collective-permute-start | bytes 884744 | tf_op jit(solution)/shard_map/ppermute | solution.py:24
  35.1 17.9 %collective-permute-start.15 = (bf16[192,768]{1,0:T(8,128)(2,1)S(1)}, bf16[192,768]{1,0:T(8,128)(2,1)S(1)}, u32[]{:S(2)}, u32[]{:S(2)}) collective-permute-start(bf16[192,768]{1,0:T(8,128)(2,1)S(1)} %get-tuple-element.201), channel_id=1, source_target_pairs={{0,24},{8,16},{16,8},{24,0},{1,25},{9,17},{17,9},{25,1},{2,26},{10... | collective-permute-start | bytes 884744 | tf_op jit(solution)/shard_map/ppermute | solution.py:24
  36.5 14.4 %collective-permute-start.17 = (bf16[128,768]{1,0:T(8,128)(2,1)S(1)}, bf16[128,768]{1,0:T(8,128)(2,1)S(1)}, u32[]{:S(2)}, u32[]{:S(2)}) collective-permute-start(bf16[128,768]{1,0:T(8,128)(2,1)S(1)} %bitcast.7), channel_id=1, source_target_pairs={{0,0},{1,1},{2,16},{3,17},{4,8},{5,9},{6,24},{7,25},{8,4},{9,5},{1... | collective-permute-start | bytes 589832 | tf_op jit(solution)/shard_map/ppermute | solution.py:44
  77.3 20.1 %collective-permute-start.34 = (bf16[4,192,384]{2,1,0:T(8,128)(2,1)S(1)}, bf16[4,192,384]{2,1,0:T(8,128)(2,1)S(1)}, u32[]{:S(2)}, u32[]{:S(2)}) collective-permute-start(bf16[4,192,384]{2,1,0:T(8,128)(2,1)S(1)} %get-tuple-element.247), channel_id=1, source_target_pairs={{0,2},{1,3},{2,0},{3,1},{4,6},{5,7},{6,4},{7,5},{8,10},{9,11},{10,... | collective-permute-start | bytes 1769480 | tf_op jit(solution)/shard_map/ppermute | solution.py:29
  80.3 17.1 %collective-permute-start.35 = (bf16[4,192,384]{2,1,0:T(8,128)(2,1)S(1)}, bf16[4,192,384]{2,1,0:T(8,128)(2,1)S(1)}, u32[]{:S(2)}, u32[]{:S(2)}) collective-permute-start(bf16[4,192,384]{2,1,0:T(8,128)(2,1)S(1)} %get-tuple-element.248), channel_id=1, source_target_pairs={{0,1},{1,0},{2,3},{3,2},{4,5},{5,4},{6,7},{7,6},{8,9},{9,8},{10,11... | collective-permute-start | bytes 1769480 | tf_op jit(solution)/shard_map/ppermute | solution.py:29
  92.7 9.0 %collective-permute-start.36 = (bf16[128,768]{1,0:T(8,128)(2,1)S(1)}, bf16[128,768]{1,0:T(8,128)(2,1)S(1)}, u32[]{:S(2)}, u32[]{:S(2)}) collective-permute-start(bf16[128,768]{1,0:T(8,128)(2,1)S(1)} %get-tuple-element.251), channel_id=1, source_target_pairs={{0,8},{8,0},{16,24},{24,16},{1,9},{9,1},{17,25},{25,17},{2,10},{10... | collective-permute-start | bytes 589832 | tf_op jit(solution)/shard_map/ppermute | solution.py:24
  98.2 9.9 %collective-permute-start.39 = (bf16[2,192,384]{2,1,0:T(8,128)(2,1)S(1)}, bf16[2,192,384]{2,1,0:T(8,128)(2,1)S(1)}, u32[]{:S(2)}, u32[]{:S(2)}) collective-permute-start(bf16[2,192,384]{2,1,0:T(8,128)(2,1)S(1)} %get-tuple-element.256), channel_id=1, source_target_pairs={{0,1},{1,0},{2,3},{3,2},{4,5},{5,4},{6,7},{7,6},{8,9},{9,8},{10,11... | collective-permute-start | bytes 884744 | tf_op jit(solution)/shard_map/ppermute | solution.py:29
  99.5 10.8 %collective-permute-start.40 = (bf16[2,192,384]{2,1,0:T(8,128)(2,1)S(1)}, bf16[2,192,384]{2,1,0:T(8,128)(2,1)S(1)}, u32[]{:S(2)}, u32[]{:S(2)}) collective-permute-start(bf16[2,192,384]{2,1,0:T(8,128)(2,1)S(1)} %get-tuple-element.258), channel_id=1, source_target_pairs={{0,2},{1,3},{2,0},{3,1},{4,6},{5,7},{6,4},{7,5},{8,10},{9,11},{10,... | collective-permute-start | bytes 884744 | tf_op jit(solution)/shard_map/ppermute | solution.py:29
  100.9 15.5 %collective-permute-start.41 = (bf16[512,256]{1,0:T(8,128)(2,1)S(1)}, bf16[512,256]{1,0:T(8,128)(2,1)S(1)}, u32[]{:S(2)}, u32[]{:S(2)}) collective-permute-start(bf16[512,256]{1,0:T(8,128)(2,1)S(1)} %get-tuple-element.242.do.refs_1_), channel_id=1, source_target_pairs={{0,1},{1,0},{2,3},{3,2},{4,5},{5,4},{6,7},{7,6},{8,9},{9,8},{10,11... | collective-permute-start | bytes 786440 | tf_op jit(solution)/shard_map/ppermute | solution.py:29
  113.9 15.4 %collective-permute-start.42 = (bf16[2,192,384]{2,1,0:T(8,128)(2,1)S(1)}, bf16[2,192,384]{2,1,0:T(8,128)(2,1)S(1)}, u32[]{:S(2)}, u32[]{:S(2)}) collective-permute-start(bf16[2,192,384]{2,1,0:T(8,128)(2,1)S(1)} %get-tuple-element.271), channel_id=1, source_target_pairs={{0,4},{1,5},{2,6},{3,7},{4,0},{5,1},{6,2},{7,3},{8,12},{9,13},{10,... | collective-permute-start | bytes 884744 | tf_op jit(solution)/shard_map/ppermute | solution.py:29
  123.8 15.6 %collective-permute-start.49 = (bf16[320,576]{1,0:T(8,128)(2,1)S(1)}, bf16[320,576]{1,0:T(8,128)(2,1)S(1)}, u32[]{:S(2)}, u32[]{:S(2)}) collective-permute-start(bf16[320,576]{1,0:T(8,128)(2,1)S(1)} %get-tuple-element.286), channel_id=1, source_target_pairs={{0,1},{1,0},{2,3},{3,2},{4,5},{5,4},{6,7},{7,6},{8,9},{9,8},{10,11... | collective-permute-start | bytes 1105928 | tf_op jit(solution)/shard_map/ppermute | solution.py:29
  124.4 15.0 %collective-permute-start.48 = (bf16[208,576]{1,0:T(8,128)(2,1)S(1)}, bf16[208,576]{1,0:T(8,128)(2,1)S(1)}, u32[]{:S(2)}, u32[]{:S(2)}) collective-permute-start(bf16[208,576]{1,0:T(8,128)(2,1)S(1)} %get-tuple-element.284), channel_id=1, source_target_pairs={{0,2},{1,3},{2,0},{3,1},{4,6},{5,7},{6,4},{7,5},{8,10},{9,11},{10,... | collective-permute-start | bytes 718856 | tf_op jit(solution)/shard_map/ppermute | solution.py:29
  129.9 9.5 %collective-permute-start.47 = (bf16[192,384]{1,0:T(8,128)(2,1)S(1)}, bf16[192,384]{1,0:T(8,128)(2,1)S(1)}, u32[]{:S(2)}, u32[]{:S(2)}) collective-permute-start(bf16[192,384]{1,0:T(8,128)(2,1)S(1)} %get-tuple-element.281.proj_own), channel_id=1, source_target_pairs={{0,4},{1,5},{2,6},{3,7},{4,0},{5,1},{6,2},{7,3},{8,12},{9,13},{10,... | collective-permute-start | bytes 442376 | tf_op jit(solution)/shard_map/ppermute | solution.py:29
  140.1 8.8 %collective-permute-start.54 = (bf16[160,576]{1,0:T(8,128)(2,1)S(1)}, bf16[160,576]{1,0:T(8,128)(2,1)S(1)}, u32[]{:S(2)}, u32[]{:S(2)}) collective-permute-start(bf16[160,576]{1,0:T(8,128)(2,1)S(1)} %get-tuple-element.297), channel_id=1, source_target_pairs={{0,2},{1,3},{2,0},{3,1},{4,6},{5,7},{6,4},{7,5},{8,10},{9,11},{10,... | collective-permute-start | bytes 552968 | tf_op jit(solution)/shard_map/ppermute | solution.py:29
  149.6 9.8 %collective-permute-start.55 = (bf16[144,576]{1,0:T(8,128)(2,1)S(1)}, bf16[144,576]{1,0:T(8,128)(2,1)S(1)}, u32[]{:S(2)}, u32[]{:S(2)}) collective-permute-start(bf16[144,576]{1,0:T(8,128)(2,1)S(1)} %get-tuple-element.303), channel_id=1, source_target_pairs={{0,4},{1,5},{2,6},{3,7},{4,0},{5,1},{6,2},{7,3},{8,12},{9,13},{10,... | collective-permute-start | bytes 497672 | tf_op jit(solution)/shard_map/ppermute | solution.py:29
  152.7 10.3 %collective-permute-start.56 = (bf16[2,192,384]{2,1,0:T(8,128)(2,1)S(1)}, bf16[2,192,384]{2,1,0:T(8,128)(2,1)S(1)}, u32[]{:S(2)}, u32[]{:S(2)}) collective-permute-start(bf16[2,192,384]{2,1,0:T(8,128)(2,1)S(1)} %get-tuple-element.300.a), channel_id=1, source_target_pairs={{0,1},{1,0},{2,3},{3,2},{4,5},{5,4},{6,7},{7,6},{8,9},{9,8},{10,11... | collective-permute-start | bytes 884744 | tf_op jit(solution)/shard_map/ppermute | solution.py:29
  154.2 8.8 %collective-permute-start.57 = (bf16[2,192,384]{2,1,0:T(8,128)(2,1)S(1)}, bf16[2,192,384]{2,1,0:T(8,128)(2,1)S(1)}, u32[]{:S(2)}, u32[]{:S(2)}) collective-permute-start(bf16[2,192,384]{2,1,0:T(8,128)(2,1)S(1)} %get-tuple-element.309.b), channel_id=1, source_target_pairs={{0,2},{1,3},{2,0},{3,1},{4,6},{5,7},{6,4},{7,5},{8,10},{9,11},{10,... | collective-permute-start | bytes 884744 | tf_op jit(solution)/shard_map/ppermute | solution.py:29
  163.6 22.3 %collective-permute-start.62 = (bf16[4,192,384]{2,1,0:T(8,128)(2,1)S(1)}, bf16[4,192,384]{2,1,0:T(8,128)(2,1)S(1)}, u32[]{:S(2)}, u32[]{:S(2)}) collective-permute-start(bf16[4,192,384]{2,1,0:T(8,128)(2,1)S(1)} %get-tuple-element.319.near), channel_id=1, source_target_pairs={{0,1},{1,0},{2,3},{3,2},{4,5},{5,4},{6,7},{7,6},{8,9},{9,8},{10,11... | collective-permute-start | bytes 1769480 | tf_op jit(solution)/shard_map/ppermute | solution.py:29
  164.9 23.2 %collective-permute-start.63 = (bf16[4,192,384]{2,1,0:T(8,128)(2,1)S(1)}, bf16[4,192,384]{2,1,0:T(8,128)(2,1)S(1)}, u32[]{:S(2)}, u32[]{:S(2)}) collective-permute-start(bf16[4,192,384]{2,1,0:T(8,128)(2,1)S(1)} %get-tuple-element.310.near), channel_id=1, source_target_pairs={{0,2},{1,3},{2,0},{3,1},{4,6},{5,7},{6,4},{7,5},{8,10},{9,11},{10,... | collective-permute-start | bytes 1769480 | tf_op jit(solution)/shard_map/ppermute | solution.py:29
  (50 other events, 280.9 us)

commit v3 on v2

--- a/solution.py
+++ b/solution.py
@@ -1185,20 +1185,20 @@
         "fc_final",
         outputs,
     )
+    near_own, far_own = order.call(
+        grow_kernel,
+        [shape((half, near_rows, cols), BF16), shape((half, far_rows, cols), BF16)],
+        [near_own, near_got, far_own, far_got],
+        name="qkv_grow",
+    )
+    near_got, far_got = c_xor(near_own, 1 << OTHER[0]), c_xor(far_own, 1 << ONE[0])
+
     (grad_proj,) = finish(
         functools.partial(proj_final_kernel, OTHER),
         [(hidden_width, width)],
         [proj_own, proj_got],
         "proj_final",
     )
-    near_own, far_own = order.call(
-        grow_kernel,
-        [shape((half, near_rows, cols), BF16), shape((half, far_rows, cols), BF16)],
-        [near_own, near_got, far_own, far_got],
-        name="qkv_grow",
-    )
-    near_got, far_got = c_xor(near_own, 1 << OTHER[0]), c_xor(far_own, 1 << ONE[0])
-
     grad_qkv, grad_out, input_grad = finish(
         functools.partial(qkv_final_kernel, OTHER, ONE),
         [(head_width, 3 * width), (head_width, width)],

time: 206 us -> 212 us (1.029); the launches traced: 202 us -> 211 us
  waiting for transfers between devices: 61.8 us -> 74.2 us
  starting transfers between devices: 67.4 us -> 64.7 us
    ppermute x26, waiting for transfers between devices: 36.9 us -> 49.3 us  [c_xor(): return lax.ppermute(x, 'ctx', [(i, i ^ k) for i in range(n)])]
    ppermute x26, starting transfers between devices: 35.4 us -> 31.4 us  [c_xor(): return lax.ppermute(x, 'ctx', [(i, i ^ k) for i in range(n)])]
  transfers between devices with their start and end apart: 69 -> 69, of which waited for: 25 -> 26; matrix products, arithmetic and copies ran while one was open for 3% -> 3% of each run, Pallas kernels for 27% -> 26%
where the time goes in v3:
time: 212 us; the launch traced here: 211 us
  waiting for transfers between devices  74.2 us (35%)
  starting transfers between devices  64.7 us (31%)
  Pallas kernels  64 us (30%)
  local copies, waits for them, and re-layouts  6.73 us (3%)
    pallas_call x43, Pallas kernels, call(): pl.pallas_call(kernel, out_shape=tuple(outs), in_specs=[pl.BlockSpec(memo...  64 us
    ppermute x26, waiting for transfers between devices, c_xor(): return lax.ppermute(x, 'ctx', [(i, i ^ k) for i in range(n)])  49.3 us
    ppermute x26, starting transfers between devices, c_xor(): return lax.ppermute(x, 'ctx', [(i, i ^ k) for i in range(n)])  31.4 us
    ppermute x39, starting transfers between devices, f_xor(): return lax.ppermute(x, 'fsdp', [(i, i ^ k) for i in range(n)])  29.5 us
    ppermute x39, waiting for transfers between devices, f_xor(): return lax.ppermute(x, 'fsdp', [(i, i ^ k) for i in range(n)])  24.9 us
    concatenate x1, local copies, waits for them, and re-layouts, body(): jnp.concatenate(vectors)  5.46 us
  transfers between devices with their start and end apart: 69, of which 26 were waited for; matrix products, arithmetic and copies ran while one was open for 3% of the time, Pallas kernels for 26%

profile of v3, /device:TPU:0, one launch (start us, length us, event | category | flops | bytes accessed | tf_op | source)
XLA Modules:
  0.0 211.5 jit_solution(14370041814846331214)
XLA Ops:
  5.2 6.7 %collective-permute-start.3 = (bf16[96,576]{1,0:T(8,128)(2,1)S(1)}, bf16[96,576]{1,0:T(8,128)(2,1)S(1)}, u32[]{:S(2)}, u32[]{:S(2)}) collective-permute-start(bf16[96,576]{1,0:T(8,128)(2,1)S(1)} %get-tuple-element.180), channel_id=1, source_target_pairs={{0,24},{8,16},{16,8},{24,0},{1,25},{9,17},{17,9},{25,1},{2,26},{10... | collective-permute-start | bytes 331784 | tf_op jit(solution)/shard_map/ppermute | solution.py:24
  11.8 5.5 %concatenate.3.vectors = bf16[2304]{0:T(1024)(128)(2,1)S(1)} concatenate(bf16[192]{0:T(256)(128)(2,1)} %param.17, bf16[192]{0:T(256)(128)(2,1)} %param.18, bf16[192]{0:T(256)(128)(2,1)} %param.22, bf16[192]{0:T(256)(128)(2,1)} %param.23, bf16[192]{0:T(256)(128)(2,1)} %param.24, bf16[192]{0:T(256)(128)(2,1)} %param.28, bf16[384]{0:T(512)(128)(2,1)} %param.20, bf16[768]{0:T(1024)(128)(2,1)} %param.26), dimensions={0} | concatenate | bytes 9216 | tf_op jit(solution)/shard_map/concatenate | solution.py:829
  18.9 2.5 %collective-permute-start.9 = (bf16[128,768]{1,0:T(8,128)(2,1)S(1)}, bf16[128,768]{1,0:T(8,128)(2,1)S(1)}, u32[]{:S(2)}, u32[]{:S(2)}) collective-permute-start(bf16[128,768]{1,0:T(8,128)(2,1)S(1)} %collective-permute-done.x0.x), channel_id=1, source_target_pairs={{0,16},{8,24},{16,0},{24,8},{1,17},{9,25},{17,1},{25,9},{2,18},{10... | collective-permute-start | bytes 589832 | tf_op jit(solution)/shard_map/ppermute | solution.py:24
  24.3 3.4 %collective-permute-done.4.w3_x = bf16[96,576]{1,0:T(8,128)(2,1)S(1)} collective-permute-done((bf16[96,576]{1,0:T(8,128)(2,1)S(1)}, bf16[96,576]{1,0:T(8,128)(2,1)S(1)}, u32[]{:S(2)}, u32[]{:S(2)}) %collective-permute-start.4) | collective-permute-done | bytes 110624 | tf_op jit(solution)/shard_map/ppermute | solution.py:29
  37.3 3.6 %attend0.1 = (f32[512,192]{1,0:T(8,128)S(1)}, f32[512,128]{1,0:T(8,128)S(1)}) custom-call(s32[6]{0:T(128)S(1)} %stack.19.sc.sc_ref, bf16[512,192]{1,0:T(8,128)(2,1)S(1)} %get-tuple-element.191.refs_0_, bf16[512,384]{1,0:T(8,128)(2,1)S(1)} %get-tuple-element.193.refs_1_.kv.refs_2_), custom_call_target="tpu_custom_call" | custom-call | flops 201326592 | bytes 1245208 | tf_op jit(solution)/shard_map/attend0/pallas_call | solution.py:105
  41.0 3.6 %collective-permute-done.12.refs_1_.refs_2_ = bf16[512,384]{1,0:T(8,128)(2,1)S(1)} collective-permute-done((bf16[512,384]{1,0:T(8,128)(2,1)S(1)}, bf16[512,384]{1,0:T(8,128)(2,1)S(1)}, u32[]{:S(2)}, u32[]{:S(2)}) %collective-permute-start.12) | collective-permute-done | bytes 393248 | tf_op jit(solution)/shard_map/ppermute | solution.py:29
  44.6 6.2 %attend1.1 = (f32[512,192]{1,0:T(8,128)S(1)}, bf16[512,192]{1,0:T(8,128)(2,1)S(1)}, bf16[512,256]{1,0:T(8,128)(2,1)S(1)}, f32[128,768]{1,0:T(8,128)S(1)}, f32[12...) custom-call(s32[6]{0:T(128)S(1)} %stack.19.sc.sc_ref, ...), custom_call_target="tpu_custom_call" | custom-call | flops 201326592 | bytes 3571736 | tf_op jit(solution)/shard_map/attend1/pallas_call | solution.py:105
  58.7 3.7 %collective-permute-done.20.far = bf16[128,768]{1,0:T(8,128)(2,1)S(1)} collective-permute-done((bf16[128,768]{1,0:T(8,128)(2,1)S(1)}, bf16[128,768]{1,0:T(8,128)(2,1)S(1)}, u32[]{:S(2)}, u32[]{:S(2)}) %collective-permute-start.20) | collective-permute-done | bytes 196640 | tf_op jit(solution)/shard_map/ppermute | solution.py:24
  65.6 4.0 %collective-permute-done.25.n2 = bf16[128,768]{1,0:T(8,128)(2,1)S(1)} collective-permute-done((bf16[128,768]{1,0:T(8,128)(2,1)S(1)}, bf16[128,768]{1,0:T(8,128)(2,1)S(1)}, u32[]{:S(2)}, u32[]{:S(2)}) %collective-permute-start.25) | collective-permute-done | bytes 196640 | tf_op jit(solution)/shard_map/ppermute | solution.py:24
  72.0 3.2 %feed.1 = (bf16[512,768]{1,0:T(8,128)(2,1)S(1)}, bf16[512,768]{1,0:T(8,128)(2,1)S(1)}, bf16[512,768]{1,0:T(8,128)(2,1)S(1)}, f32[1,768]{1,0:T(1,128)S(1)}, f32[1...) custom-call(s32[6]{0:T(128)S(1)} %stack.19.sc.sc_ref, ...), custom_call_target="tpu_custom_call" | custom-call | flops 1207959552 | bytes 7084056 | tf_op jit(solution)/shard_map/feed/pallas_call | solution.py:105
  87.6 5.2 %collective-permute-done.32.b2 = bf16[128,768]{1,0:T(8,128)(2,1)S(1)} collective-permute-done((bf16[128,768]{1,0:T(8,128)(2,1)S(1)}, bf16[128,768]{1,0:T(8,128)(2,1)S(1)}, u32[]{:S(2)}, u32[]{:S(2)}) %collective-permute-start.32) | collective-permute-done | bytes 196640 | tf_op jit(solution)/shard_map/ppermute | solution.py:24
  103.1 4.4 %back0.1 = (f32[512,192]{1,0:T(8,128)S(1)}, f32[512,384]{1,0:T(8,128)S(1)}) custom-call(s32[6]{0:T(128)S(1)} %stack.19.sc.sc_ref, bf16[512,256]{1,0:T(8,128)(2,1)S(1)} %get-tuple-element.215.q.refs_0_, bf16[512,256]{1,0:T(8,128)(2,1)S(1)} %get-tuple-element.242.do.refs_1_, bf16[512,384]{1,0:T(8,128)(2,1)S(1)} %get-tuple-element.193.refs_1_.kv.refs_2_), custom_call_target="tpu_custom_call" | custom-call | flops 503316480 | bytes 2097176 | tf_op jit(solution)/shard_map/back0/pallas_call | solution.py:105
  111.0 2.9 %back_q.1.refs_4_ = f32[512,192]{1,0:T(8,128)S(1)} custom-call(s32[6]{0:T(128)S(1)} %stack.19.sc.sc_ref, bf16[512,256]{1,0:T(8,128)(2,1)S(1)} %get-tuple-element.215.q.refs_0_, bf16[512,256]{1,0:T(8,128)(2,1)S(1)} %get-tuple-element.242.do.refs_1_, bf16[512,384]{1,0:T(8,128)(2,1)S(1)} %collective-permute-done.12.refs_1_.refs_2_, ...), custom_call_target="tpu_custom_call" | custom-call | flops 301989888 | bytes 1703960 | tf_op jit(solution)/shard_map/back_q/pallas_call | solution.py:105
  113.9 2.5 %collective-permute-start.42 = (bf16[2,192,384]{2,1,0:T(8,128)(2,1)S(1)}, bf16[2,192,384]{2,1,0:T(8,128)(2,1)S(1)}, u32[]{:S(2)}, u32[]{:S(2)}) collective-permute-start(bf16[2,192,384]{2,1,0:T(8,128)(2,1)S(1)} %get-tuple-element.271), channel_id=1, source_target_pairs={{0,4},{1,5},{2,6},{3,7},{4,0},{5,1},{6,2},{7,3},{8,12},{9,13},{10,... | collective-permute-start | bytes 884744 | tf_op jit(solution)/shard_map/ppermute | solution.py:29
  116.4 5.4 %back_kv.1 = (bf16[512,576]{1,0:T(8,128)(2,1)S(1)}, f32[128,768]{1,0:T(8,128)S(1)}, f32[128,768]{1,0:T(8,128)S(1)}, bf16[128,768]{1,0:T(8,128)(2,1)S(1)}, bf16[1...) custom-call(s32[6]{0:T(128)S(1)} %stack.19.sc.sc_ref, bf16[512,256]{1,0:T(8,128)(2,1)S(1)} %collective-permute-done.23.refs_0_, ...), custom_call_target="tpu_custom_call" | custom-call | flops 402653184 | bytes 5543960 | tf_op jit(solution)/shard_map/back_kv/pallas_call | solution.py:105
  124.4 4.3 %collective-permute-start.48 = (bf16[208,576]{1,0:T(8,128)(2,1)S(1)}, bf16[208,576]{1,0:T(8,128)(2,1)S(1)}, u32[]{:S(2)}, u32[]{:S(2)}) collective-permute-start(bf16[208,576]{1,0:T(8,128)(2,1)S(1)} %get-tuple-element.284), channel_id=1, source_target_pairs={{0,2},{1,3},{2,0},{3,1},{4,6},{5,7},{6,4},{7,5},{8,10},{9,11},{10,... | collective-permute-start | bytes 718856 | tf_op jit(solution)/shard_map/ppermute | solution.py:29
  130.1 2.6 %collective-permute-start.45 = (bf16[48,384]{1,0:T(8,128)(2,1)S(1)}, bf16[48,384]{1,0:T(8,128)(2,1)S(1)}, u32[]{:S(2)}, u32[]{:S(2)}) collective-permute-start(bf16[48,384]{1,0:T(8,128)(2,1)S(1)} %get-tuple-element.278), channel_id=1, source_target_pairs={{0,16},{8,24},{16,0},{24,8},{1,17},{9,25},{17,1},{25,9},{2,18},{10... | collective-permute-start | bytes 110600 | tf_op jit(solution)/shard_map/ppermute | solution.py:24
  144.4 3.6 %collective-permute-done.52.fc_got = bf16[192,384]{1,0:T(8,128)(2,1)S(1)} collective-permute-done((bf16[192,384]{1,0:T(8,128)(2,1)S(1)}, bf16[192,384]{1,0:T(8,128)(2,1)S(1)}, u32[]{:S(2)}, u32[]{:S(2)}) %collective-permute-start.52) | collective-permute-done | bytes 147488 | tf_op jit(solution)/shard_map/ppermute | solution.py:29
  149.6 2.5 %collective-permute-start.55 = (bf16[144,576]{1,0:T(8,128)(2,1)S(1)}, bf16[144,576]{1,0:T(8,128)(2,1)S(1)}, u32[]{:S(2)}, u32[]{:S(2)}) collective-permute-start(bf16[144,576]{1,0:T(8,128)(2,1)S(1)} %get-tuple-element.303), channel_id=1, source_target_pairs={{0,4},{1,5},{2,6},{3,7},{4,0},{5,1},{6,2},{7,3},{8,12},{9,13},{10,... | collective-permute-start | bytes 497672 | tf_op jit(solution)/shard_map/ppermute | solution.py:29
  155.8 3.5 %collective-permute-done.55.got = bf16[144,576]{1,0:T(8,128)(2,1)S(1)} collective-permute-done((bf16[144,576]{1,0:T(8,128)(2,1)S(1)}, bf16[144,576]{1,0:T(8,128)(2,1)S(1)}, u32[]{:S(2)}, u32[]{:S(2)}) %collective-permute-start.55) | collective-permute-done | bytes 165920 | tf_op jit(solution)/shard_map/ppermute | solution.py:29
  164.9 3.8 %collective-permute-start.59 = (bf16[40,576]{1,0:T(8,128)(2,1)S(1)}, bf16[40,576]{1,0:T(8,128)(2,1)S(1)}, u32[]{:S(2)}, u32[]{:S(2)}) collective-permute-start(bf16[40,576]{1,0:T(8,128)(2,1)S(1)} %get-tuple-element.312), channel_id=1, source_target_pairs={{0,16},{8,24},{16,0},{24,8},{1,17},{9,25},{17,1},{25,9},{2,18},{10... | collective-permute-start | bytes 138248 | tf_op jit(solution)/shard_map/ppermute | solution.py:24
  175.0 7.7 %collective-permute-done.61.got = bf16[128,576]{1,0:T(8,128)(2,1)S(1)} collective-permute-done((bf16[128,576]{1,0:T(8,128)(2,1)S(1)}, bf16[128,576]{1,0:T(8,128)(2,1)S(1)}, u32[]{:S(2)}, u32[]{:S(2)}) %collective-permute-start.61) | collective-permute-done | bytes 147488 | tf_op jit(solution)/shard_map/ppermute | solution.py:29
  188.4 7.9 %collective-permute-done.64.b_got = bf16[2,80,576]{2,1,0:T(8,128)(2,1)S(1)} collective-permute-done((bf16[2,80,576]{2,1,0:T(8,128)(2,1)S(1)}, bf16[2,80,576]{2,1,0:T(8,128)(2,1)S(1)}, u32[]{:S(2)}, u32[]{:S(2)}) %collective-permute-start.64) | collective-permute-done | bytes 184352 | tf_op jit(solution)/shard_map/ppermute | solution.py:29
  201.3 7.8 %collective-permute-done.66.nf = bf16[4,48,576]{2,1,0:T(8,128)(2,1)S(1)} collective-permute-done((bf16[4,48,576]{2,1,0:T(8,128)(2,1)S(1)}, bf16[4,48,576]{2,1,0:T(8,128)(2,1)S(1)}, u32[]{:S(2)}, u32[]{:S(2)}) %collective-permute-start.66) | collective-permute-done | bytes 221216 | tf_op jit(solution)/shard_map/ppermute | solution.py:29
  (169 shorter events, 103.2 us)
Async XLA Ops:
  0.6 18.3 %collective-permute-start = (bf16[128,768]{1,0:T(8,128)(2,1)}, bf16[128,768]{1,0:T(8,128)(2,1)S(1)}, u32[]{:S(2)}, u32[]{:S(2)}) collective-permute-start(bf16[128,768]{1,0:T(8,128)(2,1)} %bitcast.6), channel_id=1, source_target_pairs={{0,0},{1,1},{2,16},{3,17},{4,8},{5,9},{6,24},{7,25},{8,4},{9,5},{1... | collective-permute-start | bytes 589832 | tf_op jit(solution)/shard_map/ppermute | solution.py:44
  5.2 12.7 %collective-permute-start.3 = (bf16[96,576]{1,0:T(8,128)(2,1)S(1)}, bf16[96,576]{1,0:T(8,128)(2,1)S(1)}, u32[]{:S(2)}, u32[]{:S(2)}) collective-permute-start(bf16[96,576]{1,0:T(8,128)(2,1)S(1)} %get-tuple-element.180), channel_id=1, source_target_pairs={{0,24},{8,16},{16,8},{24,0},{1,25},{9,17},{17,9},{25,1},{2,26},{10... | collective-permute-start | bytes 331784 | tf_op jit(solution)/shard_map/ppermute | solution.py:24
  18.9 10.6 %collective-permute-start.9 = (bf16[128,768]{1,0:T(8,128)(2,1)S(1)}, bf16[128,768]{1,0:T(8,128)(2,1)S(1)}, u32[]{:S(2)}, u32[]{:S(2)}) collective-permute-start(bf16[128,768]{1,0:T(8,128)(2,1)S(1)} %collective-permute-done.x0.x), channel_id=1, source_target_pairs={{0,16},{8,24},{16,0},{24,8},{1,17},{9,25},{17,1},{25,9},{2,18},{10... | collective-permute-start | bytes 589832 | tf_op jit(solution)/shard_map/ppermute | solution.py:24
  33.1 11.5 %collective-permute-start.12 = (bf16[512,384]{1,0:T(8,128)(2,1)S(1)}, bf16[512,384]{1,0:T(8,128)(2,1)S(1)}, u32[]{:S(2)}, u32[]{:S(2)}) collective-permute-start(bf16[512,384]{1,0:T(8,128)(2,1)S(1)} %get-tuple-element.193.refs_1_.kv.refs_2_), channel_id=1, source_target_pairs={{0,1},{1,0},{2,3},{3,2},{4,5},{5,4},{6,7},{7,6},{8,9},{9,8},{10,11... | collective-permute-start | bytes 1179656 | tf_op jit(solution)/shard_map/ppermute | solution.py:29
  34.6 16.7 %collective-permute-start.13 = (bf16[192,768]{1,0:T(8,128)(2,1)S(1)}, bf16[192,768]{1,0:T(8,128)(2,1)S(1)}, u32[]{:S(2)}, u32[]{:S(2)}) collective-permute-start(bf16[192,768]{1,0:T(8,128)(2,1)S(1)} %get-tuple-element.199), channel_id=1, source_target_pairs={{0,8},{8,0},{16,24},{24,16},{1,9},{9,1},{17,25},{25,17},{2,10},{10... | collective-permute-start | bytes 884744 | tf_op jit(solution)/shard_map/ppermute | solution.py:24
  34.8 16.5 %collective-permute-start.14 = (bf16[192,768]{1,0:T(8,128)(2,1)S(1)}, bf16[192,768]{1,0:T(8,128)(2,1)S(1)}, u32[]{:S(2)}, u32[]{:S(2)}) collective-permute-start(bf16[192,768]{1,0:T(8,128)(2,1)S(1)} %get-tuple-element.200), channel_id=1, source_target_pairs={{0,16},{8,24},{16,0},{24,8},{1,17},{9,25},{17,1},{25,9},{2,18},{10... | collective-permute-start | bytes 884744 | tf_op jit(solution)/shard_map/ppermute | solution.py:24
  35.1 17.9 %collective-permute-start.15 = (bf16[192,768]{1,0:T(8,128)(2,1)S(1)}, bf16[192,768]{1,0:T(8,128)(2,1)S(1)}, u32[]{:S(2)}, u32[]{:S(2)}) collective-permute-start(bf16[192,768]{1,0:T(8,128)(2,1)S(1)} %get-tuple-element.201), channel_id=1, source_target_pairs={{0,24},{8,16},{16,8},{24,0},{1,25},{9,17},{17,9},{25,1},{2,26},{10... | collective-permute-start | bytes 884744 | tf_op jit(solution)/shard_map/ppermute | solution.py:24
  36.5 14.4 %collective-permute-start.17 = (bf16[128,768]{1,0:T(8,128)(2,1)S(1)}, bf16[128,768]{1,0:T(8,128)(2,1)S(1)}, u32[]{:S(2)}, u32[]{:S(2)}) collective-permute-start(bf16[128,768]{1,0:T(8,128)(2,1)S(1)} %bitcast.7), channel_id=1, source_target_pairs={{0,0},{1,1},{2,16},{3,17},{4,8},{5,9},{6,24},{7,25},{8,4},{9,5},{1... | collective-permute-start | bytes 589832 | tf_op jit(solution)/shard_map/ppermute | solution.py:44
  77.3 20.1 %collective-permute-start.34 = (bf16[4,192,384]{2,1,0:T(8,128)(2,1)S(1)}, bf16[4,192,384]{2,1,0:T(8,128)(2,1)S(1)}, u32[]{:S(2)}, u32[]{:S(2)}) collective-permute-start(bf16[4,192,384]{2,1,0:T(8,128)(2,1)S(1)} %get-tuple-element.247), channel_id=1, source_target_pairs={{0,2},{1,3},{2,0},{3,1},{4,6},{5,7},{6,4},{7,5},{8,10},{9,11},{10,... | collective-permute-start | bytes 1769480 | tf_op jit(solution)/shard_map/ppermute | solution.py:29
  80.3 17.1 %collective-permute-start.35 = (bf16[4,192,384]{2,1,0:T(8,128)(2,1)S(1)}, bf16[4,192,384]{2,1,0:T(8,128)(2,1)S(1)}, u32[]{:S(2)}, u32[]{:S(2)}) collective-permute-start(bf16[4,192,384]{2,1,0:T(8,128)(2,1)S(1)} %get-tuple-element.248), channel_id=1, source_target_pairs={{0,1},{1,0},{2,3},{3,2},{4,5},{5,4},{6,7},{7,6},{8,9},{9,8},{10,11... | collective-permute-start | bytes 1769480 | tf_op jit(solution)/shard_map/ppermute | solution.py:29
  98.2 9.9 %collective-permute-start.39 = (bf16[2,192,384]{2,1,0:T(8,128)(2,1)S(1)}, bf16[2,192,384]{2,1,0:T(8,128)(2,1)S(1)}, u32[]{:S(2)}, u32[]{:S(2)}) collective-permute-start(bf16[2,192,384]{2,1,0:T(8,128)(2,1)S(1)} %get-tuple-element.256), channel_id=1, source_target_pairs={{0,1},{1,0},{2,3},{3,2},{4,5},{5,4},{6,7},{7,6},{8,9},{9,8},{10,11... | collective-permute-start | bytes 884744 | tf_op jit(solution)/shard_map/ppermute | solution.py:29
  99.5 10.8 %collective-permute-start.40 = (bf16[2,192,384]{2,1,0:T(8,128)(2,1)S(1)}, bf16[2,192,384]{2,1,0:T(8,128)(2,1)S(1)}, u32[]{:S(2)}, u32[]{:S(2)}) collective-permute-start(bf16[2,192,384]{2,1,0:T(8,128)(2,1)S(1)} %get-tuple-element.258), channel_id=1, source_target_pairs={{0,2},{1,3},{2,0},{3,1},{4,6},{5,7},{6,4},{7,5},{8,10},{9,11},{10,... | collective-permute-start | bytes 884744 | tf_op jit(solution)/shard_map/ppermute | solution.py:29
  100.9 15.5 %collective-permute-start.41 = (bf16[512,256]{1,0:T(8,128)(2,1)S(1)}, bf16[512,256]{1,0:T(8,128)(2,1)S(1)}, u32[]{:S(2)}, u32[]{:S(2)}) collective-permute-start(bf16[512,256]{1,0:T(8,128)(2,1)S(1)} %get-tuple-element.242.do.refs_1_), channel_id=1, source_target_pairs={{0,1},{1,0},{2,3},{3,2},{4,5},{5,4},{6,7},{7,6},{8,9},{9,8},{10,11... | collective-permute-start | bytes 786440 | tf_op jit(solution)/shard_map/ppermute | solution.py:29
  113.9 15.4 %collective-permute-start.42 = (bf16[2,192,384]{2,1,0:T(8,128)(2,1)S(1)}, bf16[2,192,384]{2,1,0:T(8,128)(2,1)S(1)}, u32[]{:S(2)}, u32[]{:S(2)}) collective-permute-start(bf16[2,192,384]{2,1,0:T(8,128)(2,1)S(1)} %get-tuple-element.271), channel_id=1, source_target_pairs={{0,4},{1,5},{2,6},{3,7},{4,0},{5,1},{6,2},{7,3},{8,12},{9,13},{10,... | collective-permute-start | bytes 884744 | tf_op jit(solution)/shard_map/ppermute | solution.py:29
  123.8 15.6 %collective-permute-start.49 = (bf16[320,576]{1,0:T(8,128)(2,1)S(1)}, bf16[320,576]{1,0:T(8,128)(2,1)S(1)}, u32[]{:S(2)}, u32[]{:S(2)}) collective-permute-start(bf16[320,576]{1,0:T(8,128)(2,1)S(1)} %get-tuple-element.286), channel_id=1, source_target_pairs={{0,1},{1,0},{2,3},{3,2},{4,5},{5,4},{6,7},{7,6},{8,9},{9,8},{10,11... | collective-permute-start | bytes 1105928 | tf_op jit(solution)/shard_map/ppermute | solution.py:29
  124.4 15.0 %collective-permute-start.48 = (bf16[208,576]{1,0:T(8,128)(2,1)S(1)}, bf16[208,576]{1,0:T(8,128)(2,1)S(1)}, u32[]{:S(2)}, u32[]{:S(2)}) collective-permute-start(bf16[208,576]{1,0:T(8,128)(2,1)S(1)} %get-tuple-element.284), channel_id=1, source_target_pairs={{0,2},{1,3},{2,0},{3,1},{4,6},{5,7},{6,4},{7,5},{8,10},{9,11},{10,... | collective-permute-start | bytes 718856 | tf_op jit(solution)/shard_map/ppermute | solution.py:29
  129.9 9.5 %collective-permute-start.47 = (bf16[192,384]{1,0:T(8,128)(2,1)S(1)}, bf16[192,384]{1,0:T(8,128)(2,1)S(1)}, u32[]{:S(2)}, u32[]{:S(2)}) collective-permute-start(bf16[192,384]{1,0:T(8,128)(2,1)S(1)} %get-tuple-element.281.proj_own), channel_id=1, source_target_pairs={{0,4},{1,5},{2,6},{3,7},{4,0},{5,1},{6,2},{7,3},{8,12},{9,13},{10,... | collective-permute-start | bytes 442376 | tf_op jit(solution)/shard_map/ppermute | solution.py:29
  149.6 9.8 %collective-permute-start.55 = (bf16[144,576]{1,0:T(8,128)(2,1)S(1)}, bf16[144,576]{1,0:T(8,128)(2,1)S(1)}, u32[]{:S(2)}, u32[]{:S(2)}) collective-permute-start(bf16[144,576]{1,0:T(8,128)(2,1)S(1)} %get-tuple-element.303), channel_id=1, source_target_pairs={{0,4},{1,5},{2,6},{3,7},{4,0},{5,1},{6,2},{7,3},{8,12},{9,13},{10,... | collective-permute-start | bytes 497672 | tf_op jit(solution)/shard_map/ppermute | solution.py:29
  152.7 10.3 %collective-permute-start.56 = (bf16[2,192,384]{2,1,0:T(8,128)(2,1)S(1)}, bf16[2,192,384]{2,1,0:T(8,128)(2,1)S(1)}, u32[]{:S(2)}, u32[]{:S(2)}) collective-permute-start(bf16[2,192,384]{2,1,0:T(8,128)(2,1)S(1)} %get-tuple-element.300.a), channel_id=1, source_target_pairs={{0,1},{1,0},{2,3},{3,2},{4,5},{5,4},{6,7},{7,6},{8,9},{9,8},{10,11... | collective-permute-start | bytes 884744 | tf_op jit(solution)/shard_map/ppermute | solution.py:29
  163.6 20.6 %collective-permute-start.62 = (bf16[4,192,384]{2,1,0:T(8,128)(2,1)S(1)}, bf16[4,192,384]{2,1,0:T(8,128)(2,1)S(1)}, u32[]{:S(2)}, u32[]{:S(2)}) collective-permute-start(bf16[4,192,384]{2,1,0:T(8,128)(2,1)S(1)} %get-tuple-element.319.near), channel_id=1, source_target_pairs={{0,1},{1,0},{2,3},{3,2},{4,5},{5,4},{6,7},{7,6},{8,9},{9,8},{10,11... | collective-permute-start | bytes 1769480 | tf_op jit(solution)/shard_map/ppermute | solution.py:29
  173.5 25.7 %collective-permute-start.65 = (bf16[4,192,384]{2,1,0:T(8,128)(2,1)S(1)}, bf16[4,192,384]{2,1,0:T(8,128)(2,1)S(1)}, u32[]{:S(2)}, u32[]{:S(2)}) collective-permute-start(bf16[4,192,384]{2,1,0:T(8,128)(2,1)S(1)} %get-tuple-element.310.near), channel_id=1, source_target_pairs={{0,2},{1,3},{2,0},{3,1},{4,6},{5,7},{6,4},{7,5},{8,10},{9,11},{10,... | collective-permute-start | bytes 1769480 | tf_op jit(solution)/shard_map/ppermute | solution.py:29
  183.3 13.1 %collective-permute-start.64 = (bf16[2,80,576]{2,1,0:T(8,128)(2,1)S(1)}, bf16[2,80,576]{2,1,0:T(8,128)(2,1)S(1)}, u32[]{:S(2)}, u32[]{:S(2)}) collective-permute-start(bf16[2,80,576]{2,1,0:T(8,128)(2,1)S(1)} %get-tuple-element.322.b), channel_id=1, source_target_pairs={{0,2},{1,3},{2,0},{3,1},{4,6},{5,7},{6,4},{7,5},{8,10},{9,11},{10,... | collective-permute-start | bytes 552968 | tf_op jit(solution)/shard_map/ppermute | solution.py:29
  196.9 12.2 %collective-permute-start.67 = (bf16[4,80,576]{2,1,0:T(8,128)(2,1)S(1)}, bf16[4,80,576]{2,1,0:T(8,128)(2,1)S(1)}, u32[]{:S(2)}, u32[]{:S(2)}) collective-permute-start(bf16[4,80,576]{2,1,0:T(8,128)(2,1)S(1)} %get-tuple-element.326.wn), channel_id=1, source_target_pairs={{0,1},{1,0},{2,3},{3,2},{4,5},{5,4},{6,7},{7,6},{8,9},{9,8},{10,11... | collective-permute-start | bytes 1105928 | tf_op jit(solution)/shard_map/ppermute | solution.py:29
  198.2 10.9 %collective-permute-start.66 = (bf16[4,48,576]{2,1,0:T(8,128)(2,1)S(1)}, bf16[4,48,576]{2,1,0:T(8,128)(2,1)S(1)}, u32[]{:S(2)}, u32[]{:S(2)}) collective-permute-start(bf16[4,48,576]{2,1,0:T(8,128)(2,1)S(1)} %get-tuple-element.323.nn), channel_id=1, source_target_pairs={{0,2},{1,3},{2,0},{3,1},{4,6},{5,7},{6,4},{7,5},{8,10},{9,11},{10,... | collective-permute-start | bytes 663560 | tf_op jit(solution)/shard_map/ppermute | solution.py:29
  (50 other events, 288.4 us)
